TPU v7x, 32 devices: a whole 2x2x4 slice. The times are simulated.
32 devices in a mesh: groups: 2 (over y), fsdp: 4 (over z), dp: 4 (over x, core).
Axes of the slice: x: 2, y: 2, z: 4, core: 2. Of those that a mesh axis runs over, the one named last changes fastest.
Arguments:
- hidden_in: bfloat16 [4096, 8192], P(('groups', 'dp'), 'fsdp'), parts along dimension 0, may hold values from -6 to 6
- cotangent: bfloat16 [4096, 9216], P(('groups', 'dp'), 'fsdp'), parts along dimension 0, may hold values from -6 to 6
- base_codes: bfloat16 [8192, 9216], P('fsdp', 'dp'), may hold values from -1 to 1
- base_scales: bfloat16 [8192, 144], P('fsdp', 'dp'), may hold values from 0.0079956055 to 0.039794922
- factor_a: bfloat16 [32, 131072], P('groups', 'fsdp'), parts along dimension 0, may hold values from -0.0625 to 0.0625
- factor_b: bfloat16 [32, 73728], P('groups', 'fsdp'), parts along dimension 0, may hold values from -0.0625 to 0.0625
- task_state: bfloat16 [32, 512], P('groups', 'dp'), parts along dimension 0, may hold values from -0.1796875 to 0.1796875
- head_a: bfloat16 [512, 131072], P('dp', 'fsdp'), may hold values from -0.0004196167 to 0.0004196167
- head_b: bfloat16 [512, 73728], P('dp', 'fsdp'), may hold values from -0.0004196167 to 0.0004196167
- task_ids: int32 [8], P(('groups', 'dp')), parts along dimension 0, may hold values from 0 to 15
- valid_counts: int32 [8], P(('groups', 'dp')), parts along dimension 0, may hold values from 64 to 384, as said below
- owners: int32 [32], P('groups'), parts along dimension 0, may hold values from 0 to 3, as said below
Outputs:
- input_gradient: bfloat16 [4096, 8192], P(('groups', 'dp'), 'fsdp'), parts along dimension 0
- grad_head_a: float32 [1024, 131072], P(('groups', 'dp'), 'fsdp'), parts along dimension 0
- grad_head_b: float32 [1024, 73728], P(('groups', 'dp'), 'fsdp'), parts along dimension 0
- grad_state: float32 [32, 512], P(('groups', 'fsdp'), 'dp'), parts along dimension 0
There are 2 independent parts, one for each index of `groups`. A program takes and returns all parts, laid end to end along the dimension named above; an argument that names none is the same for every part. Nothing has to cross between parts.
Inputs may be any that keep to these rules, and one draw needn't show every extreme that they name: `valid_counts`: every sequence has at most 384 valid tokens, and some sequence has exactly 384. `owners`: no owner has more than 4 tasks, and some owner has exactly 4.
All inputs are finite; a program needn't handle non-finite values.
Results may differ from a plain program's by a relative error of at most 0.017.
Values may be sent and summed in bfloat16 or wider, within the bound.
No kernel may reach another device: no remote copies, remote signals or barrier semaphores. Data moves between devices by JAX's collectives and lax.ppermute only.
A program may use at most 320 MiB of HBM per device.

v0:
```python
import jax
import jax.numpy as jnp
from jax import lax
from jax.sharding import PartitionSpec as P

HEADS = 64
KV_HEADS = 8
HEAD_DIM = 128
QBLOCK = 64
SLOTS = 4


adapter_scale = 2.0


def shards(
    hidden_in,
    cotangent,
    base_codes,
    base_scales,
    factor_a,
    factor_b,
    task_state,
    head_a,
    head_b,
    task_ids,
    valid_counts,
    owners,
):
    highest = lax.Precision.HIGHEST
    seq_len, width_part = hidden_in.shape
    tasks_all, factor_cols = factor_a.shape
    rank_double = factor_cols // width_part
    rank_half = rank_double // 2
    joined_part = cotangent.shape[1]
    positions = lax.broadcasted_iota(jnp.int32, (seq_len, 1), 0)
    row_keep = (positions < valid_counts[0]).astype(jnp.bfloat16)
    masked = cotangent * row_keep
    picked = (lax.broadcasted_iota(jnp.int32, (1, tasks_all), 1) == task_ids[0]).astype(
        jnp.bfloat16
    )
    chosen_a = (
        jnp.dot(picked, factor_a, preferred_element_type=jnp.float32)
        .astype(jnp.bfloat16)
        .reshape(width_part, rank_double)
    )
    chosen_b = (
        jnp.dot(picked, factor_b, preferred_element_type=jnp.float32)
        .astype(jnp.bfloat16)
        .reshape(joined_part, rank_half)
    )
    group_cols = (HEADS // KV_HEADS + 1) * HEAD_DIM
    columns = lax.axis_index("fsdp") * joined_part + lax.broadcasted_iota(
        jnp.int32, (joined_part, 1), 0
    )
    value_column_start = columns % group_cols >= HEADS // KV_HEADS * HEAD_DIM
    empty_b = jnp.zeros_like(chosen_b)
    joined_b = jnp.concatenate(
        [
            jnp.where(value_column_start, empty_b, chosen_b),
            jnp.where(value_column_start, chosen_b, empty_b),
        ],
        axis=1,
    )
    inner_part = jnp.dot(hidden_in, chosen_a, preferred_element_type=jnp.float32)
    outer_part = jnp.dot(masked, joined_b, preferred_element_type=jnp.float32)
    lowrank_in, lowrank_out = (
        lax.psum(inner_part.astype(jnp.bfloat16), "fsdp").astype(jnp.float32),
        lax.psum(outer_part.astype(jnp.bfloat16), "fsdp").astype(jnp.float32),
    )
    lowrank_low = lowrank_in.astype(jnp.bfloat16)
    reduced_rank_gradient = lowrank_out.astype(jnp.bfloat16)
    codes_all, scales_all = (
        lax.all_gather(base_codes, "dp", axis=1, tiled=True),
        lax.all_gather(base_scales, "dp", axis=1, tiled=True),
    )
    block_count = scales_all.shape[1]
    weight = (
        (
            codes_all.astype(jnp.float32).reshape(width_part, block_count, QBLOCK)
            * scales_all.astype(jnp.float32)[:, :, None]
        )
        .reshape(width_part, block_count * QBLOCK)
        .astype(jnp.bfloat16)
    )
    merged_rows = lax.dot_general(
        lax.all_gather(masked, "fsdp", axis=1, tiled=True),
        weight,
        (((1,), (1,)), ((), ())),
        preferred_element_type=jnp.float32,
    )
    adapter_contribution = lax.dot_general(
        reduced_rank_gradient,
        chosen_a,
        (((1,), (1,)), ((), ())),
        preferred_element_type=jnp.float32,
    )
    input_gradient = (merged_rows + adapter_scale * adapter_contribution).astype(jnp.bfloat16)
    down_gradient = adapter_scale * lax.dot_general(
        hidden_in,
        reduced_rank_gradient,
        (((0,), (0,)), ((), ())),
        preferred_element_type=jnp.float32,
    )
    mixed_products = lax.dot_general(
        masked, lowrank_low, (((0,), (0,)), ((), ())), preferred_element_type=jnp.float32
    )
    up_gradient = adapter_scale * jnp.where(
        value_column_start, mixed_products[:, rank_half:], mixed_products[:, :rank_half]
    )
    task_column = picked.astype(jnp.float32).reshape(tasks_all, 1)
    task_down = task_column * down_gradient.reshape(1, -1)
    task_up = task_column * up_gradient.reshape(1, -1)
    sum_down, sum_up = (
        lax.psum(task_down.astype(jnp.bfloat16), "dp").astype(jnp.float32),
        lax.psum(task_up.astype(jnp.bfloat16), "dp").astype(jnp.float32),
    )
    state_wide = task_state.astype(jnp.float32)
    grad_head_a = lax.dot_general(state_wide, sum_down, (((0,), (0,)), ((), ())), precision=highest)
    grad_head_b = lax.dot_general(state_wide, sum_up, (((0,), (0,)), ((), ())), precision=highest)
    state_part = lax.dot_general(
        sum_down, head_a.astype(jnp.float32), (((1,), (1,)), ((), ())), precision=highest
    )
    state_part = state_part + lax.dot_general(
        sum_up, head_b.astype(jnp.float32), (((1,), (1,)), ((), ())), precision=highest
    )
    task_rows = lax.broadcasted_iota(jnp.int32, (tasks_all, tasks_all), 0)
    task_other = lax.broadcasted_iota(jnp.int32, (tasks_all, tasks_all), 1)
    same_owner = owners[:, None] == owners[None, :]
    slot_index = jnp.sum((same_owner & (task_other < task_rows)).astype(jnp.int32), axis=1)
    target = owners * SLOTS + slot_index
    rows_all = lax.axis_size("fsdp") * SLOTS
    selector = (
        lax.broadcasted_iota(jnp.int32, (rows_all, tasks_all), 0) == target[None, :]
    ).astype(jnp.float32)
    owner_terms = jnp.dot(selector, state_part, precision=highest)
    grad_state = lax.psum_scatter(
        owner_terms.astype(jnp.bfloat16), "fsdp", scatter_dimension=0, tiled=True
    ).astype(jnp.float32)
    return (input_gradient, grad_head_a, grad_head_b, grad_state)


def solution(mesh):
    placed = (
        P(("groups", "dp"), "fsdp"),
        P(("groups", "dp"), "fsdp"),
        P("fsdp", "dp"),
        P("fsdp", "dp"),
        P("groups", "fsdp"),
        P("groups", "fsdp"),
        P("groups", "dp"),
        P("dp", "fsdp"),
        P("dp", "fsdp"),
        P(("groups", "dp")),
        P(("groups", "dp")),
        P("groups"),
    )
    return jax.shard_map(
        shards,
        mesh=mesh,
        in_specs=placed,
        out_specs=(
            P(("groups", "dp"), "fsdp"),
            P(("groups", "dp"), "fsdp"),
            P(("groups", "dp"), "fsdp"),
            P(("groups", "fsdp"), "dp"),
        ),
        check_vma=False,
    )
```

profile of v0, /device:TPU:0, one launch (start us, length us, event | category | flops | bytes accessed | tf_op | source)
XLA Modules:
  0.0 524.0 jit_solution(353779576208548617)
XLA Ops:
  8.7 1.3 fusion.16
  10.0 0.7 reshape.72
  10.9 1.5 fusion.14
  12.8 3.3 broadcast_multiply_fusion
  16.1 0.6 fusion.2
  16.8 2.4 convolution_convert_fusion.1
  19.2 20.8 %all-reduce.2 = (bf16[512,16]{0,1:T(8,128)(2,1)S(1)}, bf16[512,16]{0,1:T(8,128)(2,1)S(1)}) all-reduce(bf16[512,16]{0,1:T(8,128)(2,1)S(1)} %convolution_convert_fusion.1, bf16[512,16]{0,1:T(8,128)(2,1)S(1)} %fusion.2), channel_id=1, replica_groups=mesh['groups'=2,'fsdp'=4,'dp'=4] {'fsdp'}, use_global_device_ids=true, to_apply=%region_0.1 | all-reduce | flops 16384 | bytes 65536 | tf_op jit(solution)/shard_map/psum | solution.py:69
  40.0 0.4 fusion.1
  41.0 2.1 fusion.23
  43.2 0.4 copy.37
  43.5 0.6 mul.94
  44.1 1.2 multiply_convert_fusion
  45.2 0.9 multiply_convert_fusion.1
  46.3 12.7 %copy.33 = bf16[2048,2304]{0,1:T(8,128)(2,1)} copy(bf16[2048,2304]{1,0:T(8,128)(2,1)} %param.14) | data formatting | bytes 18874368 | tf_op args[2]
  59.1 0.7 all-gather.4.cloned.1.call-update
  59.9 9.7 %all-gather = bf16[4,36,2048]{2,1,0:T(8,128)(2,1)S(1)} all-gather(bf16[1,36,2048]{2,1,0:T(8,128)(2,1)S(1)} %bitcast.56), channel_id=1, replica_groups=mesh['groups'=2,'fsdp'=4,'dp'=4] {'dp'}, dimensions={0}, use_global_device_ids=true | all-gather | bytes 737280 | tf_op jit(solution)/shard_map/all_gather | solution.py:75
  69.6 1.1 reshape.76
  70.7 0.6 dynamic-slice
  72.1 20.1 %all-reduce.5.cloned.1.call-done = (bf16[16,32768]{1,0:T(8,128)(2,1)}, bf16[16,18432]{1,0:T(8,128)(2,1)}) async-done(((bf16[16,32768]{1,0:T(8,128)(2,1)}, bf16[16,18432]{1,0:T(8,128)(2,1)}), (bf16[16,32768]{1,0:T(8,128)(2,1)}, bf16[16,18432]{1,0:T(8,128)(2,1)})) %all-reduce.5.cloned.1.call-update) | async-done | bytes 1638416 | tf_op jit(solution)/shard_map/psum | solution.py:115
  92.2 11.6 %convolution_bitcast_fusion = f32[128,32768]{0,1:T(8,128)} fusion(bf16[16,32768]{1,0:T(8,128)(2,1)} %get-tuple-element.20, bf16[16,128]{1,0:T(8,128)(2,1)S(1)} %copy-done.6), kind=kOutput, calls=%fused_computation.2 | convolution fusion | flops 134217728 | bytes 17829888 | tf_op jit(solution)/shard_map/dot_general | solution.py:119
  103.8 19.4 %copy.38 = f32[128,32768]{1,0:T(8,128)} copy(f32[128,32768]{0,1:T(8,128)} %convolution_bitcast_fusion) | data formatting | bytes 33554432
  123.2 4.6 convolution_bitcast_fusion.1
  127.8 9.7 %copy.39 = f32[128,18432]{1,0:T(8,128)} copy(f32[128,18432]{0,1:T(8,128)} %convolution_bitcast_fusion.1) | data formatting | bytes 18874368
  137.4 5.6 %fusion.22 = f32[16,128]{1,0:T(8,128)S(1)} fusion(bf16[16,32768]{1,0:T(8,128)(2,1)S(1)} %copy-done.2, bf16[128,32768]{1,0:T(8,128)(2,1)} %param.19), kind=kOutput, calls=%fused_computation.47 | convolution fusion | flops 134217728 | bytes 9445376 | tf_op jit(solution)/shard_map/dot_general | solution.py:121
  143.1 3.8 convolution_add_fusion
  147.0 11.6 %all-reduce = bf16[16,128]{1,0:T(8,128)(2,1)S(1)} all-reduce(bf16[16,128]{1,0:T(8,128)(2,1)S(1)} %convolution_convert_fusion.2), channel_id=2, replica_groups=mesh['groups'=2,'fsdp'=4,'dp'=4] {'fsdp'}, use_global_device_ids=true, to_apply=%region_5.6.clone | all-reduce | flops 2048 | bytes 8192
  158.6 0.6 dynamic-slice_convert_fusion
  159.2 161.9 %all-gather.6.cloned.1.call-done = bf16[2048,9216]{0,1:T(8,128)(2,1)} async-done(((bf16[2048,2304]{0,1:T(8,128)(2,1)}), bf16[2048,9216]{0,1:T(8,128)(2,1)}) %all-gather.6.cloned.1.call-update) | async-done | bytes 37748752 | tf_op jit(solution)/shard_map/all_gather | solution.py:74
  321.2 26.4 %fusion = bf16[2048,9216]{0,1:T(8,128)(2,1)} fusion(bf16[2048,9216]{0,1:T(8,128)(2,1)} %all-gather.6.cloned.1.call-done, f32[2048,144]{0,1:T(8,128)S(1)} %bitcast.53), kind=kLoop, calls=%fused_computation.1 | loop fusion | flops 56623104 | bytes 76677120 | tf_op jit(solution)/shard_map/convert_element_type | solution.py:84
  347.6 142.0 %all-gather.4.cloned.1.call-done = bf16[512,9216]{1,0:T(8,128)(2,1)} async-done(((bf16[512,2304]{1,0:T(8,128)(2,1)}), bf16[512,9216]{1,0:T(8,128)(2,1)}) %all-gather.4.cloned.1.call-update) | async-done | bytes 9437200 | tf_op jit(solution)/shard_map/all_gather | solution.py:87
  489.6 25.8 %fusion.21 = f32[512,2048]{1,0:T(8,128)S(1)} fusion(bf16[512,9216]{1,0:T(8,128)(2,1)} %all-gather.4.cloned.1.call-done, bf16[2048,9216]{0,1:T(8,128)(2,1)} %fusion), kind=kOutput, calls=%fused_computation.46 | convolution fusion | flops 19327352832 | bytes 51380224 | tf_op jit(solution)/shard_map/dot_general | solution.py:86
  515.4 2.1 add_convert_fusion
  (37 shorter events, 1.9 us)
Async XLA Ops:
  7.2 9.0 %copy-start = (bf16[512,2048]{1,0:T(8,128)(2,1)S(1)}, bf16[512,2048]{1,0:T(8,128)(2,1)}, u32[]{:S(2)}) copy-start(bf16[512,2048]{1,0:T(8,128)(2,1)} %param.12) | copy-start | bytes 6291460
  7.2 85.0 %all-reduce.5.cloned.1.call-start = ((), (), s32[]{:S(2)}) async-start(), calls=%async_computation.2 | async-start | bytes 3276800 | tf_op jit(solution)/shard_map/psum | solution.py:115
  46.2 274.9 %all-gather.6.cloned.1.call-start = ((), (), s32[]{:S(2)}) async-start(), calls=%async_computation.1 | async-start | bytes 47185920 | tf_op jit(solution)/shard_map/all_gather | solution.py:74
  58.9 0.9 copy-start.5
  59.0 11.7 %copy-start.8 = (u32[32]{0:T(128)S(1)}, u32[32]{0:T(128)}, u32[]{:S(2)}) copy-start(u32[32]{0:T(128)} %constant.34) | copy-start | bytes 388
  59.0 13.0 %copy-start.7 = (s32[16]{0:T(128)S(1)}, s32[16]{0:T(128)}, u32[]{:S(2)}) copy-start(s32[16]{0:T(128)} %param.23) | copy-start | bytes 196
  59.0 33.2 %copy-start.6 = (bf16[16,128]{1,0:T(8,128)(2,1)S(1)}, bf16[16,128]{1,0:T(8,128)(2,1)}, u32[]{:S(2)}) copy-start(bf16[16,128]{1,0:T(8,128)(2,1)} %param.18) | copy-start | bytes 12292
  59.0 430.6 %all-gather.4.cloned.1.call-start = ((), (), s32[]{:S(2)}) async-start(), calls=%async_computation | async-start | bytes 11796480 | tf_op jit(solution)/shard_map/all_gather | solution.py:87
  103.8 19.4 %copy-start.4 = (bf16[16,18432]{1,0:T(8,128)(2,1)S(1)}, bf16[16,18432]{1,0:T(8,128)(2,1)}, u32[]{:S(2)}) copy-start(bf16[16,18432]{1,0:T(8,128)(2,1)} %get-tuple-element.21) | copy-start | bytes 1769476
  127.8 9.7 %copy-start.2 = (bf16[16,32768]{1,0:T(8,128)(2,1)S(1)}, bf16[16,32768]{1,0:T(8,128)(2,1)}, u32[]{:S(2)}) copy-start(bf16[16,32768]{1,0:T(8,128)(2,1)} %get-tuple-element.20) | copy-start | bytes 3145732
  143.1 178.1 %copy-start.3 = (f32[144,2048]{1,0:T(8,128)S(1)}, f32[144,2048]{1,0:T(8,128)}, u32[]{:S(2)}) copy-start(f32[144,2048]{1,0:T(8,128)} %reshape.76) | copy-start | bytes 3538948
  489.6 27.9 %copy-start.1 = (bf16[512,2048]{1,0:T(8,128)(2,1)S(1)}, bf16[512,2048]{1,0:T(8,128)(2,1)}, u32[]{:S(2)}) copy-start(bf16[512,2048]{1,0:T(8,128)(2,1)} %param.12) | copy-start | bytes 6291460
Sparse Core Ops, SparseCore 0:
  46.3 45.8 all-reduce.4
  93.9 227.2 all-gather.5
  322.8 166.7 all-gather.3
where the time goes:
time: 525 us; the launch traced here: 524 us
  waiting for transfers between devices  325 us (62%)
  matrix products  62 us (12%)
  local copies, waits for them, and re-layouts  46.3 us (9%)
  blocking collectives  42.1 us (8%)
  other arithmetic  32.7 us (6%)
  between operations  16 us (3%)
    all_gather x1, waiting for transfers between devices, shards(): lax.all_gather(base_codes, 'dp', axis=1, tiled=True)  162 us
    all_gather x1, waiting for transfers between devices, shards(): lax.all_gather(masked, 'fsdp', axis=1, tiled=True)  142 us
    unnamed x22, local copies, waits for them, and re-layouts  42.4 us
    convert_element_type x1, other arithmetic, shards(): weight = (codes_all.astype(jnp.float32).reshape(width_part, block_count,...  26.4 us
    dot_general x1, matrix products, shards(): lax.dot_general(lax.all_gather(masked, 'fsdp', axis=1, tiled=True), weigh...  25.8 us
    psum x1, blocking collectives, shards(): lax.psum(outer_part.astype(jnp.bfloat16), 'fsdp').astype(jnp.float32)  20.8 us
    psum x1, waiting for transfers between devices, shards(): lax.psum(task_down.astype(jnp.bfloat16), 'dp').astype(jnp.float32)  20.1 us
    dot_general x1, matrix products, shards(): lax.dot_general(state_wide, sum_down, (((0,), (0,)), ((), ())), precision...  11.6 us
  transfers between devices with their start and end apart: 3, of which 3 were waited for; matrix products, arithmetic and copies ran while one was open for 18% of the time, Pallas kernels for 0%

commit v1 on v0

v1 whole, which is shorter than its diff:
```python
import jax
import jax.numpy as jnp
from jax import lax
from jax.experimental import pallas as pl
from jax.experimental.pallas import tpu as pltpu
from jax.sharding import PartitionSpec as P

HEADS = 64
KV_HEADS = 8
HEAD_DIM = 128
QBLOCK = 64
SLOTS = 4
LIVE = 384
TILE = 256

adapter_scale = 2.0


def dequantize(codes, scales):
    cols, blocks = codes.shape[1], scales.shape[1]
    spread = (
        lax.broadcasted_iota(jnp.int32, (blocks, cols), 1) // QBLOCK
        == lax.broadcasted_iota(jnp.int32, (blocks, cols), 0)
    ).astype(jnp.bfloat16)
    wide = jnp.dot(scales, spread, preferred_element_type=jnp.float32)
    return (codes.astype(jnp.float32) * wide).astype(jnp.bfloat16)


def after(value, *done):
    return lax.optimization_barrier((value, done))[0]


def input_gradient_kernel(tiles, where, count, *refs):
    meta, low, chosen = refs[:3]
    near = refs[3:10]
    arrays = refs[10 : 10 + count]
    out, cot, wbuf, csem, wsem = refs[10 + count :]
    weights = [arrays[index].at[pl.ds(offset * TILE, TILE)] for index, offset in where]
    z, p, y, valid = meta[0], meta[1], meta[2], meta[3]
    own, up1, dn1, up2, dn2, up3, dn3 = near
    depth = wbuf.shape[0]
    steps = 4 * tiles

    def fetch(step, slot):
        for index in range(steps):

            @pl.when(step == index)
            def _():
                pltpu.make_async_copy(weights[index], wbuf.at[slot], wsem.at[slot]).start()

    def place(first, second, take_first, slot):
        @pl.when(take_first)
        def _():
            pltpu.make_async_copy(first, cot.at[slot], csem.at[slot]).start()

        @pl.when(jnp.logical_not(take_first))
        def _():
            pltpu.make_async_copy(second, cot.at[slot], csem.at[slot]).start()

    pltpu.make_async_copy(own, cot.at[0], csem.at[0]).start()
    place(up1, dn3, z >= 1, 1)
    place(up2, dn2, z >= 2, 2)
    place(up3, dn1, z >= 3, 3)
    for slot in range(depth - 1):
        pltpu.make_async_copy(weights[slot], wbuf.at[slot], wsem.at[slot]).start()
    for slot in range(4):
        pltpu.make_async_copy(own, cot.at[slot], csem.at[slot]).wait()
    keep = lax.broadcasted_iota(jnp.int32, (LIVE, 1), 0) < valid
    out[LIVE:, :] = jnp.zeros((out.shape[0] - LIVE, out.shape[1]), out.dtype)

    @pl.loop(0, tiles)
    def _(tile):
        half = (tiles - 2) // 2
        first = tile + jnp.where(tile < half, y * half, -y * half)
        place_at = jnp.where(tile < 2 * half, first, tile)
        start = pl.multiple_of(place_at * TILE, TILE)
        acc = adapter_scale * lax.dot_general(
            low[...],
            chosen[pl.ds(start, TILE), :],
            (((1,), (1,)), ((), ())),
            preferred_element_type=jnp.float32,
        )
        total = jnp.zeros((LIVE, TILE), jnp.float32)
        for j in range(4):
            step = tile * 4 + j
            slot = lax.rem(step, depth)
            ahead = step + depth - 1
            fetch(ahead, lax.rem(ahead, depth))
            pltpu.make_async_copy(weights[0], wbuf.at[slot], wsem.at[slot]).wait()
            block = jnp.bitwise_and(z - jnp.bitwise_xor(p, j), 3)
            total = total + lax.dot_general(
                cot[block],
                wbuf[slot],
                (((1,), (1,)), ((), ())),
                preferred_element_type=jnp.float32,
            )
        result = jnp.where(keep, total, 0.0) + acc
        out[:LIVE, pl.ds(start, TILE)] = result.astype(out.dtype)


def permute_plan(own, codes, scales, y):
    rows = codes.shape[0]
    tiles = rows // TILE
    half = (tiles - 2) // 2
    up = lambda step: [(i, i + 1) for i in range(step, 3)]
    down = lambda step: [(i + 1, i) for i in range(0, 3 - step)]
    across = lambda v: lax.ppermute(v, "dp", [(i, i ^ 2) for i in range(4)])
    core = lambda v: lax.ppermute(v, "dp", [(i, i ^ 1) for i in range(4)])
    over = lambda v: lax.ppermute(v, "groups", [(0, 1), (1, 0)])

    def part(start, size):
        return dequantize(
            lax.dynamic_slice_in_dim(codes, start, size, 0),
            lax.dynamic_slice_in_dim(scales, start, size, 0),
        )

    up1 = lax.ppermute(own, "fsdp", up(0))
    dn1 = lax.ppermute(own, "fsdp", down(0))
    near_tiles = [part((y * half + i) * TILE, TILE) for i in range(half)]
    last_tiles = [part((2 * half + i) * TILE, TILE) for i in range(2)]
    middle = part((1 - y) * half * TILE, half * TILE)
    m0, m1, m2 = near_tiles
    e0, e1 = last_tiles
    x0 = across(m0)
    x1 = across(m1)
    sib_middle = core(middle)
    sib0 = core(after(m0, sib_middle))
    sib1 = core(after(m1, sib0))
    sib2 = core(after(m2, sib1))
    y0 = over(after(x0, sib2))
    x2 = across(after(m2, x0))
    up2 = lax.ppermute(after(up1, x0), "fsdp", up(1))
    dn2 = lax.ppermute(after(dn1, x0), "fsdp", down(1))
    y1 = over(after(x1, up1, dn1))
    fx0 = core(after(x0, x1, y0))
    fy0 = core(after(y0, fx0))
    sib3 = core(after(e0, fy0))
    sib4 = core(after(e1, sib3))
    x3 = across(after(e0, sib4))
    y2 = over(after(x2, sib4))
    fx1 = core(after(x1, x2))
    fy1 = core(after(y1, fx1))
    fx2 = core(after(x2, fy1))
    up3 = lax.ppermute(after(up2, x2), "fsdp", up(2))
    dn3 = lax.ppermute(after(dn2, x2), "fsdp", down(2))
    x4 = across(after(e1, fx2))
    fx3 = core(after(x3, up2, dn2))
    fy2 = core(after(y2, fx3))
    fx4 = core(x4)
    mine = [(m0, 0), (m1, 0), (m2, 0), (middle, 0), (middle, 1), (middle, 2), (e0, 0), (e1, 0)]
    sibling = [(sib0, 0), (sib1, 0), (sib2, 0), (sib_middle, 0), (sib_middle, 1), (sib_middle, 2)]
    sibling += [(sib3, 0), (sib4, 0)]
    far = [(v, 0) for v in (x0, x1, x2, y0, y1, y2, x3, x4)]
    far_sibling = [(v, 0) for v in (fx0, fx1, fx2, fy0, fy1, fy2, fx3, fx4)]
    places = []
    for i in range(tiles):
        places += [mine[i], sibling[i], far[i], far_sibling[i]]
    arrays = []
    for array, _ in places:
        if not any(array is other for other in arrays):
            arrays.append(array)
    where = [
        ([array is other for other in arrays].index(True), offset) for array, offset in places
    ]
    near = [own, up1, dn1, up2, dn2, up3, dn3]
    return near, arrays, where, tiles, (up1, dn1)


def shards(
    hidden_in,
    cotangent,
    base_codes,
    base_scales,
    factor_a,
    factor_b,
    task_state,
    head_a,
    head_b,
    task_ids,
    valid_counts,
    owners,
):
    f32, bf16 = jnp.float32, jnp.bfloat16
    n_groups, n_fsdp, n_dp = (lax.axis_size(a) for a in ("groups", "fsdp", "dp"))
    z, p, y = (lax.axis_index(a) for a in ("fsdp", "dp", "groups"))
    seq_len, width_part = hidden_in.shape
    tasks_all, factor_cols = factor_a.shape
    rank_double = factor_cols // width_part
    rank_half = rank_double // 2
    joined_part = cotangent.shape[1]
    joined_part_w = base_codes.shape[1]
    hidden = hidden_in[:LIVE]
    own = cotangent[:LIVE]
    lines = (n_groups, n_fsdp, n_dp) == (2, 4, 4) and width_part == 8 * TILE
    if lines:
        near, arrays, where, tiles, first = permute_plan(own, base_codes, base_scales, y)

    task = task_ids[0]
    chosen_a = lax.dynamic_slice_in_dim(factor_a, task, 1, 0).reshape(width_part, rank_double)
    chosen_b = lax.dynamic_slice_in_dim(factor_b, task, 1, 0).reshape(joined_part, rank_half)
    group_cols = (HEADS // KV_HEADS + 1) * HEAD_DIM
    columns = z * joined_part + lax.broadcasted_iota(jnp.int32, (joined_part, 1), 0)
    value_column = columns % group_cols >= HEADS // KV_HEADS * HEAD_DIM
    empty_b = jnp.zeros_like(chosen_b)
    joined_b = jnp.concatenate(
        [jnp.where(value_column, empty_b, chosen_b), jnp.where(value_column, chosen_b, empty_b)],
        axis=1,
    )
    inner_part = jnp.dot(hidden, chosen_a, preferred_element_type=f32)
    outer_part = jnp.dot(own, joined_b, preferred_element_type=f32)
    parts = jnp.concatenate([inner_part, outer_part], axis=1).astype(bf16)
    sums = jnp.sum(lax.all_gather(parts, "fsdp", axis=0).astype(f32), axis=0)
    keep = lax.broadcasted_iota(jnp.int32, (LIVE, 1), 0) < valid_counts[0]
    sums = jnp.where(keep, sums, 0.0).astype(bf16)
    low_in, low_grad = sums[:, :rank_double], sums[:, rank_double:]

    down_gradient = adapter_scale * lax.dot_general(
        hidden, low_grad, (((0,), (0,)), ((), ())), preferred_element_type=f32
    )
    mixed = lax.dot_general(own, low_in, (((0,), (0,)), ((), ())), preferred_element_type=f32)
    up_gradient = adapter_scale * jnp.where(value_column, mixed[:, rank_half:], mixed[:, :rank_half])
    down_cols = width_part * rank_double
    up_cols = joined_part * rank_half
    row = jnp.concatenate(
        [
            down_gradient.astype(bf16).reshape(1, down_cols),
            up_gradient.astype(bf16).reshape(1, up_cols),
            jnp.full((1, 128), task, f32).astype(bf16),
        ],
        axis=1,
    )
    if lines:
        row = after(row, *first)
    rows = lax.all_gather(row, "dp", axis=0, tiled=True)
    ids = rows[:, down_cols + up_cols].astype(jnp.int32)
    rows_down, rows_up = rows[:, :down_cols], rows[:, down_cols : down_cols + up_cols]
    one_hot = ids[:, None] == lax.broadcasted_iota(jnp.int32, (1, tasks_all), 1)
    states = jnp.dot(one_hot.astype(bf16), task_state, preferred_element_type=f32).astype(bf16)
    grad_head_a = lax.dot_general(
        states, rows_down, (((0,), (0,)), ((), ())), preferred_element_type=f32
    )
    grad_head_b = lax.dot_general(
        states, rows_up, (((0,), (0,)), ((), ())), preferred_element_type=f32
    )
    state_part = lax.dot_general(
        rows_down, head_a, (((1,), (1,)), ((), ())), preferred_element_type=f32
    ) + lax.dot_general(rows_up, head_b, (((1,), (1,)), ((), ())), preferred_element_type=f32)
    state_sum = jnp.sum(lax.all_gather(state_part, "fsdp", axis=0), axis=0)
    task_rows = lax.broadcasted_iota(jnp.int32, (tasks_all, tasks_all), 0)
    task_other = lax.broadcasted_iota(jnp.int32, (tasks_all, tasks_all), 1)
    same_owner = owners[:, None] == owners[None, :]
    slot_index = jnp.sum((same_owner & (task_other < task_rows)).astype(jnp.int32), axis=1)
    target = owners * SLOTS + slot_index
    seq_target = jnp.sum(jnp.where(one_hot, target[None, :], 0), axis=1)
    own_rows = z * SLOTS + lax.broadcasted_iota(jnp.int32, (SLOTS, 1), 0)
    selector = (own_rows == seq_target[None, :]).astype(f32)
    grad_state = jnp.sum(selector[:, :, None] * state_sum[None, :, :], axis=1)

    if lines:
        meta = jnp.stack([z, p, y, valid_counts[0]]).astype(jnp.int32)
        any_spec = pl.BlockSpec(memory_space=pl.ANY)
        vmem_spec = pl.BlockSpec(memory_space=pltpu.VMEM)
        depth = 4
        input_gradient = pl.pallas_call(
            lambda *refs: input_gradient_kernel(tiles, where, len(arrays), *refs),
            out_shape=jax.ShapeDtypeStruct((seq_len, width_part), bf16),
            in_specs=[pl.BlockSpec(memory_space=pltpu.SMEM), vmem_spec, vmem_spec]
            + [any_spec] * (len(near) + len(arrays)),
            out_specs=vmem_spec,
            scratch_shapes=[
                pltpu.VMEM((4, LIVE, joined_part), bf16),
                pltpu.VMEM((depth, TILE, joined_part_w), bf16),
                pltpu.SemaphoreType.DMA((4,)),
                pltpu.SemaphoreType.DMA((depth,)),
            ],
            compiler_params=pltpu.CompilerParams(vmem_limit_bytes=40 * 2**20),
        )(meta, low_grad, chosen_a, *near, *arrays)
    else:
        weight = dequantize(
            lax.all_gather(base_codes, "dp", axis=1, tiled=True),
            lax.all_gather(base_scales, "dp", axis=1, tiled=True),
        )
        merged = lax.dot_general(
            lax.all_gather(own, "fsdp", axis=1, tiled=True),
            weight,
            (((1,), (1,)), ((), ())),
            preferred_element_type=f32,
        )
        adapter = lax.dot_general(
            low_grad, chosen_a, (((1,), (1,)), ((), ())), preferred_element_type=f32
        )
        live = (jnp.where(keep, merged, 0.0) + adapter_scale * adapter).astype(bf16)
        input_gradient = jnp.pad(live, ((0, seq_len - LIVE), (0, 0)))
    return (input_gradient, grad_head_a, grad_head_b, grad_state)


def solution(mesh):
    placed = (
        P(("groups", "dp"), "fsdp"),
        P(("groups", "dp"), "fsdp"),
        P("fsdp", "dp"),
        P("fsdp", "dp"),
        P("groups", "fsdp"),
        P("groups", "fsdp"),
        P("groups", "dp"),
        P("dp", "fsdp"),
        P("dp", "fsdp"),
        P(("groups", "dp")),
        P(("groups", "dp")),
        P("groups"),
    )
    return jax.shard_map(
        shards,
        mesh=mesh,
        in_specs=placed,
        out_specs=(
            P(("groups", "dp"), "fsdp"),
            P(("groups", "dp"), "fsdp"),
            P(("groups", "dp"), "fsdp"),
            P(("groups", "fsdp"), "dp"),
        ),
        check_vma=False,
    )
```

time: 525 us -> 306 us (0.58)
  waiting for transfers between devices: 325 us -> 121 us
  Pallas kernels: 0 us -> 41.3 us
  local copies, waits for them, and re-layouts: 46.3 us -> 11 us
  other arithmetic: 32.7 us -> 1.83 us
  starting transfers between devices: 0.12 us -> 26.6 us
  matrix products: 62 us -> 43.9 us
  blocking collectives: 42.1 us -> 56.8 us
  between operations: 16 us -> 2.61 us
    all_gather x2 -> x0, waiting for transfers between devices: 304 us -> none  [the longest x1 162 us: shards(): lax.all_gather(base_codes, 'dp', axis=1, tiled=True)]
    ppermute x0 -> x28, waiting for transfers between devices: none -> 121 us  [the longest x5 45.3 us: permute_plan(): across = lambda v: lax.ppermute(v, 'dp', [(i, i ^ 2) for i in range(4)])]
    all_gather x1 -> x3, blocking collectives: 9.73 us -> 56.8 us  [the longest x1 31.7 us: shards(): rows = lax.all_gather(row, 'dp', axis=0, tiled=True)]
    pallas_call x0 -> x1, Pallas kernels: none -> 41.3 us  [shards(): pl.pallas_call(lambda *refs: input_gradient_kernel(tiles, where, len(arra...]
    unnamed x22 -> x37, local copies, waits for them, and re-layouts: 42.4 us -> 5.01 us
    convert_element_type x8 -> x3, other arithmetic: 29.1 us -> 0.22 us  [the longest x1 0.12 us: shards(): sums = jnp.where(keep, sums, 0.0).astype(bf16)]
    ppermute x0 -> x28, starting transfers between devices: none -> 26.6 us  [the longest x5 7.64 us: permute_plan(): across = lambda v: lax.ppermute(v, 'dp', [(i, i ^ 2) for i in range(4)])]
    psum x1 -> x0, blocking collectives: 20.8 us -> none  [shards(): lax.psum(outer_part.astype(jnp.bfloat16), 'fsdp').astype(jnp.float32)]
  transfers between devices with their start and end apart: 3 -> 28, of which waited for: 3 -> 9; matrix products, arithmetic and copies ran while one was open for 18% -> 15% of each run, Pallas kernels for 0% -> 0%
where the time goes in v1:
time: 306 us
  waiting for transfers between devices  121 us (40%)
  blocking collectives  56.8 us (19%)
  matrix products  43.9 us (14%)
  Pallas kernels  41.3 us (13%)
  starting transfers between devices  26.6 us (9%)
  local copies, waits for them, and re-layouts  11 us (4%)
    ppermute x5, waiting for transfers between devices, permute_plan(): across = lambda v: lax.ppermute(v, 'dp', [(i, i ^ 2) for i in range(4)])  45.3 us
    pallas_call x1, Pallas kernels, shards(): pl.pallas_call(lambda *refs: input_gradient_kernel(tiles, where, len(arra...  41.3 us
    all_gather x1, blocking collectives, shards(): rows = lax.all_gather(row, 'dp', axis=0, tiled=True)  31.7 us
    ppermute x1, waiting for transfers between devices, permute_plan(): up1 = lax.ppermute(own, 'fsdp', up(0))  28 us
    ppermute x1, waiting for transfers between devices, permute_plan(): dn3 = lax.ppermute(after(dn2, x2), 'fsdp', down(2))  24.3 us
    dot_general x6, matrix products, dequantize(): wide = jnp.dot(scales, spread, preferred_element_type=jnp.float32)  18.3 us
    all_gather x1, blocking collectives, shards(): sums = jnp.sum(lax.all_gather(parts, 'fsdp', axis=0).astype(f32), axis=0)  13.3 us
    all_gather x1, blocking collectives, shards(): state_sum = jnp.sum(lax.all_gather(state_part, 'fsdp', axis=0), axis=0)  11.9 us
  transfers between devices with their start and end apart: 28, of which 9 were waited for; matrix products, arithmetic and copies ran while one was open for 15% of the time, Pallas kernels for 0%

profile of v1, /device:TPU:0, one launch (start us, length us, event | category | flops | bytes accessed | tf_op | source)
XLA Modules:
  0.0 305.5 jit_solution(17429495625149567717)
XLA Ops:
  0.7 5.0 %multiply_convert_fusion.refs_22_ = bf16[768,2304]{1,0:T(8,128)(2,1)} fusion(bf16[2048,2304]{1,0:T(8,128)(2,1)} %param.14, s32[]{:T(128)S(6)} %select_n.79, s32[2304]{0:T(1024)S(1)} %get-tuple-element.52, s32[2304]{0:T(1024)S(1)} %get-tuple-element.53, pred[2304]{0:T(1024)(128)(4,1)S(1)} %fusion.63, bf16[2048,36]{0,1:T(8,128)(2,1)} %param.15), kind=kOutput, calls=%fused_computation | convolution fusion | flops 132876288 | bytes 7161088 | tf_op jit(solution)/shard_map/dot_general | solution.py:25
  6.2 1.8 fusion.4.refs_10_
  7.9 4.4 %collective-permute-done.8.refs_23_ = bf16[768,2304]{1,0:T(8,128)(2,1)} collective-permute-done((bf16[768,2304]{1,0:T(8,128)(2,1)}, bf16[768,2304]{1,0:T(8,128)(2,1)}, u32[]{:S(2)}, u32[]{:S(2)}) %collective-permute-start.8) | collective-permute-done | bytes 3538976 | tf_op jit(solution)/shard_map/ppermute | solution.py:108
  12.7 2.8 fusion.6.refs_14_
  15.7 2.9 collective-permute-start.2
  18.6 3.0 fusion.5.refs_18_
  21.8 23.7 %collective-permute-done.2.refs_12_ = bf16[256,2304]{1,0:T(8,128)(2,1)} collective-permute-done((bf16[256,2304]{1,0:T(8,128)(2,1)S(1)}, bf16[256,2304]{1,0:T(8,128)(2,1)}, u32[]{:S(2)}, u32[]{:S(2)}) %collective-permute-start.2) | collective-permute-done | bytes 1179680 | tf_op jit(solution)/shard_map/ppermute | solution.py:107
  46.5 2.1 collective-permute-start.13
  48.6 21.6 %collective-permute-done.10.refs_16_ = bf16[256,2304]{1,0:T(8,128)(2,1)} collective-permute-done((bf16[256,2304]{1,0:T(8,128)(2,1)}, bf16[256,2304]{1,0:T(8,128)(2,1)}, u32[]{:S(2)}, u32[]{:S(2)}) %collective-permute-start.10) | collective-permute-done | bytes 1179680 | tf_op jit(solution)/shard_map/ppermute | solution.py:107
  70.2 3.6 %collective-permute-done.13.refs_24_ = bf16[256,2304]{1,0:T(8,128)(2,1)} collective-permute-done((bf16[256,2304]{1,0:T(8,128)(2,1)}, bf16[256,2304]{1,0:T(8,128)(2,1)}, u32[]{:S(2)}, u32[]{:S(2)}) %collective-permute-start.13) | collective-permute-done | bytes 1179680 | tf_op jit(solution)/shard_map/ppermute | solution.py:109
  75.2 4.7 %collective-permute-start = (bf16[384,2304]{1,0:T(8,128)(2,1)}, bf16[384,2304]{1,0:T(8,128)(2,1)}, u32[]{:S(2)}, u32[]{:S(2)}) collective-permute-start(bf16[384,2304]{1,0:T(8,128)(2,1)} %slice.28.refs_3_), channel_id=1, source_target_pairs={{0,4},{4,8},{8,12},{1,5},{5,9},{9,13},{2,6},{6,10},{10,14},{3,7},{... | collective-permute-start | bytes 5308424 | tf_op jit(solution)/shard_map/ppermute | solution.py:117
  81.2 1.5 collective-permute-start.5
  86.5 2.9 fusion.3.refs_30_
  89.5 28.0 %collective-permute-done.refs_4_ = bf16[384,2304]{1,0:T(8,128)(2,1)} collective-permute-done((bf16[384,2304]{1,0:T(8,128)(2,1)}, bf16[384,2304]{1,0:T(8,128)(2,1)}, u32[]{:S(2)}, u32[]{:S(2)}) %collective-permute-start) | collective-permute-done | bytes 1769504 | tf_op jit(solution)/shard_map/ppermute | solution.py:117
  117.5 5.3 %collective-permute-done.1.refs_5_ = bf16[384,2304]{1,0:T(8,128)(2,1)} collective-permute-done((bf16[384,2304]{1,0:T(8,128)(2,1)}, bf16[384,2304]{1,0:T(8,128)(2,1)}, u32[]{:S(2)}, u32[]{:S(2)}) %collective-permute-start.1) | collective-permute-done | bytes 1769504 | tf_op jit(solution)/shard_map/ppermute | solution.py:118
  122.8 1.5 collective-permute-start.16
  126.2 1.9 fusion.16
  128.2 13.3 %all_gather.13 = bf16[4,384,32]{1,2,0:T(8,128)(2,1)S(1)} all-gather(bf16[1,384,32]{1,2,0:T(8,128)(2,1)S(1)} %pad_maximum_fusion), channel_id=1, replica_groups=mesh['groups'=2,'fsdp'=4,'dp'=4] {'fsdp'}, dimensions={0}, use_global_device_ids=true | all-gather | bytes 122880 | tf_op jit(solution)/shard_map/all_gather | solution.py:212
  142.5 2.8 fusion.2.refs_34_
  145.3 5.1 %collective-permute-done.16.refs_26_ = bf16[256,2304]{1,0:T(8,128)(2,1)} collective-permute-done((bf16[256,2304]{1,0:T(8,128)(2,1)}, bf16[256,2304]{1,0:T(8,128)(2,1)}, u32[]{:S(2)}, u32[]{:S(2)}) %collective-permute-start.16) | collective-permute-done | bytes 1179680 | tf_op jit(solution)/shard_map/ppermute | solution.py:109
  152.2 1.8 fusion.8
  154.8 1.9 collective-permute-start.3
  160.3 31.7 %all-gather.1 = bf16[4,1,51328]{2,1,0:T(2,128)(2,1)S(1)} all-gather(bf16[1,1,51328]{2,1,0:T(2,128)(2,1)S(1)} %bitcast.53), channel_id=1, replica_groups=mesh['groups'=2,'fsdp'=4,'dp'=4] {'dp'}, dimensions={0}, use_global_device_ids=true | all-gather | bytes 513280 | tf_op jit(solution)/shard_map/all_gather | solution.py:234
  192.2 1.5 collective-permute-start.26
  193.7 1.5 collective-permute-start.22
  195.2 5.4 %collective-permute-done.4.refs_7_ = bf16[384,2304]{1,0:T(8,128)(2,1)} collective-permute-done((bf16[384,2304]{1,0:T(8,128)(2,1)}, bf16[384,2304]{1,0:T(8,128)(2,1)}, u32[]{:S(2)}, u32[]{:S(2)}) %collective-permute-start.4) | collective-permute-done | bytes 1769504 | tf_op jit(solution)/shard_map/ppermute | solution.py:133
  200.6 5.7 %fusion.20 = f32[4,128]{1,0:T(4,128)S(1)} fusion(bf16[128,32768]{1,0:T(8,128)(2,1)} %param.19, bf16[4,51328]{1,0:T(4,128)(2,1)S(1)} %bitcast.48), kind=kOutput, calls=%fused_computation.30 | convolution fusion | flops 33554432 | bytes 8652800 | tf_op jit(solution)/shard_map/dot_general | solution.py:245
  207.7 11.9 %all-gather.2 = f32[4,4,128]{2,1,0:T(4,128)S(1)} all-gather(f32[1,4,128]{2,1,0:T(4,128)S(1)} %fusion.19), channel_id=2, replica_groups=mesh['groups'=2,'fsdp'=4,'dp'=4] {'fsdp'}, dimensions={0}, use_global_device_ids=true | all-gather | bytes 10240 | tf_op jit(solution)/shard_map/all_gather | solution.py:248
  223.4 5.2 %fusion.43 = f32[128,18432]{1,0:T(8,128)} fusion(bf16[4,128]{1,0:T(4,128)(2,1)S(1)} %convolution_convert_fusion.1, bf16[4,51328]{1,0:T(4,128)(2,1)S(1)} %bitcast.51), kind=kOutput, calls=%fused_computation.56 | convolution fusion | flops 18874368 | bytes 9585664 | tf_op jit(solution)/shard_map/dot_general | solution.py:242
  228.6 8.5 %fusion.22 = f32[128,32768]{1,0:T(8,128)} fusion(bf16[4,128]{1,0:T(4,128)(2,1)S(1)} %convolution_convert_fusion.1, bf16[4,51328]{1,0:T(4,128)(2,1)S(1)} %bitcast.52), kind=kOutput, calls=%fused_computation.32 | convolution fusion | flops 33554432 | bytes 17040384 | tf_op jit(solution)/shard_map/dot_general | solution.py:239
  237.1 24.3 %collective-permute-done.7.refs_9_ = bf16[384,2304]{1,0:T(8,128)(2,1)S(1)} collective-permute-done((bf16[384,2304]{1,0:T(8,128)(2,1)}, bf16[384,2304]{1,0:T(8,128)(2,1)S(1)}, u32[]{:S(2)}, u32[]{:S(2)}) %collective-permute-start.7) | collective-permute-done | bytes 1769504 | tf_op jit(solution)/shard_map/ppermute | solution.py:145
  264.1 41.3 %shard_map.147 = bf16[512,2048]{1,0:T(8,128)(2,1)} custom-call(s32[4]{0:T(128)S(1)} %pad_add_fusion.refs_0_, bf16[384,16]{1,0:T(8,128)(2,1)S(1)} %slice.36.refs_1_, bf16[2048,16]{1,0:T(8,128)(2,1)S(1)} %reshape.111.refs_2_, bf16[384,2304]{1,0:T(8,128)(2,1)} %slice.28.refs_3_, bf16[384,2304]{1,0:T(8,128)(2,1)} %collective-permute-done.refs_4_, ...), custom_call_target="tpu_custom_call" | custom-call | tf_op jit(solution)/shard_map/pallas_call | solution.py:264
  (114 shorter events, 24.3 us)
Async XLA Ops:
  0.6 124.8 %copy-start = (bf16[16,32768]{1,0:T(8,128)(2,1)S(1)}, bf16[16,32768]{1,0:T(8,128)(2,1)}, u32[]{:S(2)}) copy-start(bf16[16,32768]{1,0:T(8,128)(2,1)} %param.16) | copy-start | bytes 3145732
  5.7 6.6 %collective-permute-start.8 = (bf16[768,2304]{1,0:T(8,128)(2,1)}, bf16[768,2304]{1,0:T(8,128)(2,1)}, u32[]{:S(2)}, u32[]{:S(2)}) collective-permute-start(bf16[768,2304]{1,0:T(8,128)(2,1)} %multiply_convert_fusion.refs_22_), channel_id=1, source_target_pairs={{0,1},{1,0},{2,3},{3,2},{4,5},{5,4},{6,7},{7,6},{8,9},{9,8},{10,11... | collective-permute-start | bytes 10616840 | tf_op jit(solution)/shard_map/ppermute | solution.py:108
  12.4 3.2 %collective-permute-start.9 = (bf16[256,2304]{1,0:T(8,128)(2,1)S(1)}, bf16[256,2304]{1,0:T(8,128)(2,1)}, u32[]{:S(2)}, u32[]{:S(2)}) collective-permute-start(bf16[256,2304]{1,0:T(8,128)(2,1)S(1)} %fusion.4.refs_10_), channel_id=1, source_target_pairs={{0,1},{1,0},{2,3},{3,2},{4,5},{5,4},{6,7},{7,6},{8,9},{9,8},{10,11... | collective-permute-start | bytes 3538952 | tf_op jit(solution)/shard_map/ppermute | solution.py:108
  15.6 6.0 %collective-permute-start.11 = (bf16[256,2304]{1,0:T(8,128)(2,1)}, bf16[256,2304]{1,0:T(8,128)(2,1)}, u32[]{:S(2)}, u32[]{:S(2)}) collective-permute-start(bf16[256,2304]{1,0:T(8,128)(2,1)} %fusion.6.refs_14_), channel_id=1, source_target_pairs={{0,1},{1,0},{2,3},{3,2},{4,5},{5,4},{6,7},{7,6},{8,9},{9,8},{10,11... | collective-permute-start | bytes 3538952 | tf_op jit(solution)/shard_map/ppermute | solution.py:108
  15.7 29.7 %collective-permute-start.2 = (bf16[256,2304]{1,0:T(8,128)(2,1)S(1)}, bf16[256,2304]{1,0:T(8,128)(2,1)}, u32[]{:S(2)}, u32[]{:S(2)}) collective-permute-start(bf16[256,2304]{1,0:T(8,128)(2,1)S(1)} %fusion.4.refs_10_), channel_id=1, source_target_pairs={{0,2},{1,3},{2,0},{3,1},{4,6},{5,7},{6,4},{7,5},{8,10},{9,11},{10,... | collective-permute-start | bytes 3538952 | tf_op jit(solution)/shard_map/ppermute | solution.py:107
  18.6 55.3 %copy-start.6 = (bf16[512,2304]{1,0:T(8,128)(2,1)S(1)}, bf16[512,2304]{1,0:T(8,128)(2,1)}, u32[]{:S(2)}) copy-start(bf16[512,2304]{1,0:T(8,128)(2,1)} %param.13) | copy-start | bytes 7077892
  21.5 23.9 %collective-permute-start.12 = (bf16[256,2304]{1,0:T(8,128)(2,1)}, bf16[256,2304]{1,0:T(8,128)(2,1)S(1)}, u32[]{:S(2)}, u32[]{:S(2)}) collective-permute-start(bf16[256,2304]{1,0:T(8,128)(2,1)} %fusion.5.refs_18_), channel_id=1, source_target_pairs={{0,1},{1,0},{2,3},{3,2},{4,5},{5,4},{6,7},{7,6},{8,9},{9,8},{10,11... | collective-permute-start | bytes 3538952 | tf_op jit(solution)/shard_map/ppermute | solution.py:108
  21.5 48.7 %collective-permute-start.10 = (bf16[256,2304]{1,0:T(8,128)(2,1)}, bf16[256,2304]{1,0:T(8,128)(2,1)}, u32[]{:S(2)}, u32[]{:S(2)}) collective-permute-start(bf16[256,2304]{1,0:T(8,128)(2,1)} %fusion.6.refs_14_), channel_id=1, source_target_pairs={{0,2},{1,3},{2,0},{3,1},{4,6},{5,7},{6,4},{7,5},{8,10},{9,11},{10,... | collective-permute-start | bytes 3538952 | tf_op jit(solution)/shard_map/ppermute | solution.py:107
  46.5 27.3 %collective-permute-start.13 = (bf16[256,2304]{1,0:T(8,128)(2,1)}, bf16[256,2304]{1,0:T(8,128)(2,1)}, u32[]{:S(2)}, u32[]{:S(2)}) collective-permute-start(bf16[256,2304]{1,0:T(8,128)(2,1)} %collective-permute-done.2.refs_12_), channel_id=1, source_target_pairs={{0,16},{16,0},{1,17},{17,1},{2,18},{18,2},{3,19},{19,3},{4,20},{20... | collective-permute-start | bytes 3538952 | tf_op jit(solution)/shard_map/ppermute | solution.py:109
  73.8 8.9 %collective-permute-start.14 = (bf16[256,2304]{1,0:T(8,128)(2,1)}, bf16[256,2304]{1,0:T(8,128)(2,1)S(1)}, u32[]{:S(2)}, u32[]{:S(2)}) collective-permute-start(bf16[256,2304]{1,0:T(8,128)(2,1)} %collective-permute-done.2.refs_12_), channel_id=1, source_target_pairs={{0,1},{1,0},{2,3},{3,2},{4,5},{5,4},{6,7},{7,6},{8,9},{9,8},{10,11... | collective-permute-start | bytes 3538952 | tf_op jit(solution)/shard_map/ppermute | solution.py:108
  75.2 42.3 %collective-permute-start = (bf16[384,2304]{1,0:T(8,128)(2,1)}, bf16[384,2304]{1,0:T(8,128)(2,1)}, u32[]{:S(2)}, u32[]{:S(2)}) collective-permute-start(bf16[384,2304]{1,0:T(8,128)(2,1)} %slice.28.refs_3_), channel_id=1, source_target_pairs={{0,4},{4,8},{8,12},{1,5},{5,9},{9,13},{2,6},{6,10},{10,14},{3,7},{... | collective-permute-start | bytes 5308424 | tf_op jit(solution)/shard_map/ppermute | solution.py:117
  79.9 42.9 %collective-permute-start.1 = (bf16[384,2304]{1,0:T(8,128)(2,1)}, bf16[384,2304]{1,0:T(8,128)(2,1)}, u32[]{:S(2)}, u32[]{:S(2)}) collective-permute-start(bf16[384,2304]{1,0:T(8,128)(2,1)} %slice.28.refs_3_), channel_id=1, source_target_pairs={{4,0},{8,4},{12,8},{5,1},{9,5},{13,9},{6,2},{10,6},{14,10},{7,3},{... | collective-permute-start | bytes 5308424 | tf_op jit(solution)/shard_map/ppermute | solution.py:118
  81.2 43.2 %collective-permute-start.5 = (bf16[256,2304]{1,0:T(8,128)(2,1)}, bf16[256,2304]{1,0:T(8,128)(2,1)}, u32[]{:S(2)}, u32[]{:S(2)}) collective-permute-start(bf16[256,2304]{1,0:T(8,128)(2,1)} %fusion.5.refs_18_), channel_id=1, source_target_pairs={{0,2},{1,3},{2,0},{3,1},{4,6},{5,7},{6,4},{7,5},{8,10},{9,11},{10,... | collective-permute-start | bytes 3538952 | tf_op jit(solution)/shard_map/ppermute | solution.py:107
  83.7 40.6 %collective-permute-start.19 = (bf16[256,2304]{1,0:T(8,128)(2,1)}, bf16[256,2304]{1,0:T(8,128)(2,1)}, u32[]{:S(2)}, u32[]{:S(2)}) collective-permute-start(bf16[256,2304]{1,0:T(8,128)(2,1)} %collective-permute-done.13.refs_24_), channel_id=1, source_target_pairs={{0,1},{1,0},{2,3},{3,2},{4,5},{5,4},{6,7},{7,6},{8,9},{9,8},{10,11... | collective-permute-start | bytes 3538952 | tf_op jit(solution)/shard_map/ppermute | solution.py:108
  86.5 38.4 %copy-start.7 = (bf16[512,2304]{1,0:T(8,128)(2,1)S(1)}, bf16[512,2304]{1,0:T(8,128)(2,1)}, u32[]{:S(2)}) copy-start(bf16[512,2304]{1,0:T(8,128)(2,1)} %param.13) | copy-start | bytes 7077892
  122.8 27.6 %collective-permute-start.16 = (bf16[256,2304]{1,0:T(8,128)(2,1)}, bf16[256,2304]{1,0:T(8,128)(2,1)}, u32[]{:S(2)}, u32[]{:S(2)}) collective-permute-start(bf16[256,2304]{1,0:T(8,128)(2,1)} %collective-permute-done.10.refs_16_), channel_id=1, source_target_pairs={{0,16},{16,0},{1,17},{17,1},{2,18},{18,2},{3,19},{19,3},{4,20},{20... | collective-permute-start | bytes 3538952 | tf_op jit(solution)/shard_map/ppermute | solution.py:109
  124.3 26.1 %collective-permute-start.15 = (bf16[256,2304]{1,0:T(8,128)(2,1)}, bf16[256,2304]{1,0:T(8,128)(2,1)}, u32[]{:S(2)}, u32[]{:S(2)}) collective-permute-start(bf16[256,2304]{1,0:T(8,128)(2,1)} %collective-permute-done.10.refs_16_), channel_id=1, source_target_pairs={{0,1},{1,0},{2,3},{3,2},{4,5},{5,4},{6,7},{7,6},{8,9},{9,8},{10,11... | collective-permute-start | bytes 3538952 | tf_op jit(solution)/shard_map/ppermute | solution.py:108
  124.3 26.1 %collective-permute-start.20 = (bf16[256,2304]{1,0:T(8,128)(2,1)}, bf16[256,2304]{1,0:T(8,128)(2,1)}, u32[]{:S(2)}, u32[]{:S(2)}) collective-permute-start(bf16[256,2304]{1,0:T(8,128)(2,1)} %fusion.3.refs_30_), channel_id=1, source_target_pairs={{0,1},{1,0},{2,3},{3,2},{4,5},{5,4},{6,7},{7,6},{8,9},{9,8},{10,11... | collective-permute-start | bytes 3538952 | tf_op jit(solution)/shard_map/ppermute | solution.py:108
  150.4 7.5 %collective-permute-start.17 = (bf16[256,2304]{1,0:T(8,128)(2,1)}, bf16[256,2304]{1,0:T(8,128)(2,1)}, u32[]{:S(2)}, u32[]{:S(2)}) collective-permute-start(bf16[256,2304]{1,0:T(8,128)(2,1)} %collective-permute-done.16.refs_26_), channel_id=1, source_target_pairs={{0,1},{1,0},{2,3},{3,2},{4,5},{5,4},{6,7},{7,6},{8,9},{9,8},{10,11... | collective-permute-start | bytes 3538952 | tf_op jit(solution)/shard_map/ppermute | solution.py:108
  150.4 7.7 %collective-permute-start.21 = (bf16[256,2304]{1,0:T(8,128)(2,1)}, bf16[256,2304]{1,0:T(8,128)(2,1)}, u32[]{:S(2)}, u32[]{:S(2)}) collective-permute-start(bf16[256,2304]{1,0:T(8,128)(2,1)} %fusion.2.refs_34_), channel_id=1, source_target_pairs={{0,1},{1,0},{2,3},{3,2},{4,5},{5,4},{6,7},{7,6},{8,9},{9,8},{10,11... | collective-permute-start | bytes 3538952 | tf_op jit(solution)/shard_map/ppermute | solution.py:108
  154.8 40.5 %collective-permute-start.3 = (bf16[384,2304]{1,0:T(8,128)(2,1)}, bf16[384,2304]{1,0:T(8,128)(2,1)}, u32[]{:S(2)}, u32[]{:S(2)}) collective-permute-start(bf16[384,2304]{1,0:T(8,128)(2,1)} %collective-permute-done.refs_4_), channel_id=1, source_target_pairs={{4,8},{8,12},{5,9},{9,13},{6,10},{10,14},{7,11},{11,15},{20,24},{2... | collective-permute-start | bytes 5308424 | tf_op jit(solution)/shard_map/ppermute | solution.py:132
  156.7 43.9 %collective-permute-start.4 = (bf16[384,2304]{1,0:T(8,128)(2,1)}, bf16[384,2304]{1,0:T(8,128)(2,1)}, u32[]{:S(2)}, u32[]{:S(2)}) collective-permute-start(bf16[384,2304]{1,0:T(8,128)(2,1)} %collective-permute-done.1.refs_5_), channel_id=1, source_target_pairs={{4,0},{8,4},{5,1},{9,5},{6,2},{10,6},{7,3},{11,7},{20,16},{24,20},... | collective-permute-start | bytes 5308424 | tf_op jit(solution)/shard_map/ppermute | solution.py:133
  158.0 34.2 %collective-permute-start.18 = (bf16[256,2304]{1,0:T(8,128)(2,1)}, bf16[256,2304]{1,0:T(8,128)(2,1)}, u32[]{:S(2)}, u32[]{:S(2)}) collective-permute-start(bf16[256,2304]{1,0:T(8,128)(2,1)} %collective-permute-done.5.refs_20_), channel_id=1, source_target_pairs={{0,1},{1,0},{2,3},{3,2},{4,5},{5,4},{6,7},{7,6},{8,9},{9,8},{10,11... | collective-permute-start | bytes 3538952 | tf_op jit(solution)/shard_map/ppermute | solution.py:108
  158.1 42.5 %collective-permute-start.23 = (bf16[256,2304]{1,0:T(8,128)(2,1)}, bf16[256,2304]{1,0:T(8,128)(2,1)}, u32[]{:S(2)}, u32[]{:S(2)}) collective-permute-start(bf16[256,2304]{1,0:T(8,128)(2,1)} %fusion.3.refs_30_), channel_id=1, source_target_pairs={{0,2},{1,3},{2,0},{3,1},{4,6},{5,7},{6,4},{7,5},{8,10},{9,11},{10,... | collective-permute-start | bytes 3538952 | tf_op jit(solution)/shard_map/ppermute | solution.py:107
  192.2 30.0 %collective-permute-start.26 = (bf16[256,2304]{1,0:T(8,128)(2,1)}, bf16[256,2304]{1,0:T(8,128)(2,1)}, u32[]{:S(2)}, u32[]{:S(2)}) collective-permute-start(bf16[256,2304]{1,0:T(8,128)(2,1)} %fusion.2.refs_34_), channel_id=1, source_target_pairs={{0,2},{1,3},{2,0},{3,1},{4,6},{5,7},{6,4},{7,5},{8,10},{9,11},{10,... | collective-permute-start | bytes 3538952 | tf_op jit(solution)/shard_map/ppermute | solution.py:107
  193.7 28.5 %collective-permute-start.22 = (bf16[256,2304]{1,0:T(8,128)(2,1)}, bf16[256,2304]{1,0:T(8,128)(2,1)}, u32[]{:S(2)}, u32[]{:S(2)}) collective-permute-start(bf16[256,2304]{1,0:T(8,128)(2,1)} %collective-permute-done.5.refs_20_), channel_id=1, source_target_pairs={{0,16},{16,0},{1,17},{17,1},{2,18},{18,2},{3,19},{19,3},{4,20},{20... | collective-permute-start | bytes 3538952 | tf_op jit(solution)/shard_map/ppermute | solution.py:109
  200.6 21.6 %collective-permute-start.24 = (bf16[256,2304]{1,0:T(8,128)(2,1)}, bf16[256,2304]{1,0:T(8,128)(2,1)}, u32[]{:S(2)}, u32[]{:S(2)}) collective-permute-start(bf16[256,2304]{1,0:T(8,128)(2,1)} %collective-permute-done.23.refs_32_), channel_id=1, source_target_pairs={{0,1},{1,0},{2,3},{3,2},{4,5},{5,4},{6,7},{7,6},{8,9},{9,8},{10,11... | collective-permute-start | bytes 3538952 | tf_op jit(solution)/shard_map/ppermute | solution.py:108
  219.7 17.4 %collective-permute-start.6 = (bf16[384,2304]{1,0:T(8,128)(2,1)}, bf16[384,2304]{1,0:T(8,128)(2,1)S(1)}, u32[]{:S(2)}, u32[]{:S(2)}) collective-permute-start(bf16[384,2304]{1,0:T(8,128)(2,1)} %collective-permute-done.3.refs_6_), channel_id=1, source_target_pairs={{8,12},{9,13},{10,14},{11,15},{24,28},{25,29},{26,30},{27,31}} | collective-permute-start | bytes 5308424 | tf_op jit(solution)/shard_map/ppermute | solution.py:144
  220.5 40.9 %collective-permute-start.7 = (bf16[384,2304]{1,0:T(8,128)(2,1)}, bf16[384,2304]{1,0:T(8,128)(2,1)S(1)}, u32[]{:S(2)}, u32[]{:S(2)}) collective-permute-start(bf16[384,2304]{1,0:T(8,128)(2,1)} %collective-permute-done.4.refs_7_), channel_id=1, source_target_pairs={{4,0},{5,1},{6,2},{7,3},{20,16},{21,17},{22,18},{23,19}} | collective-permute-start | bytes 5308424 | tf_op jit(solution)/shard_map/ppermute | solution.py:145
  222.2 39.2 %collective-permute-start.27 = (bf16[256,2304]{1,0:T(8,128)(2,1)}, bf16[256,2304]{1,0:T(8,128)(2,1)S(1)}, u32[]{:S(2)}, u32[]{:S(2)}) collective-permute-start(bf16[256,2304]{1,0:T(8,128)(2,1)} %collective-permute-done.26.refs_36_), channel_id=1, source_target_pairs={{0,1},{1,0},{2,3},{3,2},{4,5},{5,4},{6,7},{7,6},{8,9},{9,8},{10,11... | collective-permute-start | bytes 3538952 | tf_op jit(solution)/shard_map/ppermute | solution.py:108
  222.2 39.2 %collective-permute-start.25 = (bf16[256,2304]{1,0:T(8,128)(2,1)}, bf16[256,2304]{1,0:T(8,128)(2,1)S(1)}, u32[]{:S(2)}, u32[]{:S(2)}) collective-permute-start(bf16[256,2304]{1,0:T(8,128)(2,1)} %collective-permute-done.22.refs_28_), channel_id=1, source_target_pairs={{0,1},{1,0},{2,3},{3,2},{4,5},{5,4},{6,7},{7,6},{8,9},{9,8},{10,11... | collective-permute-start | bytes 3538952 | tf_op jit(solution)/shard_map/ppermute | solution.py:108
  264.1 41.3 %copy-start.1 = (bf16[16,32768]{1,0:T(8,128)(2,1)S(1)}, bf16[16,32768]{1,0:T(8,128)(2,1)}, u32[]{:S(2)}) copy-start(bf16[16,32768]{1,0:T(8,128)(2,1)} %param.16) | copy-start | bytes 3145732
  (14 other events, 160.3 us)

commit v2 on v1

--- a/solution.py
+++ b/solution.py
@@ -1,3 +1,5 @@
+import math
+
 import jax
 import jax.numpy as jnp
 from jax import lax
@@ -17,13 +19,117 @@
 
 
 def dequantize(codes, scales):
-    cols, blocks = codes.shape[1], scales.shape[1]
+    rows, cols = codes.shape
+    blocks = scales.shape[1]
+    return (
+        (
+            codes.astype(jnp.float32).reshape(rows, blocks, QBLOCK)
+            * scales.astype(jnp.float32)[:, :, None]
+        )
+        .reshape(rows, cols)
+        .astype(jnp.bfloat16)
+    )
+
+
+def weight_kernel(group, codes, scales, out):
+    cols, blocks = codes.shape[1], scales.shape[0]
     spread = (
-        lax.broadcasted_iota(jnp.int32, (blocks, cols), 1) // QBLOCK
-        == lax.broadcasted_iota(jnp.int32, (blocks, cols), 0)
+        lax.broadcasted_iota(jnp.int32, (cols, blocks), 0) // QBLOCK
+        == lax.broadcasted_iota(jnp.int32, (cols, blocks), 1)
     ).astype(jnp.bfloat16)
-    wide = jnp.dot(scales, spread, preferred_element_type=jnp.float32)
-    return (codes.astype(jnp.float32) * wide).astype(jnp.bfloat16)
+    wide = jnp.dot(spread, scales[...], preferred_element_type=jnp.float32)
+    out[0] = (jnp.transpose(codes[...]).astype(jnp.float32) * wide).astype(jnp.bfloat16)
+
+
+def weight_tiles(group, codes, scales, first, count, half):
+    cols, blocks = codes.shape[1], scales.shape[0]
+
+    def place(i, group):
+        at = first + i
+        moved = jnp.where(at < half, at + group[0] * half, at - group[0] * half)
+        return jnp.where(at < 2 * half, moved, at)
+
+    return pl.pallas_call(
+        weight_kernel,
+        out_shape=jax.ShapeDtypeStruct((count, cols, TILE), jnp.bfloat16),
+        grid_spec=pltpu.PrefetchScalarGridSpec(
+            num_scalar_prefetch=1,
+            grid=(count,),
+            in_specs=[
+                pl.BlockSpec((TILE, cols), lambda i, group: (place(i, group), 0)),
+                pl.BlockSpec((blocks, TILE), lambda i, group: (0, place(i, group))),
+            ],
+            out_specs=pl.BlockSpec((1, cols, TILE), lambda i, group: (i, 0, 0)),
+        ),
+        compiler_params=pltpu.CompilerParams(vmem_limit_bytes=32 * 2**20),
+        cost_estimate=pl.CostEstimate(flops=0, transcendentals=0, bytes_accessed=0),
+    )(group, codes, scales)
+
+
+def product_kernel(hidden, cotangent, chosen, joined, out):
+    inner = jnp.dot(hidden[:LIVE, :], chosen[...], preferred_element_type=jnp.float32)
+    outer = jnp.dot(cotangent[:LIVE, :], joined[...], preferred_element_type=jnp.float32)
+    out[...] = jnp.concatenate([inner, outer], axis=1).astype(out.dtype)
+
+
+def factor_kernel(hidden, cotangent, grad, low, down, up):
+    contract = (((0,), (0,)), ((), ()))
+    down[...] = adapter_scale * lax.dot_general(
+        hidden[:LIVE, :], grad[...], contract, preferred_element_type=jnp.float32
+    )
+    up[...] = adapter_scale * lax.dot_general(
+        cotangent[:LIVE, :], low[...], contract, preferred_element_type=jnp.float32
+    )
+
+
+def head_kernel(states, rows, head, grad, part):
+    grad[...] = lax.dot_general(
+        states[...], rows[...], (((0,), (0,)), ((), ())), preferred_element_type=jnp.float32
+    )
+
+    @pl.when(pl.program_id(0) == 0)
+    def _():
+        part[...] = jnp.zeros_like(part)
+
+    part[...] += lax.dot_general(
+        rows[...], head[...], (((1,), (1,)), ((), ())), preferred_element_type=jnp.float32
+    )
+
+
+def head_grads(states, rows, head, first, block):
+    hidden_units, cols = head.shape
+    sequences = rows.shape[0]
+    return pl.pallas_call(
+        head_kernel,
+        out_shape=[
+            jax.ShapeDtypeStruct((hidden_units, cols), jnp.float32),
+            jax.ShapeDtypeStruct((sequences, hidden_units), jnp.float32),
+        ],
+        grid=(cols // block,),
+        in_specs=[
+            pl.BlockSpec((sequences, hidden_units), lambda i: (0, 0)),
+            pl.BlockSpec((sequences, block), lambda i: (0, first // block + i)),
+            pl.BlockSpec((hidden_units, block), lambda i: (0, i)),
+        ],
+        out_specs=[
+            pl.BlockSpec((hidden_units, block), lambda i: (0, i)),
+            pl.BlockSpec((sequences, hidden_units), lambda i: (0, 0)),
+        ],
+        compiler_params=pltpu.CompilerParams(vmem_limit_bytes=32 * 2**20),
+        cost_estimate=pl.CostEstimate(flops=0, transcendentals=0, bytes_accessed=0),
+    )(states, rows, head)
+
+
+def whole_call(kernel, out_shape, *operands):
+    spec = pl.BlockSpec(memory_space=pltpu.VMEM)
+    return pl.pallas_call(
+        kernel,
+        out_shape=out_shape,
+        in_specs=[spec] * len(operands),
+        out_specs=jax.tree.map(lambda _: spec, out_shape),
+        compiler_params=pltpu.CompilerParams(vmem_limit_bytes=32 * 2**20),
+        cost_estimate=pl.CostEstimate(flops=0, transcendentals=0, bytes_accessed=0),
+    )(*operands)
 
 
 def after(value, *done):
@@ -35,7 +141,7 @@
     near = refs[3:10]
     arrays = refs[10 : 10 + count]
     out, cot, wbuf, csem, wsem = refs[10 + count :]
-    weights = [arrays[index].at[pl.ds(offset * TILE, TILE)] for index, offset in where]
+    weights = [arrays[index].at[offset] for index, offset in where]
     z, p, y, valid = meta[0], meta[1], meta[2], meta[3]
     own, up1, dn1, up2, dn2, up3, dn3 = near
     depth = wbuf.shape[0]
@@ -91,79 +197,78 @@
             total = total + lax.dot_general(
                 cot[block],
                 wbuf[slot],
-                (((1,), (1,)), ((), ())),
+                (((1,), (0,)), ((), ())),
                 preferred_element_type=jnp.float32,
             )
         result = jnp.where(keep, total, 0.0) + acc
         out[:LIVE, pl.ds(start, TILE)] = result.astype(out.dtype)
 
 
+def gather_kernel(*refs):
+    inputs, out, sem = refs[:-2], refs[-2], refs[-1]
+    for i, ref in enumerate(inputs):
+        pltpu.make_async_copy(ref, out.at[pl.ds(i, 1)], sem.at[i]).start()
+    for i, ref in enumerate(inputs):
+        pltpu.make_async_copy(ref, out.at[pl.ds(i, 1)], sem.at[i]).wait()
+
+
+def gather_tiles(tiles):
+    spec = pl.BlockSpec(memory_space=pl.ANY)
+    return pl.pallas_call(
+        gather_kernel,
+        out_shape=jax.ShapeDtypeStruct((len(tiles),) + tiles[0].shape[1:], tiles[0].dtype),
+        in_specs=[spec] * len(tiles),
+        out_specs=spec,
+        scratch_shapes=[pltpu.SemaphoreType.DMA((len(tiles),))],
+        cost_estimate=pl.CostEstimate(flops=0, transcendentals=0, bytes_accessed=0),
+    )(*tiles)
+
+
 def permute_plan(own, codes, scales, y):
-    rows = codes.shape[0]
-    tiles = rows // TILE
+    tiles = codes.shape[0] // TILE
     half = (tiles - 2) // 2
     up = lambda step: [(i, i + 1) for i in range(step, 3)]
     down = lambda step: [(i + 1, i) for i in range(0, 3 - step)]
     across = lambda v: lax.ppermute(v, "dp", [(i, i ^ 2) for i in range(4)])
     core = lambda v: lax.ppermute(v, "dp", [(i, i ^ 1) for i in range(4)])
     over = lambda v: lax.ppermute(v, "groups", [(0, 1), (1, 0)])
-
-    def part(start, size):
-        return dequantize(
-            lax.dynamic_slice_in_dim(codes, start, size, 0),
-            lax.dynamic_slice_in_dim(scales, start, size, 0),
-        )
+    group = y.astype(jnp.int32).reshape(1)
+    columns = scales.T
 
     up1 = lax.ppermute(own, "fsdp", up(0))
     dn1 = lax.ppermute(own, "fsdp", down(0))
-    near_tiles = [part((y * half + i) * TILE, TILE) for i in range(half)]
-    last_tiles = [part((2 * half + i) * TILE, TILE) for i in range(2)]
-    middle = part((1 - y) * half * TILE, half * TILE)
-    m0, m1, m2 = near_tiles
-    e0, e1 = last_tiles
-    x0 = across(m0)
-    x1 = across(m1)
-    sib_middle = core(middle)
-    sib0 = core(after(m0, sib_middle))
-    sib1 = core(after(m1, sib0))
-    sib2 = core(after(m2, sib1))
-    y0 = over(after(x0, sib2))
-    x2 = across(after(m2, x0))
-    up2 = lax.ppermute(after(up1, x0), "fsdp", up(1))
-    dn2 = lax.ppermute(after(dn1, x0), "fsdp", down(1))
-    y1 = over(after(x1, up1, dn1))
-    fx0 = core(after(x0, x1, y0))
-    fy0 = core(after(y0, fx0))
-    sib3 = core(after(e0, fy0))
-    sib4 = core(after(e1, sib3))
-    x3 = across(after(e0, sib4))
-    y2 = over(after(x2, sib4))
-    fx1 = core(after(x1, x2))
-    fy1 = core(after(y1, fx1))
-    fx2 = core(after(x2, fy1))
-    up3 = lax.ppermute(after(up2, x2), "fsdp", up(2))
-    dn3 = lax.ppermute(after(dn2, x2), "fsdp", down(2))
-    x4 = across(after(e1, fx2))
-    fx3 = core(after(x3, up2, dn2))
-    fy2 = core(after(y2, fx3))
-    fx4 = core(x4)
-    mine = [(m0, 0), (m1, 0), (m2, 0), (middle, 0), (middle, 1), (middle, 2), (e0, 0), (e1, 0)]
-    sibling = [(sib0, 0), (sib1, 0), (sib2, 0), (sib_middle, 0), (sib_middle, 1), (sib_middle, 2)]
-    sibling += [(sib3, 0), (sib4, 0)]
-    far = [(v, 0) for v in (x0, x1, x2, y0, y1, y2, x3, x4)]
-    far_sibling = [(v, 0) for v in (fx0, fx1, fx2, fy0, fy1, fy2, fx3, fx4)]
-    places = []
-    for i in range(tiles):
-        places += [mine[i], sibling[i], far[i], far_sibling[i]]
-    arrays = []
-    for array, _ in places:
-        if not any(array is other for other in arrays):
-            arrays.append(array)
-    where = [
-        ([array is other for other in arrays].index(True), offset) for array, offset in places
-    ]
-    near = [own, up1, dn1, up2, dn2, up3, dn3]
-    return near, arrays, where, tiles, (up1, dn1)
+    head = weight_tiles(group, codes, columns, 0, 1, half)
+    tail = weight_tiles(after(group, head), codes, columns, 1, tiles - 1, half)
+    x0 = across(head)
+    x1 = across(tail[0:1])
+    sib_tail = core(tail)
+    sib_head = core(after(head, sib_tail))
+    y0 = over(x0)
+    x2 = across(after(tail[1:2], sib_tail))
+
+    def rest(row, done):
+        up2 = lax.ppermute(after(up1, row), "fsdp", up(1))
+        dn2 = lax.ppermute(after(dn1, row), "fsdp", down(1))
+        y1 = over(after(x1, up1, dn1))
+        x3 = across(after(tail[5:7], y0))
+        y2 = over(after(x2, done))
+        up3 = lax.ppermute(after(up2, done), "fsdp", up(2))
+        dn3 = lax.ppermute(after(dn2, done), "fsdp", down(2))
+        far1 = gather_tiles(after((x0, x1, y0, x2, y1), up2, dn2, done, sib_head))
+        sib_far1 = core(far1)
+        sib_far2 = core(after(y2, sib_far1))
+        sib_far3 = core(after(x3, up3, dn3, sib_far2))
+        arrays = [head, tail, sib_head, sib_tail, far1, y2, x3, sib_far1, sib_far2, sib_far3]
+        far_places = [(4, 0), (4, 1), (4, 3), (4, 2), (4, 4), (5, 0), (6, 0), (6, 1)]
+        where = []
+        for i in range(tiles):
+            mine = (0, 0) if i == 0 else (1, i - 1)
+            far = far_places[i]
+            where += [mine, (mine[0] + 2, mine[1]), far, (far[0] + 3, far[1])]
+        near = [own, up1, dn1, up2, dn2, up3, dn3]
+        return near, arrays, where
+
+    return rest, tiles, (up1, dn1), (y0,)
 
 
 def shards(
@@ -189,11 +294,10 @@
     rank_half = rank_double // 2
     joined_part = cotangent.shape[1]
     joined_part_w = base_codes.shape[1]
-    hidden = hidden_in[:LIVE]
     own = cotangent[:LIVE]
     lines = (n_groups, n_fsdp, n_dp) == (2, 4, 4) and width_part == 8 * TILE
     if lines:
-        near, arrays, where, tiles, first = permute_plan(own, base_codes, base_scales, y)
+        rest, tiles, first, second = permute_plan(own, base_codes, base_scales, y)
 
     task = task_ids[0]
     chosen_a = lax.dynamic_slice_in_dim(factor_a, task, 1, 0).reshape(width_part, rank_double)
@@ -206,19 +310,31 @@
         [jnp.where(value_column, empty_b, chosen_b), jnp.where(value_column, chosen_b, empty_b)],
         axis=1,
     )
-    inner_part = jnp.dot(hidden, chosen_a, preferred_element_type=f32)
-    outer_part = jnp.dot(own, joined_b, preferred_element_type=f32)
-    parts = jnp.concatenate([inner_part, outer_part], axis=1).astype(bf16)
+    parts = whole_call(
+        product_kernel,
+        jax.ShapeDtypeStruct((LIVE, 2 * rank_double), bf16),
+        hidden_in,
+        cotangent,
+        chosen_a,
+        joined_b,
+    )
     sums = jnp.sum(lax.all_gather(parts, "fsdp", axis=0).astype(f32), axis=0)
     keep = lax.broadcasted_iota(jnp.int32, (LIVE, 1), 0) < valid_counts[0]
     sums = jnp.where(keep, sums, 0.0).astype(bf16)
     low_in, low_grad = sums[:, :rank_double], sums[:, rank_double:]
 
-    down_gradient = adapter_scale * lax.dot_general(
-        hidden, low_grad, (((0,), (0,)), ((), ())), preferred_element_type=f32
-    )
-    mixed = lax.dot_general(own, low_in, (((0,), (0,)), ((), ())), preferred_element_type=f32)
-    up_gradient = adapter_scale * jnp.where(value_column, mixed[:, rank_half:], mixed[:, :rank_half])
+    down_gradient, mixed = whole_call(
+        factor_kernel,
+        [
+            jax.ShapeDtypeStruct((width_part, rank_double), f32),
+            jax.ShapeDtypeStruct((joined_part, rank_double), f32),
+        ],
+        hidden_in,
+        cotangent,
+        low_grad,
+        low_in,
+    )
+    up_gradient = jnp.where(value_column, mixed[:, rank_half:], mixed[:, :rank_half])
     down_cols = width_part * rank_double
     up_cols = joined_part * rank_half
     row = jnp.concatenate(
@@ -230,21 +346,18 @@
         axis=1,
     )
     if lines:
+        packed = row
         row = after(row, *first)
     rows = lax.all_gather(row, "dp", axis=0, tiled=True)
+    if lines:
+        rows = after(rows, *second)
     ids = rows[:, down_cols + up_cols].astype(jnp.int32)
-    rows_down, rows_up = rows[:, :down_cols], rows[:, down_cols : down_cols + up_cols]
     one_hot = ids[:, None] == lax.broadcasted_iota(jnp.int32, (1, tasks_all), 1)
     states = jnp.dot(one_hot.astype(bf16), task_state, preferred_element_type=f32).astype(bf16)
-    grad_head_a = lax.dot_general(
-        states, rows_down, (((0,), (0,)), ((), ())), preferred_element_type=f32
-    )
-    grad_head_b = lax.dot_general(
-        states, rows_up, (((0,), (0,)), ((), ())), preferred_element_type=f32
-    )
-    state_part = lax.dot_general(
-        rows_down, head_a, (((1,), (1,)), ((), ())), preferred_element_type=f32
-    ) + lax.dot_general(rows_up, head_b, (((1,), (1,)), ((), ())), preferred_element_type=f32)
+    block = math.gcd(down_cols, up_cols)
+    grad_head_a, part_a = head_grads(states, rows, head_a, 0, block)
+    grad_head_b, part_b = head_grads(states, rows, head_b, down_cols, block)
+    state_part = part_a + part_b
     state_sum = jnp.sum(lax.all_gather(state_part, "fsdp", axis=0), axis=0)
     task_rows = lax.broadcasted_iota(jnp.int32, (tasks_all, tasks_all), 0)
     task_other = lax.broadcasted_iota(jnp.int32, (tasks_all, tasks_all), 1)
@@ -257,6 +370,7 @@
     grad_state = jnp.sum(selector[:, :, None] * state_sum[None, :, :], axis=1)
 
     if lines:
+        near, arrays, where = rest(packed, (grad_head_a, grad_head_b, grad_state))
         meta = jnp.stack([z, p, y, valid_counts[0]]).astype(jnp.int32)
         any_spec = pl.BlockSpec(memory_space=pl.ANY)
         vmem_spec = pl.BlockSpec(memory_space=pltpu.VMEM)
@@ -269,7 +383,7 @@
             out_specs=vmem_spec,
             scratch_shapes=[
                 pltpu.VMEM((4, LIVE, joined_part), bf16),
-                pltpu.VMEM((depth, TILE, joined_part_w), bf16),
+                pltpu.VMEM((depth, joined_part_w, TILE), bf16),
                 pltpu.SemaphoreType.DMA((4,)),
                 pltpu.SemaphoreType.DMA((depth,)),
             ],

time: 306 us -> 449 us (1.47)
  Pallas kernels: 41.3 us -> 249 us
  matrix products: 43.9 us -> 0.19 us
  waiting for transfers between devices: 121 us -> 78.2 us
  local copies, waits for them, and re-layouts: 11 us -> 34.2 us
  other arithmetic: 1.83 us -> 8 us
  starting transfers between devices: 26.6 us -> 20.7 us
    pallas_call x0 -> x7, Pallas kernels: none -> 208 us  [the longest x1 180 us: gather_tiles(): pl.pallas_call(gather_kernel, out_shape=jax.ShapeDtypeStruct((len(tiles),...]
    dot_general x14 -> x0, matrix products: 43.7 us -> none  [the longest x6 18.3 us: dequantize(): wide = jnp.dot(scales, spread, preferred_element_type=jnp.float32)]
    ppermute x3, waiting for transfers between devices: 8.75 us -> 48.3 us  [permute_plan(): over = lambda v: lax.ppermute(v, 'groups', [(0, 1), (1, 0)])]
    ppermute x4, waiting for transfers between devices: 29.6 us -> 0.01 us  [the longest x1 0.01 us: rest(): up2 = lax.ppermute(after(up1, row), 'fsdp', up(1))]
    ppermute x1, waiting for transfers between devices: 28 us -> 0.01 us  [permute_plan(): up1 = lax.ppermute(own, 'fsdp', up(0))]
    ppermute x5 -> x4, waiting for transfers between devices: 45.3 us -> 25.1 us  [permute_plan(): across = lambda v: lax.ppermute(v, 'dp', [(i, i ^ 2) for i in range(4)])]
    unnamed x37 -> x47, local copies, waits for them, and re-layouts: 5.01 us -> 21.7 us
    all_gather x1, blocking collectives: 31.7 us -> 22.9 us  [shards(): rows = lax.all_gather(row, 'dp', axis=0, tiled=True)]
  transfers between devices with their start and end apart: 28 -> 18, of which waited for: 9 -> 4; matrix products, arithmetic and copies ran while one was open for 15% -> 4% of each run, Pallas kernels for 0% -> 6%
where the time goes in v2:
time: 449 us
  Pallas kernels  249 us (55%)
  waiting for transfers between devices  78.2 us (17%)
  blocking collectives  55.8 us (12%)
  local copies, waits for them, and re-layouts  34.2 us (8%)
  starting transfers between devices  20.7 us (5%)
  other arithmetic  8 us (2%)
    pallas_call x1, Pallas kernels, gather_tiles(): pl.pallas_call(gather_kernel, out_shape=jax.ShapeDtypeStruct((len(tiles),...  180 us
    ppermute x3, waiting for transfers between devices, permute_plan(): over = lambda v: lax.ppermute(v, 'groups', [(0, 1), (1, 0)])  48.3 us
    pallas_call x1, Pallas kernels, shards(): pl.pallas_call(lambda *refs: input_gradient_kernel(tiles, where, len(arra...  41.5 us
    ppermute x4, waiting for transfers between devices, permute_plan(): across = lambda v: lax.ppermute(v, 'dp', [(i, i ^ 2) for i in range(4)])  25.1 us
    all_gather x1, blocking collectives, shards(): rows = lax.all_gather(row, 'dp', axis=0, tiled=True)  22.9 us
    unnamed x47, local copies, waits for them, and re-layouts  21.7 us
    all_gather x1, blocking collectives, shards(): sums = jnp.sum(lax.all_gather(parts, 'fsdp', axis=0).astype(f32), axis=0)  21 us
    pallas_call x2, Pallas kernels, head_grads(): pl.pallas_call(head_kernel, out_shape=[jax.ShapeDtypeStruct((hidden_units...  18 us
  transfers between devices with their start and end apart: 18, of which 4 were waited for; matrix products, arithmetic and copies ran while one was open for 4% of the time, Pallas kernels for 6%

profile of v2, /device:TPU:0, one launch (start us, length us, event | category | flops | bytes accessed | tf_op | source)
XLA Modules:
  0.0 448.7 jit_solution(17495329170089743719)
XLA Ops:
  0.7 2.9 slice.28.refs_3_
  3.6 1.3 collective-permute-start.1
  4.9 6.7 %collective-permute-start = (bf16[384,2304]{1,0:T(8,128)(2,1)}, bf16[384,2304]{1,0:T(8,128)(2,1)}, u32[]{:S(2)}, u32[]{:S(2)}) collective-permute-start(bf16[384,2304]{1,0:T(8,128)(2,1)} %slice.28.refs_3_), channel_id=1, source_target_pairs={{0,4},{4,8},{8,12},{1,5},{5,9},{9,13},{2,6},{6,10},{10,14},{3,7},{... | collective-permute-start | bytes 5308424 | tf_op jit(solution)/shard_map/ppermute | solution.py:238
  11.6 3.7 copy-done.2
  15.3 1.5 shard_map.149.refs_10_
  16.8 1.9 collective-permute-start.4
  18.7 6.2 %shard_map.152.refs_11_ = bf16[7,2304,256]{2,1,0:T(8,128)(2,1)} custom-call(s32[1]{0:T(128)} %bitcast.2.group, bf16[2048,2304]{1,0:T(8,128)(2,1)S(1)} %copy-done.2, bf16[36,2048]{1,0:T(8,128)(2,1)S(1)} %bitcast.24), custom_call_target="tpu_custom_call" | custom-call | tf_op jit(solution)/shard_map/pallas_call | solution.py:52
  24.9 3.2 fusion.6
  30.1 1.5 reshape.82
  31.6 3.1 broadcast_select_fusion.1
  36.1 1.8 pad_maximum_fusion.joined
  37.9 1.6 copy-done.5
  40.6 21.0 %all-gather = bf16[1536,32]{1,0:T(8,128)(2,1)S(1)} all-gather(bf16[384,32]{1,0:T(8,128)(2,1)S(1)} %shard_map.147), channel_id=2, replica_groups=mesh['groups'=2,'fsdp'=4,'dp'=4] {'fsdp'}, dimensions={0}, use_global_device_ids=true | all-gather | bytes 122880 | tf_op jit(solution)/shard_map/all_gather | solution.py:321
  67.2 1.6 collective-permute-start.5
  69.9 1.3 collective-permute-start.3
  72.0 24.5 %collective-permute-done.5.refs_2_ = bf16[1,2304,256]{2,1,0:T(8,128)(2,1)} collective-permute-done((bf16[1,2304,256]{2,1,0:T(8,128)(2,1)}, bf16[1,2304,256]{2,1,0:T(8,128)(2,1)}, u32[]{:S(2)}, u32[]{:S(2)}) %collective-permute-start.5) | collective-permute-done | bytes 1179680 | tf_op jit(solution)/shard_map/ppermute | solution.py:234
  96.5 1.5 collective-permute-start.11
  98.0 22.9 %all-gather.2 = bf16[4,1,51328]{2,1,0:T(2,128)(2,1)S(1)} all-gather(bf16[1,1,51328]{2,1,0:T(2,128)(2,1)S(1)} %bitcast.26), channel_id=1, replica_groups=mesh['groups'=2,'fsdp'=4,'dp'=4] {'dp'}, dimensions={0}, use_global_device_ids=true | all-gather | bytes 513280 | tf_op jit(solution)/shard_map/all_gather | solution.py:351
  121.5 2.3 copy-done.8
  123.8 6.7 %shard_map.151 = (f32[128,18432]{1,0:T(8,128)}, f32[4,128]{1,0:T(4,128)S(1)}) custom-call(bf16[4,128]{1,0:T(4,128)(2,1)S(1)} %convolution_convert_fusion.states, bf16[4,51328]{1,0:T(4,128)(2,1)S(1)} %bitcast.21, bf16[128,18432]{1,0:T(8,128)(2,1)S(1)} %copy-done.8), custom_call_target="tpu_custom_call" | custom-call | tf_op jit(solution)/shard_map/pallas_call | solution.py:102
  130.5 3.4 copy-done.4
  133.8 11.3 %shard_map.150 = (f32[128,32768]{1,0:T(8,128)}, f32[4,128]{1,0:T(4,128)S(1)}) custom-call(bf16[4,128]{1,0:T(4,128)(2,1)S(1)} %convolution_convert_fusion.states, bf16[4,51328]{1,0:T(4,128)(2,1)S(1)} %bitcast.22, bf16[128,32768]{1,0:T(8,128)(2,1)S(1)} %copy-done.4), custom_call_target="tpu_custom_call" | custom-call | tf_op jit(solution)/shard_map/pallas_call | solution.py:102
  145.1 11.9 %all-gather.3 = f32[4,4,128]{2,1,0:T(4,128)S(1)} all-gather(f32[1,4,128]{2,1,0:T(4,128)S(1)} %add_bitcast_fusion), channel_id=3, replica_groups=mesh['groups'=2,'fsdp'=4,'dp'=4] {'fsdp'}, dimensions={0}, use_global_device_ids=true | all-gather | bytes 10240 | tf_op jit(solution)/shard_map/all_gather | solution.py:361
  159.0 179.8 %shard_map.153.refs_14_ = bf16[5,2304,256]{2,1,0:T(8,128)(2,1)} custom-call(bf16[1,2304,256]{2,1,0:T(8,128)(2,1)} %collective-permute-done.4.refs_0_, bf16[1,2304,256]{2,1,0:T(8,128)(2,1)} %collective-permute-done.10.refs_1_, bf16[1,2304,256]{2,1,0:T(8,128)(2,1)} %collective-permute-done.5.refs_2_, bf16[1,2304,256]{2,1,0:T(8,128)(2,1)} %collective-permute-done.11.refs_3_, ...), custom_call_target="tpu_custom_call" | custom-call | tf_op jit(solution)/shard_map/pallas_call | solution.py:217
  338.9 1.9 slice.40
  340.8 1.3 collective-permute-start.13
  342.1 1.5 collective-permute-start.14
  344.4 1.3 collective-permute-start.7
  345.7 23.7 %collective-permute-done.13.refs_15_ = bf16[1,2304,256]{2,1,0:T(8,128)(2,1)S(1)} collective-permute-done((bf16[1,2304,256]{2,1,0:T(8,128)(2,1)}, bf16[1,2304,256]{2,1,0:T(8,128)(2,1)S(1)}, u32[]{:S(2)}, u32[]{:S(2)}) %collective-permute-start.13) | collective-permute-done | bytes 1179680 | tf_op jit(solution)/shard_map/ppermute | solution.py:234
  370.4 25.1 %collective-permute-done.14.refs_16_ = bf16[2,2304,256]{2,1,0:T(8,128)(2,1)} collective-permute-done((bf16[2,2304,256]{2,1,0:T(8,128)(2,1)S(1)}, bf16[2,2304,256]{2,1,0:T(8,128)(2,1)}, u32[]{:S(2)}, u32[]{:S(2)}) %collective-permute-start.14) | collective-permute-done | bytes 2359328 | tf_op jit(solution)/shard_map/ppermute | solution.py:232
  398.4 4.8 %collective-permute-done.17.refs_19_ = bf16[2,2304,256]{2,1,0:T(8,128)(2,1)} collective-permute-done((bf16[2,2304,256]{2,1,0:T(8,128)(2,1)}, bf16[2,2304,256]{2,1,0:T(8,128)(2,1)}, u32[]{:S(2)}, u32[]{:S(2)}) %collective-permute-start.17) | collective-permute-done | bytes 2359328 | tf_op jit(solution)/shard_map/ppermute | solution.py:233
  407.1 41.5 %shard_map.154 = bf16[512,2048]{1,0:T(8,128)(2,1)} custom-call(s32[4]{0:T(128)S(1)} %pad_add_fusion.refs_0_, bf16[384,16]{1,0:T(8,128)(2,1)S(1)} %get-tuple-element.59.grad.refs_1_, bf16[2048,16]{1,0:T(8,128)(2,1)S(1)} %copy-done.7, bf16[384,2304]{1,0:T(8,128)(2,1)} %slice.28.refs_3_, bf16[384,2304]{1,0:T(8,128)(2,1)} %collective-permute-done.refs_4_, ...), custom_call_target="tpu_custom_call" | custom-call | tf_op jit(solution)/shard_map/pallas_call | solution.py:378
  (94 shorter events, 21.6 us)
Async XLA Ops:
  0.6 34.7 %copy-start = (bf16[16,32768]{1,0:T(8,128)(2,1)S(1)}, bf16[16,32768]{1,0:T(8,128)(2,1)}, u32[]{:S(2)}) copy-start(bf16[16,32768]{1,0:T(8,128)(2,1)} %param.16) | copy-start | bytes 3145732
  0.6 11.0 %copy-start.17 = (bf16[2048,36]{0,1:T(8,128)(2,1)S(1)}, bf16[2048,36]{0,1:T(8,128)(2,1)}, u32[]{:S(2)}) copy-start(bf16[2048,36]{0,1:T(8,128)(2,1)} %param.15) | copy-start | bytes 442372
  3.6 65.5 %collective-permute-start.1 = (bf16[384,2304]{1,0:T(8,128)(2,1)}, bf16[384,2304]{1,0:T(8,128)(2,1)}, u32[]{:S(2)}, u32[]{:S(2)}) collective-permute-start(bf16[384,2304]{1,0:T(8,128)(2,1)} %slice.28.refs_3_), channel_id=1, source_target_pairs={{4,0},{8,4},{12,8},{5,1},{9,5},{13,9},{6,2},{10,6},{14,10},{7,3},{... | collective-permute-start | bytes 5308424 | tf_op jit(solution)/shard_map/ppermute | solution.py:239
  4.9 64.2 %collective-permute-start = (bf16[384,2304]{1,0:T(8,128)(2,1)}, bf16[384,2304]{1,0:T(8,128)(2,1)}, u32[]{:S(2)}, u32[]{:S(2)}) collective-permute-start(bf16[384,2304]{1,0:T(8,128)(2,1)} %slice.28.refs_3_), channel_id=1, source_target_pairs={{0,4},{4,8},{8,12},{1,5},{5,9},{9,13},{2,6},{6,10},{10,14},{3,7},{... | collective-permute-start | bytes 5308424 | tf_op jit(solution)/shard_map/ppermute | solution.py:238
  11.6 3.7 copy-start.2
  16.8 50.4 %collective-permute-start.4 = (bf16[1,2304,256]{2,1,0:T(8,128)(2,1)}, bf16[1,2304,256]{2,1,0:T(8,128)(2,1)}, u32[]{:S(2)}, u32[]{:S(2)}) collective-permute-start(bf16[1,2304,256]{2,1,0:T(8,128)(2,1)} %shard_map.149.refs_10_), channel_id=1, source_target_pairs={{0,2},{1,3},{2,0},{3,1},{4,6},{5,7},{6,4},{7,5},{8,10},{9,11},{10,... | collective-permute-start | bytes 3538952 | tf_op jit(solution)/shard_map/ppermute | solution.py:232
  24.9 47.0 %collective-permute-start.8 = (bf16[7,2304,256]{2,1,0:T(8,128)(2,1)}, bf16[7,2304,256]{2,1,0:T(8,128)(2,1)}, u32[]{:S(2)}, u32[]{:S(2)}) collective-permute-start(bf16[7,2304,256]{2,1,0:T(8,128)(2,1)} %shard_map.152.refs_11_), channel_id=1, source_target_pairs={{0,1},{1,0},{2,3},{3,2},{4,5},{5,4},{6,7},{7,6},{8,9},{9,8},{10,11... | collective-permute-start | bytes 24772616 | tf_op jit(solution)/shard_map/ppermute | solution.py:233
  28.1 43.3 %collective-permute-start.10 = (bf16[1,2304,256]{2,1,0:T(8,128)(2,1)}, bf16[1,2304,256]{2,1,0:T(8,128)(2,1)}, u32[]{:S(2)}, u32[]{:S(2)}) collective-permute-start(bf16[1,2304,256]{2,1,0:T(8,128)(2,1)} %get-tuple-element.55), channel_id=1, source_target_pairs={{0,2},{1,3},{2,0},{3,1},{4,6},{5,7},{6,4},{7,5},{8,10},{9,11},{10,... | collective-permute-start | bytes 3538952 | tf_op jit(solution)/shard_map/ppermute | solution.py:232
  31.6 6.4 %copy-start.3 = (bf16[512,2304]{1,0:T(8,128)(2,1)S(1)}, bf16[512,2304]{1,0:T(8,128)(2,1)}, u32[]{:S(2)}) copy-start(bf16[512,2304]{1,0:T(8,128)(2,1)} %cotangent.3) | copy-start | bytes 7077892
  36.1 4.5 %copy-start.6 = (bf16[2048,16]{1,0:T(8,128)(2,1)}, bf16[2048,16]{1,0:T(8,128)(2,1)S(1)}, u32[]{:S(2)}) copy-start(bf16[2048,16]{1,0:T(8,128)(2,1)S(1)} %reshape.81.chosen.refs_2_) | copy-start | bytes 196612
  37.9 1.6 copy-start.5
  64.1 7.0 %copy-start.22 = (s32[16]{0:T(128)S(1)}, s32[16]{0:T(128)}, u32[]{:S(2)}) copy-start(s32[16]{0:T(128)} %param.23) | copy-start | bytes 196
  66.6 54.7 %copy-start.21 = (bf16[16,128]{1,0:T(8,128)(2,1)S(1)}, bf16[16,128]{1,0:T(8,128)(2,1)}, u32[]{:S(2)}) copy-start(bf16[16,128]{1,0:T(8,128)(2,1)} %param.18) | copy-start | bytes 12292
  67.2 29.3 %collective-permute-start.5 = (bf16[1,2304,256]{2,1,0:T(8,128)(2,1)}, bf16[1,2304,256]{2,1,0:T(8,128)(2,1)}, u32[]{:S(2)}, u32[]{:S(2)}) collective-permute-start(bf16[1,2304,256]{2,1,0:T(8,128)(2,1)} %collective-permute-done.4.refs_0_), channel_id=1, source_target_pairs={{0,16},{16,0},{1,17},{17,1},{2,18},{18,2},{3,19},{19,3},{4,20},{20... | collective-permute-start | bytes 3538952 | tf_op jit(solution)/shard_map/ppermute | solution.py:234
  69.1 88.9 %collective-permute-start.2 = (bf16[384,2304]{1,0:T(8,128)(2,1)}, bf16[384,2304]{1,0:T(8,128)(2,1)S(1)}, u32[]{:S(2)}, u32[]{:S(2)}) collective-permute-start(bf16[384,2304]{1,0:T(8,128)(2,1)} %collective-permute-done.refs_4_), channel_id=1, source_target_pairs={{4,8},{8,12},{5,9},{9,13},{6,10},{10,14},{7,11},{11,15},{20,24},{2... | collective-permute-start | bytes 5308424 | tf_op jit(solution)/shard_map/ppermute | solution.py:250
  69.9 88.1 %collective-permute-start.3 = (bf16[384,2304]{1,0:T(8,128)(2,1)}, bf16[384,2304]{1,0:T(8,128)(2,1)}, u32[]{:S(2)}, u32[]{:S(2)}) collective-permute-start(bf16[384,2304]{1,0:T(8,128)(2,1)} %collective-permute-done.1.refs_5_), channel_id=1, source_target_pairs={{4,0},{8,4},{5,1},{9,5},{6,2},{10,6},{7,3},{11,7},{20,16},{24,20},... | collective-permute-start | bytes 5308424 | tf_op jit(solution)/shard_map/ppermute | solution.py:251
  71.4 86.6 %collective-permute-start.12 = (bf16[1,2304,256]{2,1,0:T(8,128)(2,1)}, bf16[1,2304,256]{2,1,0:T(8,128)(2,1)}, u32[]{:S(2)}, u32[]{:S(2)}) collective-permute-start(bf16[1,2304,256]{2,1,0:T(8,128)(2,1)} %collective-permute-done.10.refs_1_), channel_id=1, source_target_pairs={{0,16},{16,0},{1,17},{17,1},{2,18},{18,2},{3,19},{19,3},{4,20},{20... | collective-permute-start | bytes 3538952 | tf_op jit(solution)/shard_map/ppermute | solution.py:234
  72.0 86.0 %collective-permute-start.9 = (bf16[1,2304,256]{2,1,0:T(8,128)(2,1)}, bf16[1,2304,256]{2,1,0:T(8,128)(2,1)S(1)}, u32[]{:S(2)}, u32[]{:S(2)}) collective-permute-start(bf16[1,2304,256]{2,1,0:T(8,128)(2,1)} %shard_map.149.refs_10_), channel_id=1, source_target_pairs={{0,1},{1,0},{2,3},{3,2},{4,5},{5,4},{6,7},{7,6},{8,9},{9,8},{10,11... | collective-permute-start | bytes 3538952 | tf_op jit(solution)/shard_map/ppermute | solution.py:233
  96.5 62.5 %collective-permute-start.11 = (bf16[1,2304,256]{2,1,0:T(8,128)(2,1)}, bf16[1,2304,256]{2,1,0:T(8,128)(2,1)}, u32[]{:S(2)}, u32[]{:S(2)}) collective-permute-start(bf16[1,2304,256]{2,1,0:T(8,128)(2,1)} %get-tuple-element.43), channel_id=1, source_target_pairs={{0,2},{1,3},{2,0},{3,1},{4,6},{5,7},{6,4},{7,5},{8,10},{9,11},{10,... | collective-permute-start | bytes 3538952 | tf_op jit(solution)/shard_map/ppermute | solution.py:232
  121.4 2.3 copy-start.8
  130.5 3.4 copy-start.4
  338.8 64.4 %copy-start.7 = (bf16[2048,16]{1,0:T(8,128)(2,1)S(1)}, bf16[2048,16]{1,0:T(8,128)(2,1)}, u32[]{:S(2)}) copy-start(bf16[2048,16]{1,0:T(8,128)(2,1)} %copy-done.6) | copy-start | bytes 196612
  338.8 30.5 %collective-permute-start.15 = (bf16[5,2304,256]{2,1,0:T(8,128)(2,1)}, bf16[5,2304,256]{2,1,0:T(8,128)(2,1)S(1)}, u32[]{:S(2)}, u32[]{:S(2)}) collective-permute-start(bf16[5,2304,256]{2,1,0:T(8,128)(2,1)} %shard_map.153.refs_14_), channel_id=1, source_target_pairs={{0,1},{1,0},{2,3},{3,2},{4,5},{5,4},{6,7},{7,6},{8,9},{9,8},{10,11... | collective-permute-start | bytes 17694728 | tf_op jit(solution)/shard_map/ppermute | solution.py:233
  340.8 28.6 %collective-permute-start.13 = (bf16[1,2304,256]{2,1,0:T(8,128)(2,1)}, bf16[1,2304,256]{2,1,0:T(8,128)(2,1)S(1)}, u32[]{:S(2)}, u32[]{:S(2)}) collective-permute-start(bf16[1,2304,256]{2,1,0:T(8,128)(2,1)} %collective-permute-done.11.refs_3_), channel_id=1, source_target_pairs={{0,16},{16,0},{1,17},{17,1},{2,18},{18,2},{3,19},{19,3},{4,20},{20... | collective-permute-start | bytes 3538952 | tf_op jit(solution)/shard_map/ppermute | solution.py:234
  342.1 53.4 %collective-permute-start.14 = (bf16[2,2304,256]{2,1,0:T(8,128)(2,1)S(1)}, bf16[2,2304,256]{2,1,0:T(8,128)(2,1)}, u32[]{:S(2)}, u32[]{:S(2)}) collective-permute-start(bf16[2,2304,256]{2,1,0:T(8,128)(2,1)S(1)} %slice.40), channel_id=1, source_target_pairs={{0,2},{1,3},{2,0},{3,1},{4,6},{5,7},{6,4},{7,5},{8,10},{9,11},{10,... | collective-permute-start | bytes 7077896 | tf_op jit(solution)/shard_map/ppermute | solution.py:232
  343.6 51.9 %collective-permute-start.6 = (bf16[384,2304]{1,0:T(8,128)(2,1)S(1)}, bf16[384,2304]{1,0:T(8,128)(2,1)S(1)}, u32[]{:S(2)}, u32[]{:S(2)}) collective-permute-start(bf16[384,2304]{1,0:T(8,128)(2,1)S(1)} %collective-permute-done.2.refs_6_), channel_id=1, source_target_pairs={{8,12},{9,13},{10,14},{11,15},{24,28},{25,29},{26,30},{27,31}} | collective-permute-start | bytes 5308424 | tf_op jit(solution)/shard_map/ppermute | solution.py:255
  344.4 51.2 %collective-permute-start.7 = (bf16[384,2304]{1,0:T(8,128)(2,1)}, bf16[384,2304]{1,0:T(8,128)(2,1)S(1)}, u32[]{:S(2)}, u32[]{:S(2)}) collective-permute-start(bf16[384,2304]{1,0:T(8,128)(2,1)} %collective-permute-done.3.refs_7_), channel_id=1, source_target_pairs={{4,0},{5,1},{6,2},{7,3},{20,16},{21,17},{22,18},{23,19}} | collective-permute-start | bytes 5308424 | tf_op jit(solution)/shard_map/ppermute | solution.py:256
  369.4 26.2 %copy-start.18 = (bf16[5,2304,256]{2,1,0:T(8,128)(2,1)}, bf16[5,2304,256]{2,1,0:T(8,128)(2,1)S(1)}, u32[]{:S(2)}) copy-start(bf16[5,2304,256]{2,1,0:T(8,128)(2,1)S(1)} %collective-permute-done.15.refs_17_) | copy-start | bytes 17694724
  369.4 26.2 %collective-permute-start.16 = (bf16[1,2304,256]{2,1,0:T(8,128)(2,1)S(1)}, bf16[1,2304,256]{2,1,0:T(8,128)(2,1)S(1)}, u32[]{:S(2)}, u32[]{:S(2)}) collective-permute-start(bf16[1,2304,256]{2,1,0:T(8,128)(2,1)S(1)} %collective-permute-done.13.refs_15_), channel_id=1, source_target_pairs={{0,1},{1,0},{2,3},{3,2},{4,5},{5,4},{6,7},{7,6},{8,9},{9,8},{10,11... | collective-permute-start | bytes 3538952 | tf_op jit(solution)/shard_map/ppermute | solution.py:233
  395.5 1.8 copy-start.20
  398.4 4.9 %collective-permute-start.17 = (bf16[2,2304,256]{2,1,0:T(8,128)(2,1)}, bf16[2,2304,256]{2,1,0:T(8,128)(2,1)}, u32[]{:S(2)}, u32[]{:S(2)}) collective-permute-start(bf16[2,2304,256]{2,1,0:T(8,128)(2,1)} %collective-permute-done.14.refs_16_), channel_id=1, source_target_pairs={{0,1},{1,0},{2,3},{3,2},{4,5},{5,4},{6,7},{7,6},{8,9},{9,8},{10,11... | collective-permute-start | bytes 7077896 | tf_op jit(solution)/shard_map/ppermute | solution.py:233
  407.0 41.5 %copy-start.1 = (bf16[16,32768]{1,0:T(8,128)(2,1)S(1)}, bf16[16,32768]{1,0:T(8,128)(2,1)}, u32[]{:S(2)}) copy-start(bf16[16,32768]{1,0:T(8,128)(2,1)} %param.16) | copy-start | bytes 3145732
  (9 other events, 10.4 us)

commit v3 on v2

v3 whole, which is shorter than its diff:
```python
import math

import jax
import jax.numpy as jnp
from jax import lax
from jax.experimental import pallas as pl
from jax.experimental.pallas import tpu as pltpu
from jax.sharding import PartitionSpec as P

HEADS = 64
KV_HEADS = 8
HEAD_DIM = 128
QBLOCK = 64
SLOTS = 4
LIVE = 384
TILE = 256

adapter_scale = 2.0


def dequantize(codes, scales):
    rows, cols = codes.shape
    blocks = scales.shape[1]
    return (
        (
            codes.astype(jnp.float32).reshape(rows, blocks, QBLOCK)
            * scales.astype(jnp.float32)[:, :, None]
        )
        .reshape(rows, cols)
        .astype(jnp.bfloat16)
    )


def weight_kernel(group, codes, scales, out):
    cols, blocks = codes.shape[1], scales.shape[0]
    spread = (
        lax.broadcasted_iota(jnp.int32, (blocks, cols), 1) // QBLOCK
        == lax.broadcasted_iota(jnp.int32, (blocks, cols), 0)
    ).astype(jnp.bfloat16)
    wide = lax.dot_general(
        scales[...], spread, (((0,), (0,)), ((), ())), preferred_element_type=jnp.float32
    )
    out[0] = (codes[...].astype(jnp.float32) * wide).astype(jnp.bfloat16)


def weight_tiles(group, codes, scales, first, count, half):
    cols, blocks = codes.shape[1], scales.shape[0]

    def place(i, group):
        at = first + i
        moved = jnp.where(at < half, at + group[0] * half, at - group[0] * half)
        return jnp.where(at < 2 * half, moved, at)

    return pl.pallas_call(
        weight_kernel,
        out_shape=jax.ShapeDtypeStruct((count, TILE, cols), jnp.bfloat16),
        grid_spec=pltpu.PrefetchScalarGridSpec(
            num_scalar_prefetch=1,
            grid=(count,),
            in_specs=[
                pl.BlockSpec((TILE, cols), lambda i, group: (place(i, group), 0)),
                pl.BlockSpec((blocks, TILE), lambda i, group: (0, place(i, group))),
            ],
            out_specs=pl.BlockSpec((1, TILE, cols), lambda i, group: (i, 0, 0)),
        ),
        compiler_params=pltpu.CompilerParams(vmem_limit_bytes=32 * 2**20),
        cost_estimate=pl.CostEstimate(flops=0, transcendentals=0, bytes_accessed=0),
    )(group, codes, scales)


def value_columns(first, count):
    group_cols = (HEADS // KV_HEADS + 1) * HEAD_DIM
    column = first + lax.broadcasted_iota(jnp.int32, (count, 1), 0)
    return lax.rem(column, group_cols) >= HEADS // KV_HEADS * HEAD_DIM


def product_kernel(first, hidden, cotangent, chosen_a, chosen_b, out):
    value = value_columns(first[0], cotangent.shape[1])
    plain = chosen_b[...]
    empty = jnp.zeros_like(plain)
    joined = jnp.concatenate(
        [jnp.where(value, empty, plain), jnp.where(value, plain, empty)], axis=1
    )
    inner = jnp.dot(hidden[:LIVE, :], chosen_a[...], preferred_element_type=jnp.float32)
    outer = jnp.dot(cotangent[:LIVE, :], joined, preferred_element_type=jnp.float32)
    out[...] = jnp.concatenate([inner, outer], axis=1).astype(out.dtype)


def factor_kernel(first, hidden, cotangent, grad, low, down, up):
    contract = (((0,), (0,)), ((), ()))
    down[...] = adapter_scale * lax.dot_general(
        hidden[:LIVE, :], grad[...], contract, preferred_element_type=jnp.float32
    )
    mixed = lax.dot_general(
        cotangent[:LIVE, :], low[...], contract, preferred_element_type=jnp.float32
    )
    half = low.shape[1] // 2
    value = value_columns(first[0], cotangent.shape[1])
    up[...] = adapter_scale * jnp.where(value, mixed[:, half:], mixed[:, :half])


def head_kernel(states, rows, head, grad, part):
    grad[...] = lax.dot_general(
        states[...], rows[...], (((0,), (0,)), ((), ())), preferred_element_type=jnp.float32
    )

    @pl.when(pl.program_id(0) == 0)
    def _():
        part[...] = jnp.zeros_like(part)

    part[...] += lax.dot_general(
        rows[...], head[...], (((1,), (1,)), ((), ())), preferred_element_type=jnp.float32
    )


def head_grads(states, rows, head, first, block):
    hidden_units, cols = head.shape
    sequences = rows.shape[0]
    return pl.pallas_call(
        head_kernel,
        out_shape=[
            jax.ShapeDtypeStruct((hidden_units, cols), jnp.float32),
            jax.ShapeDtypeStruct((sequences, hidden_units), jnp.float32),
        ],
        grid=(cols // block,),
        in_specs=[
            pl.BlockSpec((sequences, hidden_units), lambda i: (0, 0)),
            pl.BlockSpec((sequences, block), lambda i: (0, first // block + i)),
            pl.BlockSpec((hidden_units, block), lambda i: (0, i)),
        ],
        out_specs=[
            pl.BlockSpec((hidden_units, block), lambda i: (0, i)),
            pl.BlockSpec((sequences, hidden_units), lambda i: (0, 0)),
        ],
        compiler_params=pltpu.CompilerParams(vmem_limit_bytes=32 * 2**20),
        cost_estimate=pl.CostEstimate(flops=0, transcendentals=0, bytes_accessed=0),
    )(states, rows, head)


def whole_call(kernel, out_shape, *operands, scalars=()):
    spec = pl.BlockSpec(memory_space=pltpu.VMEM)
    return pl.pallas_call(
        kernel,
        out_shape=out_shape,
        in_specs=[pl.BlockSpec(memory_space=pltpu.SMEM)] * len(scalars) + [spec] * len(operands),
        out_specs=jax.tree.map(lambda _: spec, out_shape),
        compiler_params=pltpu.CompilerParams(vmem_limit_bytes=32 * 2**20),
        cost_estimate=pl.CostEstimate(flops=0, transcendentals=0, bytes_accessed=0),
    )(*scalars, *operands)


def after(value, *done):
    return lax.optimization_barrier((value, done))[0]


def input_gradient_kernel(tiles, where, count, *refs):
    meta, low, chosen = refs[:3]
    near = refs[3:10]
    arrays = refs[10 : 10 + count]
    out, cot, wbuf, csem, wsem = refs[10 + count :]
    weights = [arrays[index].at[offset] for index, offset in where]
    z, p, y, valid = meta[0], meta[1], meta[2], meta[3]
    own, up1, dn1, up2, dn2, up3, dn3 = near
    depth, cols = wbuf.shape[0], own.shape[1]
    half = (tiles - 2) // 2

    def send(tile, slot):
        for j in range(4):
            pltpu.make_async_copy(
                weights[tile * 4 + j], wbuf.at[slot, :, pl.ds(j * cols, cols)], wsem.at[slot, j]
            ).start()

    def arrive(source, slot):
        j = jnp.bitwise_xor(jnp.bitwise_and(z - slot, 3), p)
        target = cot.at[:, pl.ds(pl.multiple_of(j * cols, 128), cols)]
        return pltpu.make_async_copy(source, target, csem.at[slot])

    def place(first, second, take_first, slot):
        pl.when(take_first)(lambda: arrive(first, slot).start())
        pl.when(jnp.logical_not(take_first))(lambda: arrive(second, slot).start())

    for slot in range(depth - 1):
        send(slot, slot)
    arrive(own, 0).start()
    place(up1, dn3, z >= 1, 1)
    place(up2, dn2, z >= 2, 2)
    place(up3, dn1, z >= 3, 3)
    keep = lax.broadcasted_iota(jnp.int32, (LIVE, 1), 0) < valid
    out[LIVE:, :] = jnp.zeros((out.shape[0] - LIVE, out.shape[1]), out.dtype)
    for slot in range(4):
        arrive(own, slot).wait()

    @pl.loop(0, tiles)
    def _(tile):
        slot = lax.rem(tile, depth)
        ahead = tile + depth - 1
        for index in range(depth - 1, tiles):
            pl.when(ahead == index)(lambda index=index: send(index, index % depth))
        for j in range(4):
            pltpu.make_async_copy(
                weights[0], wbuf.at[slot, :, pl.ds(j * cols, cols)], wsem.at[slot, j]
            ).wait()
        moved = jnp.where(tile < half, tile + y * half, tile - y * half)
        start = pl.multiple_of(jnp.where(tile < 2 * half, moved, tile) * TILE, TILE)
        rows = (((1,), (1,)), ((), ()))
        total = lax.dot_general(cot[...], wbuf[slot], rows, preferred_element_type=jnp.float32)
        adapter = adapter_scale * lax.dot_general(
            low[...], chosen[pl.ds(start, TILE), :], rows, preferred_element_type=jnp.float32
        )
        result = jnp.where(keep, total, 0.0) + adapter
        out[:LIVE, pl.ds(start, TILE)] = result.astype(out.dtype)


def input_gradient_call(meta, low_grad, chosen_a, near, arrays, where, tiles, seq_len):
    any_spec = pl.BlockSpec(memory_space=pl.ANY)
    vmem_spec = pl.BlockSpec(memory_space=pltpu.VMEM)
    depth = 3
    cols = near[0].shape[1]
    return pl.pallas_call(
        lambda *refs: input_gradient_kernel(tiles, where, len(arrays), *refs),
        out_shape=jax.ShapeDtypeStruct((seq_len, tiles * TILE), jnp.bfloat16),
        in_specs=[pl.BlockSpec(memory_space=pltpu.SMEM), vmem_spec, vmem_spec]
        + [any_spec] * (len(near) + len(arrays)),
        out_specs=vmem_spec,
        scratch_shapes=[
            pltpu.VMEM((LIVE, 4 * cols), jnp.bfloat16),
            pltpu.VMEM((depth, TILE, 4 * cols), jnp.bfloat16),
            pltpu.SemaphoreType.DMA((4,)),
            pltpu.SemaphoreType.DMA((depth, 4)),
        ],
        compiler_params=pltpu.CompilerParams(vmem_limit_bytes=40 * 2**20),
    )(meta, low_grad, chosen_a, *near, *arrays)


def gather_kernel(*refs):
    out = refs[-1]
    for i, ref in enumerate(refs[:-1]):
        out[i] = ref[0]


def gather_tiles(tiles):
    shape = jax.ShapeDtypeStruct((len(tiles),) + tiles[0].shape[1:], tiles[0].dtype)
    return whole_call(gather_kernel, shape, *tiles)


def across(value):
    return lax.ppermute(value, "dp", [(i, i ^ 2) for i in range(4)])


def core(value):
    return lax.ppermute(value, "dp", [(i, i ^ 1) for i in range(4)])


def over(value):
    return lax.ppermute(value, "groups", [(0, 1), (1, 0)])


def line(value, step):
    def send(value, sign, far):
        pairs = [(i, i + 1) for i in range(far, 3)]
        return lax.ppermute(value, "fsdp", pairs if sign > 0 else [(3 - a, 3 - b) for a, b in pairs])

    return lambda sign: send(value, sign, step)


def turns(value):
    return [lax.ppermute(value, "fsdp", [(i, (i + k) % 4) for i in range(4)]) for k in (1, 2, 3)]


class Plan:
    def __init__(self, own, codes, scales, y):
        self.own, self.codes, self.scales = own, codes, scales.T
        self.tiles = codes.shape[0] // TILE
        self.half = (self.tiles - 2) // 2
        self.group = y.astype(jnp.int32).reshape(1)
        self.head = weight_tiles(self.group, codes, self.scales, 0, 1, self.half)
        self.x0 = across(self.head)

    def sum_parts(self, parts):
        others = turns(parts)
        self.up1 = line(after(self.own, parts), 0)(1)
        self.dn1 = line(after(self.own, parts), 0)(-1)
        group = after(self.group, *others)
        self.tail = weight_tiles(group, self.codes, self.scales, 1, self.tiles - 1, self.half)
        self.x1 = across(self.tail[0:1])
        self.sib_tail = core(self.tail)
        self.sib_head = core(after(self.head, self.sib_tail))
        self.y0 = over(self.x0)
        self.x2 = across(after(self.tail[1:2], self.sib_tail))
        total = parts.astype(jnp.float32)
        for other in others:
            total = total + other.astype(jnp.float32)
        return total

    def gather_rows(self, row):
        pair = jnp.concatenate([row, core(row)])
        rows = jnp.concatenate([pair, across(pair)])
        return after(rows, self.y0)

    def finish(self, done, state_part):
        up2, dn2 = line(self.up1, 1)(1), line(self.dn1, 1)(-1)
        y1 = over(after(self.x1, self.up1, self.dn1))
        x3 = across(after(self.tail[5:7], self.y0))
        y2 = over(after(self.x2, done))
        up3, dn3 = line(after(up2, done), 2)(1), line(after(dn2, done), 2)(-1)
        early = after((self.x0, self.x1, self.y0, self.x2, y1), up2, dn2, done, self.sib_head)
        far1 = gather_tiles(early)
        sib_far1 = core(far1)
        sib_far2 = core(after(y2, sib_far1))
        state_sum = state_part
        for other in turns(after(state_part, up3, dn3)):
            state_sum = state_sum + other
        sib_far3 = core(after(x3, up3, dn3, sib_far2))
        arrays = [self.head, self.tail, self.sib_head, self.sib_tail]
        arrays += [far1, y2, x3, sib_far1, sib_far2, sib_far3]
        far_places = [(4, 0), (4, 1), (4, 3), (4, 2), (4, 4), (5, 0), (6, 0), (6, 1)]
        where = []
        for i in range(self.tiles):
            mine = (0, 0) if i == 0 else (1, i - 1)
            far = far_places[i]
            where += [mine, (mine[0] + 2, mine[1]), far, (far[0] + 3, far[1])]
        near = [self.own, self.up1, self.dn1, up2, dn2, up3, dn3]
        return near, arrays, where, state_sum


def shards(
    hidden_in,
    cotangent,
    base_codes,
    base_scales,
    factor_a,
    factor_b,
    task_state,
    head_a,
    head_b,
    task_ids,
    valid_counts,
    owners,
):
    f32, bf16 = jnp.float32, jnp.bfloat16
    n_groups, n_fsdp, n_dp = (lax.axis_size(a) for a in ("groups", "fsdp", "dp"))
    z, p, y = (lax.axis_index(a) for a in ("fsdp", "dp", "groups"))
    seq_len, width_part = hidden_in.shape
    tasks_all, factor_cols = factor_a.shape
    rank_double = factor_cols // width_part
    rank_half = rank_double // 2
    joined_part = cotangent.shape[1]
    own = cotangent[:LIVE]
    lines = (n_groups, n_fsdp, n_dp) == (2, 4, 4) and width_part == 8 * TILE
    plan = Plan(own, base_codes, base_scales, y) if lines else None

    task = task_ids[0]
    chosen_a = lax.dynamic_slice_in_dim(factor_a, task, 1, 0).reshape(width_part, rank_double)
    chosen_b = lax.dynamic_slice_in_dim(factor_b, task, 1, 0).reshape(joined_part, rank_half)
    first_column = (z * joined_part).astype(jnp.int32).reshape(1)
    parts = whole_call(
        product_kernel,
        jax.ShapeDtypeStruct((LIVE, 2 * rank_double), bf16),
        hidden_in,
        cotangent,
        chosen_a,
        chosen_b,
        scalars=(first_column,),
    )
    if lines:
        sums = plan.sum_parts(parts)
    else:
        sums = jnp.sum(lax.all_gather(parts, "fsdp", axis=0).astype(f32), axis=0)
    keep = lax.broadcasted_iota(jnp.int32, (LIVE, 1), 0) < valid_counts[0]
    sums = jnp.where(keep, sums, 0.0).astype(bf16)
    low_in, low_grad = sums[:, :rank_double], sums[:, rank_double:]

    down_gradient, up_gradient = whole_call(
        factor_kernel,
        [
            jax.ShapeDtypeStruct((width_part, rank_double), f32),
            jax.ShapeDtypeStruct((joined_part, rank_half), f32),
        ],
        hidden_in,
        cotangent,
        low_grad,
        low_in,
        scalars=(first_column,),
    )
    down_cols = width_part * rank_double
    up_cols = joined_part * rank_half
    row = jnp.concatenate(
        [
            down_gradient.astype(bf16).reshape(1, down_cols),
            up_gradient.astype(bf16).reshape(1, up_cols),
            jnp.full((1, 128), task, f32).astype(bf16),
        ],
        axis=1,
    )
    rows = plan.gather_rows(row) if lines else lax.all_gather(row, "dp", axis=0, tiled=True)
    ids = rows[:, down_cols + up_cols].astype(jnp.int32)
    one_hot = ids[:, None] == lax.broadcasted_iota(jnp.int32, (1, tasks_all), 1)
    states = jnp.dot(one_hot.astype(bf16), task_state, preferred_element_type=f32).astype(bf16)
    block = math.gcd(down_cols, up_cols)
    grad_head_a, part_a = head_grads(states, rows, head_a, 0, block)
    grad_head_b, part_b = head_grads(states, rows, head_b, down_cols, block)
    state_part = part_a + part_b
    if lines:
        done = (grad_head_a, grad_head_b)
        near, arrays, where, state_sum = plan.finish(done, state_part)
    else:
        state_sum = jnp.sum(lax.all_gather(state_part, "fsdp", axis=0), axis=0)
    task_rows = lax.broadcasted_iota(jnp.int32, (tasks_all, tasks_all), 0)
    task_other = lax.broadcasted_iota(jnp.int32, (tasks_all, tasks_all), 1)
    same_owner = owners[:, None] == owners[None, :]
    slot_index = jnp.sum((same_owner & (task_other < task_rows)).astype(jnp.int32), axis=1)
    target = owners * SLOTS + slot_index
    seq_target = jnp.sum(jnp.where(one_hot, target[None, :], 0), axis=1)
    own_rows = z * SLOTS + lax.broadcasted_iota(jnp.int32, (SLOTS, 1), 0)
    selector = (own_rows == seq_target[None, :]).astype(f32)
    grad_state = jnp.sum(selector[:, :, None] * state_sum[None, :, :], axis=1)

    if lines:
        meta = jnp.stack([z, p, y, valid_counts[0]]).astype(jnp.int32)
        input_gradient = input_gradient_call(
            meta, low_grad, chosen_a, near, arrays, where, plan.tiles, seq_len
        )
    else:
        weight = dequantize(
            lax.all_gather(base_codes, "dp", axis=1, tiled=True),
            lax.all_gather(base_scales, "dp", axis=1, tiled=True),
        )
        merged = lax.dot_general(
            lax.all_gather(own, "fsdp", axis=1, tiled=True),
            weight,
            (((1,), (1,)), ((), ())),
            preferred_element_type=f32,
        )
        adapter = lax.dot_general(
            low_grad, chosen_a, (((1,), (1,)), ((), ())), preferred_element_type=f32
        )
        live = (jnp.where(keep, merged, 0.0) + adapter_scale * adapter).astype(bf16)
        input_gradient = jnp.pad(live, ((0, seq_len - LIVE), (0, 0)))
    return (input_gradient, grad_head_a, grad_head_b, grad_state)


def solution(mesh):
    placed = (
        P(("groups", "dp"), "fsdp"),
        P(("groups", "dp"), "fsdp"),
        P("fsdp", "dp"),
        P("fsdp", "dp"),
        P("groups", "fsdp"),
        P("groups", "fsdp"),
        P("groups", "dp"),
        P("dp", "fsdp"),
        P("dp", "fsdp"),
        P(("groups", "dp")),
        P(("groups", "dp")),
        P("groups"),
    )
    return jax.shard_map(
        shards,
        mesh=mesh,
        in_specs=placed,
        out_specs=(
            P(("groups", "dp"), "fsdp"),
            P(("groups", "dp"), "fsdp"),
            P(("groups", "dp"), "fsdp"),
            P(("groups", "fsdp"), "dp"),
        ),
        check_vma=False,
    )
```

time: 449 us -> 235 us (0.52)
  Pallas kernels: 249 us -> 52.3 us
  blocking collectives: 55.8 us -> 0 us
  waiting for transfers between devices: 78.2 us -> 101 us
  starting transfers between devices: 20.7 us -> 33.7 us
    pallas_call x6, Pallas kernels: 231 us -> 34.3 us  [the longest x1 23.6 us: input_gradient_call(): pl.pallas_call(lambda *refs: input_gradient_kernel(tiles, where, len(arra...]
    all_gather x3 -> x0, blocking collectives: 55.8 us -> none  [the longest x1 22.9 us: shards(): rows = lax.all_gather(row, 'dp', axis=0, tiled=True)]
    ppermute x18 -> x26, waiting for transfers between devices: 78.2 us -> 101 us  [the longest x5 51.2 us: across(): return lax.ppermute(value, 'dp', [(i, i ^ 2) for i in range(4)])]
    ppermute x18 -> x26, starting transfers between devices: 20.7 us -> 33.7 us  [the longest x6 12.2 us: turns(): lax.ppermute(value, 'fsdp', [(i, (i + k) % 4) for i in range(4)])]
    unnamed x47 -> x70, local copies, waits for them, and re-layouts: 21.7 us -> 31.3 us
  transfers between devices with their start and end apart: 18 -> 26, of which waited for: 4 -> 8; matrix products, arithmetic and copies ran while one was open for 4% -> 4% of each run, Pallas kernels for 6% -> 11%
where the time goes in v3:
time: 235 us; the launch traced here: 234 us
  waiting for transfers between devices  101 us (43%)
  Pallas kernels  52.3 us (22%)
  local copies, waits for them, and re-layouts  38 us (16%)
  starting transfers between devices  33.7 us (14%)
  other arithmetic  5.97 us (3%)
  between operations  2.65 us (1%)
    ppermute x5, waiting for transfers between devices, across(): return lax.ppermute(value, 'dp', [(i, i ^ 2) for i in range(4)])  51.2 us
    unnamed x70, local copies, waits for them, and re-layouts  31.3 us
    pallas_call x1, Pallas kernels, input_gradient_call(): pl.pallas_call(lambda *refs: input_gradient_kernel(tiles, where, len(arra...  23.6 us
    ppermute x3, waiting for transfers between devices, over(): return lax.ppermute(value, 'groups', [(0, 1), (1, 0)])  22.5 us
    pallas_call x2, Pallas kernels, head_grads(): pl.pallas_call(head_kernel, out_shape=[jax.ShapeDtypeStruct((hidden_units...  17.9 us
    ppermute x6, waiting for transfers between devices, send(): lax.ppermute(value, 'fsdp', pairs if sign > 0 else [(3 - a, 3 - b) for a,...  13.3 us
    ppermute x6, starting transfers between devices, turns(): lax.ppermute(value, 'fsdp', [(i, (i + k) % 4) for i in range(4)])  12.2 us
    ppermute x6, starting transfers between devices, send(): lax.ppermute(value, 'fsdp', pairs if sign > 0 else [(3 - a, 3 - b) for a,...  11.8 us
  transfers between devices with their start and end apart: 26, of which 8 were waited for; matrix products, arithmetic and copies ran while one was open for 4% of the time, Pallas kernels for 11%

profile of v3, /device:TPU:0, one launch (start us, length us, event | category | flops | bytes accessed | tf_op | source)
XLA Modules:
  0.0 233.8 jit_solution(5246941569900906983)
XLA Ops:
  4.1 1.7 copy-done.6
  5.7 1.6 copy-done.8
  8.6 5.1 %collective-permute-start.2 = (bf16[384,32]{1,0:T(8,128)(2,1)S(1)}, bf16[384,32]{1,0:T(8,128)(2,1)S(1)}, u32[]{:S(2)}, u32[]{:S(2)}) collective-permute-start(bf16[384,32]{1,0:T(8,128)(2,1)S(1)} %shard_map.147), channel_id=1, source_target_pairs={{0,12},{4,0},{8,4},{12,8},{1,13},{5,1},{9,5},{13,9},{2,14},{6,2},{... | collective-permute-start | bytes 73736 | tf_op jit(solution)/shard_map/ppermute | solution.py:267
  16.1 6.2 %collective-permute-start.3 = (bf16[384,2304]{1,0:T(8,128)(2,1)S(1)}, bf16[384,2304]{1,0:T(8,128)(2,1)}, u32[]{:S(2)}, u32[]{:S(2)}) collective-permute-start(bf16[384,2304]{1,0:T(8,128)(2,1)S(1)} %slice.22.refs_3_), channel_id=1, source_target_pairs={{0,4},{4,8},{8,12},{1,5},{5,9},{9,13},{2,6},{6,10},{10,14},{3,7},{... | collective-permute-start | bytes 5308424 | tf_op jit(solution)/shard_map/ppermute | solution.py:261
  23.1 3.7 %copy-done.3 = bf16[2048,2304]{1,0:T(8,128)(2,1)S(1)} copy-done((bf16[2048,2304]{1,0:T(8,128)(2,1)S(1)}, bf16[2048,2304]{1,0:T(8,128)(2,1)}, u32[]{:S(2)}) %copy-start.3) | copy-done | bytes 9437208
  26.7 1.5 shard_map.149.refs_10_
  28.3 1.5 collective-permute-start.9
  30.0 1.8 shard_map.148
  33.3 2.2 convert_element_type.50
  35.5 1.6 reshape.69
  37.1 3.7 %copy-done.4 = bf16[2048,2304]{1,0:T(8,128)(2,1)S(1)} copy-done((bf16[2048,2304]{1,0:T(8,128)(2,1)S(1)}, bf16[2048,2304]{1,0:T(8,128)(2,1)}, u32[]{:S(2)}) %copy-start.4) | copy-done | bytes 9437208
  40.8 3.7 %shard_map.152.refs_11_ = bf16[7,256,2304]{2,1,0:T(8,128)(2,1)S(1)} custom-call(s32[1]{0:T(128)} %bitcast.2.group, bf16[2048,2304]{1,0:T(8,128)(2,1)S(1)} %copy-done.4, bf16[36,2048]{1,0:T(8,128)(2,1)S(1)} %bitcast.16), custom_call_target="tpu_custom_call" | custom-call | tf_op jit(solution)/shard_map/pallas_call | solution.py:54
  45.3 1.7 fusion.2
  47.0 10.8 %collective-permute-done.7 = bf16[1,51328]{1,0:T(2,128)(2,1)S(1)} collective-permute-done((bf16[1,51328]{1,0:T(2,128)(2,1)S(1)}, bf16[1,51328]{1,0:T(2,128)(2,1)S(1)}, u32[]{:S(2)}, u32[]{:S(2)}) %collective-permute-start.7) | collective-permute-done | bytes 102688 | tf_op jit(solution)/shard_map/ppermute | solution.py:251
  58.7 1.5 collective-permute-start.10
  60.7 25.1 %collective-permute-done.15.refs_1_ = bf16[1,256,2304]{2,1,0:T(8,128)(2,1)S(1)} collective-permute-done((bf16[1,256,2304]{2,1,0:T(8,128)(2,1)S(1)}, bf16[1,256,2304]{2,1,0:T(8,128)(2,1)S(1)}, u32[]{:S(2)}, u32[]{:S(2)}) %collective-permute-start.15) | collective-permute-done | bytes 1179680 | tf_op jit(solution)/shard_map/ppermute | solution.py:247
  86.7 1.5 collective-permute-start.17
  90.3 1.8 collective-permute-done.8
  93.1 1.6 pad_maximum_fusion.rows
  95.0 6.7 %shard_map.151 = (f32[128,18432]{1,0:T(8,128)}, f32[4,128]{1,0:T(4,128)S(1)}) custom-call(bf16[4,128]{1,0:T(4,128)(2,1)S(1)} %convolution_convert_fusion.states, bf16[4,51328]{1,0:T(4,128)(2,1)S(1)} %pad_maximum_fusion.rows, bf16[128,18432]{1,0:T(8,128)(2,1)S(1)} %bitcast.14), custom_call_target="tpu_custom_call" | custom-call | tf_op jit(solution)/shard_map/pallas_call | solution.py:119
  101.7 3.4 %copy-done.10 = bf16[128,32768]{1,0:T(8,128)(2,1)S(1)} copy-done((bf16[128,32768]{1,0:T(8,128)(2,1)S(1)}, bf16[128,32768]{1,0:T(8,128)(2,1)}, u32[]{:S(2)}) %copy-start.10) | copy-done | bytes 8388632
  105.1 11.3 %shard_map.150 = (f32[128,32768]{1,0:T(8,128)}, f32[4,128]{1,0:T(4,128)S(1)}) custom-call(bf16[4,128]{1,0:T(4,128)(2,1)S(1)} %convolution_convert_fusion.states, bf16[4,51328]{1,0:T(4,128)(2,1)S(1)} %pad_maximum_fusion.rows, bf16[128,32768]{1,0:T(8,128)(2,1)S(1)} %copy-done.10), custom_call_target="tpu_custom_call" | custom-call | tf_op jit(solution)/shard_map/pallas_call | solution.py:119
  116.4 13.2 %collective-permute-done.6.refs_7_ = bf16[384,2304]{1,0:T(8,128)(2,1)S(1)} collective-permute-done((bf16[384,2304]{1,0:T(8,128)(2,1)}, bf16[384,2304]{1,0:T(8,128)(2,1)S(1)}, u32[]{:S(2)}, u32[]{:S(2)}) %collective-permute-start.6) | collective-permute-done | bytes 1769504 | tf_op jit(solution)/shard_map/ppermute | solution.py:261
  129.7 2.1 copy-done.22
  133.1 2.4 %shard_map.153.refs_14_ = bf16[5,256,2304]{2,1,0:T(8,128)(2,1)S(1)} custom-call(bf16[1,256,2304]{2,1,0:T(8,128)(2,1)} %collective-permute-done.9.refs_0_, bf16[1,256,2304]{2,1,0:T(8,128)(2,1)S(1)} %copy-done.22, bf16[1,256,2304]{2,1,0:T(8,128)(2,1)S(1)} %copy-done.24, bf16[1,256,2304]{2,1,0:T(8,128)(2,1)} %collective-permute-done.16.refs_3_, ...), custom_call_target="tpu_custom_call" | custom-call | tf_op jit(solution)/shard_map/pallas_call | solution.py:142
  135.7 2.3 copy-done.5
  141.9 22.5 %collective-permute-done.18.refs_15_ = bf16[1,256,2304]{2,1,0:T(8,128)(2,1)S(1)} collective-permute-done((bf16[1,256,2304]{2,1,0:T(8,128)(2,1)}, bf16[1,256,2304]{2,1,0:T(8,128)(2,1)S(1)}, u32[]{:S(2)}, u32[]{:S(2)}) %collective-permute-start.18) | collective-permute-done | bytes 1179680 | tf_op jit(solution)/shard_map/ppermute | solution.py:255
  165.4 24.4 %collective-permute-done.19.refs_16_ = bf16[2,256,2304]{2,1,0:T(8,128)(2,1)} collective-permute-done((bf16[2,256,2304]{2,1,0:T(8,128)(2,1)S(1)}, bf16[2,256,2304]{2,1,0:T(8,128)(2,1)}, u32[]{:S(2)}, u32[]{:S(2)}) %collective-permute-start.19) | collective-permute-done | bytes 2359328 | tf_op jit(solution)/shard_map/ppermute | solution.py:247
  193.1 3.8 %collective-permute-start.25 = (f32[4,128]{1,0:T(4,128)S(1)}, f32[4,128]{1,0:T(4,128)S(1)}, u32[]{:S(2)}, u32[]{:S(2)}) collective-permute-start(f32[4,128]{1,0:T(4,128)S(1)} %add.46), channel_id=1, source_target_pairs={{0,12},{4,0},{8,4},{12,8},{1,13},{5,1},{9,5},{13,9},{2,14},{6,2},{... | collective-permute-start | bytes 6152 | tf_op jit(solution)/shard_map/ppermute | solution.py:267
  197.2 1.9 collective-permute-start.23
  199.2 2.1 collective-permute-done.24
  210.0 23.6 %shard_map.154 = bf16[512,2048]{1,0:T(8,128)(2,1)} custom-call(s32[4]{0:T(128)S(1)} %pad_add_fusion.refs_0_, bf16[384,16]{1,0:T(8,128)(2,1)S(1)} %get-tuple-element.55.grad.refs_1_, bf16[2048,16]{1,0:T(8,128)(2,1)S(1)} %reshape.66.chosen_a.refs_2_, bf16[384,2304]{1,0:T(8,128)(2,1)S(1)} %slice.22.refs_3_, bf16[384,2304]{1,0:T(8,128)(2,1)} %collective-permute-done.3.refs_4_, ...), custom_call_target="tpu_custom_call" | custom-call | tf_op jit(solution)/shard_map/pallas_call | solution.py:219
  (128 shorter events, 33.3 us)
Async XLA Ops:
  8.6 19.7 %collective-permute-start.2 = (bf16[384,32]{1,0:T(8,128)(2,1)S(1)}, bf16[384,32]{1,0:T(8,128)(2,1)S(1)}, u32[]{:S(2)}, u32[]{:S(2)}) collective-permute-start(bf16[384,32]{1,0:T(8,128)(2,1)S(1)} %shard_map.147), channel_id=1, source_target_pairs={{0,12},{4,0},{8,4},{12,8},{1,13},{5,1},{9,5},{13,9},{2,14},{6,2},{... | collective-permute-start | bytes 73736 | tf_op jit(solution)/shard_map/ppermute | solution.py:267
  13.7 16.1 %collective-permute-start.1 = (bf16[384,32]{1,0:T(8,128)(2,1)S(1)}, bf16[384,32]{1,0:T(8,128)(2,1)S(1)}, u32[]{:S(2)}, u32[]{:S(2)}) collective-permute-start(bf16[384,32]{1,0:T(8,128)(2,1)S(1)} %shard_map.147), channel_id=1, source_target_pairs={{0,8},{4,12},{8,0},{12,4},{1,9},{5,13},{9,1},{13,5},{2,10},{6,14},... | collective-permute-start | bytes 73736 | tf_op jit(solution)/shard_map/ppermute | solution.py:267
  13.7 16.1 %collective-permute-start = (bf16[384,32]{1,0:T(8,128)(2,1)S(1)}, bf16[384,32]{1,0:T(8,128)(2,1)S(1)}, u32[]{:S(2)}, u32[]{:S(2)}) collective-permute-start(bf16[384,32]{1,0:T(8,128)(2,1)S(1)} %shard_map.147), channel_id=1, source_target_pairs={{0,4},{4,8},{8,12},{12,0},{1,5},{5,9},{9,13},{13,1},{2,6},{6,10},{... | collective-permute-start | bytes 73736 | tf_op jit(solution)/shard_map/ppermute | solution.py:267
  14.8 71.9 %collective-permute-start.4 = (bf16[384,2304]{1,0:T(8,128)(2,1)S(1)}, bf16[384,2304]{1,0:T(8,128)(2,1)}, u32[]{:S(2)}, u32[]{:S(2)}) collective-permute-start(bf16[384,2304]{1,0:T(8,128)(2,1)S(1)} %slice.22.refs_3_), channel_id=1, source_target_pairs={{12,8},{8,4},{4,0},{13,9},{9,5},{5,1},{14,10},{10,6},{6,2},{15,11}... | collective-permute-start | bytes 5308424 | tf_op jit(solution)/shard_map/ppermute | solution.py:261
  16.1 70.6 %collective-permute-start.3 = (bf16[384,2304]{1,0:T(8,128)(2,1)S(1)}, bf16[384,2304]{1,0:T(8,128)(2,1)}, u32[]{:S(2)}, u32[]{:S(2)}) collective-permute-start(bf16[384,2304]{1,0:T(8,128)(2,1)S(1)} %slice.22.refs_3_), channel_id=1, source_target_pairs={{0,4},{4,8},{8,12},{1,5},{5,9},{9,13},{2,6},{6,10},{10,14},{3,7},{... | collective-permute-start | bytes 5308424 | tf_op jit(solution)/shard_map/ppermute | solution.py:261
  28.3 30.5 %collective-permute-start.9 = (bf16[1,256,2304]{2,1,0:T(8,128)(2,1)}, bf16[1,256,2304]{2,1,0:T(8,128)(2,1)}, u32[]{:S(2)}, u32[]{:S(2)}) collective-permute-start(bf16[1,256,2304]{2,1,0:T(8,128)(2,1)} %shard_map.149.refs_10_), channel_id=1, source_target_pairs={{0,2},{1,3},{2,0},{3,1},{4,6},{5,7},{6,4},{7,5},{8,10},{9,11},{10,... | collective-permute-start | bytes 3538952 | tf_op jit(solution)/shard_map/ppermute | solution.py:247
  33.3 27.0 %copy-start.28 = (bf16[1,32768]{1,0:T(2,128)(2,1)}, bf16[1,32768]{1,0:T(2,128)(2,1)S(1)}, u32[]{:S(2)}) copy-start(bf16[1,32768]{1,0:T(2,128)(2,1)S(1)} %reshape.68) | copy-start | bytes 196612
  33.3 61.7 %slice-start = ((s8[4718592]{0:T(1024)(128)(4,1)}), s8[524288]{0:T(1024)(128)(4,1)S(1)}, s32[]{:S(2)}) async-start(s8[4718592]{0:T(1024)(128)(4,1)} %bitcast.13), calls=%async_computation | async-start | bytes 1048576
  40.8 54.2 %slice-start.1 = ((s8[4718592]{0:T(1024)(128)(4,1)}), s8[4194304]{0:T(1024)(128)(4,1)S(1)}, s32[]{:S(2)}) async-start(s8[4718592]{0:T(1024)(128)(4,1)} %bitcast.13), calls=%async_computation.1 | async-start | bytes 8388608
  44.5 91.1 %copy-start.2 = (bf16[7,256,2304]{2,1,0:T(8,128)(2,1)}, bf16[7,256,2304]{2,1,0:T(8,128)(2,1)S(1)}, u32[]{:S(2)}) copy-start(bf16[7,256,2304]{2,1,0:T(8,128)(2,1)S(1)} %shard_map.152.refs_11_) | copy-start | bytes 24772612
  44.5 45.1 %collective-permute-start.13 = (bf16[7,256,2304]{2,1,0:T(8,128)(2,1)S(1)}, bf16[7,256,2304]{2,1,0:T(8,128)(2,1)S(1)}, u32[]{:S(2)}, u32[]{:S(2)}) collective-permute-start(bf16[7,256,2304]{2,1,0:T(8,128)(2,1)S(1)} %shard_map.152.refs_11_), channel_id=1, source_target_pairs={{0,1},{1,0},{2,3},{3,2},{4,5},{5,4},{6,7},{7,6},{8,9},{9,8},{10,11... | collective-permute-start | bytes 24772616 | tf_op jit(solution)/shard_map/ppermute | solution.py:251
  44.8 50.1 %copy-start.31 = (bf16[16,128]{1,0:T(8,128)(2,1)S(1)}, bf16[16,128]{1,0:T(8,128)(2,1)}, u32[]{:S(2)}) copy-start(bf16[16,128]{1,0:T(8,128)(2,1)} %param.18) | copy-start | bytes 12292
  44.8 13.0 %collective-permute-start.7 = (bf16[1,51328]{1,0:T(2,128)(2,1)S(1)}, bf16[1,51328]{1,0:T(2,128)(2,1)S(1)}, u32[]{:S(2)}, u32[]{:S(2)}) collective-permute-start(bf16[1,51328]{1,0:T(2,128)(2,1)S(1)} %pad_maximum_fusion.1), channel_id=1, source_target_pairs={{0,1},{1,0},{2,3},{3,2},{4,5},{5,4},{6,7},{7,6},{8,9},{9,8},{10,11... | collective-permute-start | bytes 307976 | tf_op jit(solution)/shard_map/ppermute | solution.py:251
  57.8 28.0 %collective-permute-start.15 = (bf16[1,256,2304]{2,1,0:T(8,128)(2,1)S(1)}, bf16[1,256,2304]{2,1,0:T(8,128)(2,1)S(1)}, u32[]{:S(2)}, u32[]{:S(2)}) collective-permute-start(bf16[1,256,2304]{2,1,0:T(8,128)(2,1)S(1)} %get-tuple-element.53), channel_id=1, source_target_pairs={{0,2},{1,3},{2,0},{3,1},{4,6},{5,7},{6,4},{7,5},{8,10},{9,11},{10,... | collective-permute-start | bytes 3538952 | tf_op jit(solution)/shard_map/ppermute | solution.py:247
  58.7 33.4 %collective-permute-start.10 = (bf16[1,256,2304]{2,1,0:T(8,128)(2,1)}, bf16[1,256,2304]{2,1,0:T(8,128)(2,1)S(1)}, u32[]{:S(2)}, u32[]{:S(2)}) collective-permute-start(bf16[1,256,2304]{2,1,0:T(8,128)(2,1)} %collective-permute-done.9.refs_0_), channel_id=1, source_target_pairs={{0,16},{16,0},{1,17},{17,1},{2,18},{18,2},{3,19},{19,3},{4,20},{20... | collective-permute-start | bytes 3538952 | tf_op jit(solution)/shard_map/ppermute | solution.py:255
  85.8 6.3 %collective-permute-start.8 = (bf16[2,51328]{1,0:T(2,128)(2,1)S(1)}, bf16[2,51328]{1,0:T(2,128)(2,1)S(1)}, u32[]{:S(2)}, u32[]{:S(2)}) collective-permute-start(bf16[2,51328]{1,0:T(2,128)(2,1)S(1)} %pad_maximum_fusion.2), channel_id=1, source_target_pairs={{0,2},{1,3},{2,0},{3,1},{4,6},{5,7},{6,4},{7,5},{8,10},{9,11},{10,... | collective-permute-start | bytes 615944 | tf_op jit(solution)/shard_map/ppermute | solution.py:247
  86.7 29.6 %collective-permute-start.17 = (bf16[1,256,2304]{2,1,0:T(8,128)(2,1)S(1)}, bf16[1,256,2304]{2,1,0:T(8,128)(2,1)}, u32[]{:S(2)}, u32[]{:S(2)}) collective-permute-start(bf16[1,256,2304]{2,1,0:T(8,128)(2,1)S(1)} %collective-permute-done.15.refs_1_), channel_id=1, source_target_pairs={{0,16},{16,0},{1,17},{17,1},{2,18},{18,2},{3,19},{19,3},{4,20},{20... | collective-permute-start | bytes 3538952 | tf_op jit(solution)/shard_map/ppermute | solution.py:255
  88.3 41.4 %collective-permute-start.6 = (bf16[384,2304]{1,0:T(8,128)(2,1)}, bf16[384,2304]{1,0:T(8,128)(2,1)S(1)}, u32[]{:S(2)}, u32[]{:S(2)}) collective-permute-start(bf16[384,2304]{1,0:T(8,128)(2,1)} %collective-permute-done.4.refs_5_), channel_id=1, source_target_pairs={{8,4},{4,0},{9,5},{5,1},{10,6},{6,2},{11,7},{7,3},{24,20},{20,16},... | collective-permute-start | bytes 5308424 | tf_op jit(solution)/shard_map/ppermute | solution.py:261
  89.6 40.0 %collective-permute-start.5 = (bf16[384,2304]{1,0:T(8,128)(2,1)}, bf16[384,2304]{1,0:T(8,128)(2,1)S(1)}, u32[]{:S(2)}, u32[]{:S(2)}) collective-permute-start(bf16[384,2304]{1,0:T(8,128)(2,1)} %collective-permute-done.3.refs_4_), channel_id=1, source_target_pairs={{4,8},{8,12},{5,9},{9,13},{6,10},{10,14},{7,11},{11,15},{20,24},{2... | collective-permute-start | bytes 5308424 | tf_op jit(solution)/shard_map/ppermute | solution.py:261
  92.1 37.5 %collective-permute-start.14 = (bf16[1,256,2304]{2,1,0:T(8,128)(2,1)}, bf16[1,256,2304]{2,1,0:T(8,128)(2,1)S(1)}, u32[]{:S(2)}, u32[]{:S(2)}) collective-permute-start(bf16[1,256,2304]{2,1,0:T(8,128)(2,1)} %shard_map.149.refs_10_), channel_id=1, source_target_pairs={{0,1},{1,0},{2,3},{3,2},{4,5},{5,4},{6,7},{7,6},{8,9},{9,8},{10,11... | collective-permute-start | bytes 3538952 | tf_op jit(solution)/shard_map/ppermute | solution.py:251
  92.1 37.5 %collective-permute-start.16 = (bf16[1,256,2304]{2,1,0:T(8,128)(2,1)}, bf16[1,256,2304]{2,1,0:T(8,128)(2,1)}, u32[]{:S(2)}, u32[]{:S(2)}) collective-permute-start(bf16[1,256,2304]{2,1,0:T(8,128)(2,1)} %get-tuple-element.38), channel_id=1, source_target_pairs={{0,2},{1,3},{2,0},{3,1},{4,6},{5,7},{6,4},{7,5},{8,10},{9,11},{10,... | collective-permute-start | bytes 3538952 | tf_op jit(solution)/shard_map/ppermute | solution.py:247
  135.5 57.2 %copy-start.32 = (s32[16]{0:T(128)S(1)}, s32[16]{0:T(128)}, u32[]{:S(2)}) copy-start(s32[16]{0:T(128)} %param.23) | copy-start | bytes 196
  135.5 28.9 %collective-permute-start.20 = (bf16[5,256,2304]{2,1,0:T(8,128)(2,1)S(1)}, bf16[5,256,2304]{2,1,0:T(8,128)(2,1)}, u32[]{:S(2)}, u32[]{:S(2)}) collective-permute-start(bf16[5,256,2304]{2,1,0:T(8,128)(2,1)S(1)} %shard_map.153.refs_14_), channel_id=1, source_target_pairs={{0,1},{1,0},{2,3},{3,2},{4,5},{5,4},{6,7},{7,6},{8,9},{9,8},{10,11... | collective-permute-start | bytes 17694728 | tf_op jit(solution)/shard_map/ppermute | solution.py:251
  138.0 26.4 %collective-permute-start.18 = (bf16[1,256,2304]{2,1,0:T(8,128)(2,1)}, bf16[1,256,2304]{2,1,0:T(8,128)(2,1)S(1)}, u32[]{:S(2)}, u32[]{:S(2)}) collective-permute-start(bf16[1,256,2304]{2,1,0:T(8,128)(2,1)} %collective-permute-done.16.refs_3_), channel_id=1, source_target_pairs={{0,16},{16,0},{1,17},{17,1},{2,18},{18,2},{3,19},{19,3},{4,20},{20... | collective-permute-start | bytes 3538952 | tf_op jit(solution)/shard_map/ppermute | solution.py:255
  138.5 51.3 %collective-permute-start.19 = (bf16[2,256,2304]{2,1,0:T(8,128)(2,1)S(1)}, bf16[2,256,2304]{2,1,0:T(8,128)(2,1)}, u32[]{:S(2)}, u32[]{:S(2)}) collective-permute-start(bf16[2,256,2304]{2,1,0:T(8,128)(2,1)S(1)} %slice.32), channel_id=1, source_target_pairs={{0,2},{1,3},{2,0},{3,1},{4,6},{5,7},{6,4},{7,5},{8,10},{9,11},{10,... | collective-permute-start | bytes 7077896 | tf_op jit(solution)/shard_map/ppermute | solution.py:247
  139.6 50.2 %collective-permute-start.11 = (bf16[384,2304]{1,0:T(8,128)(2,1)S(1)}, bf16[384,2304]{1,0:T(8,128)(2,1)S(1)}, u32[]{:S(2)}, u32[]{:S(2)}) collective-permute-start(bf16[384,2304]{1,0:T(8,128)(2,1)S(1)} %collective-permute-done.5.refs_6_), channel_id=1, source_target_pairs={{8,12},{9,13},{10,14},{11,15},{24,28},{25,29},{26,30},{27,31}} | collective-permute-start | bytes 5308424 | tf_op jit(solution)/shard_map/ppermute | solution.py:261
  140.4 49.4 %collective-permute-start.12 = (bf16[384,2304]{1,0:T(8,128)(2,1)S(1)}, bf16[384,2304]{1,0:T(8,128)(2,1)S(1)}, u32[]{:S(2)}, u32[]{:S(2)}) collective-permute-start(bf16[384,2304]{1,0:T(8,128)(2,1)S(1)} %collective-permute-done.6.refs_7_), channel_id=1, source_target_pairs={{4,0},{5,1},{6,2},{7,3},{20,16},{21,17},{22,18},{23,19}} | collective-permute-start | bytes 5308424 | tf_op jit(solution)/shard_map/ppermute | solution.py:261
  164.4 25.4 %collective-permute-start.21 = (bf16[1,256,2304]{2,1,0:T(8,128)(2,1)S(1)}, bf16[1,256,2304]{2,1,0:T(8,128)(2,1)S(1)}, u32[]{:S(2)}, u32[]{:S(2)}) collective-permute-start(bf16[1,256,2304]{2,1,0:T(8,128)(2,1)S(1)} %collective-permute-done.18.refs_15_), channel_id=1, source_target_pairs={{0,1},{1,0},{2,3},{3,2},{4,5},{5,4},{6,7},{7,6},{8,9},{9,8},{10,11... | collective-permute-start | bytes 3538952 | tf_op jit(solution)/shard_map/ppermute | solution.py:251
  192.6 10.7 %collective-permute-start.22 = (bf16[2,256,2304]{2,1,0:T(8,128)(2,1)}, bf16[2,256,2304]{2,1,0:T(8,128)(2,1)}, u32[]{:S(2)}, u32[]{:S(2)}) collective-permute-start(bf16[2,256,2304]{2,1,0:T(8,128)(2,1)} %collective-permute-done.19.refs_16_), channel_id=1, source_target_pairs={{0,1},{1,0},{2,3},{3,2},{4,5},{5,4},{6,7},{7,6},{8,9},{9,8},{10,11... | collective-permute-start | bytes 7077896 | tf_op jit(solution)/shard_map/ppermute | solution.py:251
  193.1 6.1 %collective-permute-start.25 = (f32[4,128]{1,0:T(4,128)S(1)}, f32[4,128]{1,0:T(4,128)S(1)}, u32[]{:S(2)}, u32[]{:S(2)}) collective-permute-start(f32[4,128]{1,0:T(4,128)S(1)} %add.46), channel_id=1, source_target_pairs={{0,12},{4,0},{8,4},{12,8},{1,13},{5,1},{9,5},{13,9},{2,14},{6,2},{... | collective-permute-start | bytes 6152 | tf_op jit(solution)/shard_map/ppermute | solution.py:267
  196.9 4.5 %collective-permute-start.24 = (f32[4,128]{1,0:T(4,128)S(1)}, f32[4,128]{1,0:T(4,128)S(1)}, u32[]{:S(2)}, u32[]{:S(2)}) collective-permute-start(f32[4,128]{1,0:T(4,128)S(1)} %add.46), channel_id=1, source_target_pairs={{0,8},{4,12},{8,0},{12,4},{1,9},{5,13},{9,1},{13,5},{2,10},{6,14},... | collective-permute-start | bytes 6152 | tf_op jit(solution)/shard_map/ppermute | solution.py:267
  197.2 5.4 %collective-permute-start.23 = (f32[4,128]{1,0:T(4,128)S(1)}, f32[4,128]{1,0:T(4,128)S(1)}, u32[]{:S(2)}, u32[]{:S(2)}) collective-permute-start(f32[4,128]{1,0:T(4,128)S(1)} %add.46), channel_id=1, source_target_pairs={{0,4},{4,8},{8,12},{12,0},{1,5},{5,9},{9,13},{13,1},{2,6},{6,10},{... | collective-permute-start | bytes 6152 | tf_op jit(solution)/shard_map/ppermute | solution.py:267
  (29 other events, 136.8 us)

commit v4 on v3

v4 whole, which is shorter than its diff:
```python
import math

import jax
import jax.numpy as jnp
from jax import lax
from jax.experimental import pallas as pl
from jax.experimental.pallas import tpu as pltpu
from jax.sharding import PartitionSpec as P

HEADS = 64
KV_HEADS = 8
HEAD_DIM = 128
QBLOCK = 64
SLOTS = 4
LIVE = 384
TILE = 256
PIECE = 128
SENT = (3, 3)

adapter_scale = 2.0


def dequantize(codes, scales):
    rows, cols = codes.shape
    blocks = scales.shape[1]
    return (
        (
            codes.astype(jnp.float32).reshape(rows, blocks, QBLOCK)
            * scales.astype(jnp.float32)[:, :, None]
        )
        .reshape(rows, cols)
        .astype(jnp.bfloat16)
    )


def weight_kernel(ranges, group, codes, scales, out, *copies):
    cols, blocks = codes.shape[1], scales.shape[0]
    spread = (
        lax.broadcasted_iota(jnp.int32, (blocks, cols), 1) // QBLOCK
        == lax.broadcasted_iota(jnp.int32, (blocks, cols), 0)
    ).astype(jnp.bfloat16)
    wide = lax.dot_general(
        scales[...], spread, (((0,), (0,)), ((), ())), preferred_element_type=jnp.float32
    )
    piece = (codes[...].astype(jnp.float32) * wide).astype(jnp.bfloat16)
    out[0] = piece
    i = pl.program_id(0)
    for (low, high), copy in zip(ranges, copies):

        @pl.when((i >= low) & (i < high))
        def _(copy=copy):
            copy[0] = piece


def placed_piece(at, group, half):
    moved = jnp.where(at < half, at + group * half, at - group * half)
    return jnp.where(at < 2 * half, moved, at)


def weight_pieces(group, codes, scales, count, half, ranges):
    cols, blocks = codes.shape[1], scales.shape[0]
    spans = [(0, count)] + list(ranges)

    def span_spec(low, high):
        return pl.BlockSpec(
            (1, PIECE, cols), lambda i, group: (jnp.clip(i - low, 0, high - low - 1), 0, 0)
        )

    return pl.pallas_call(
        lambda *refs: weight_kernel(ranges, *refs),
        out_shape=[
            jax.ShapeDtypeStruct((high - low, PIECE, cols), jnp.bfloat16) for low, high in spans
        ],
        grid_spec=pltpu.PrefetchScalarGridSpec(
            num_scalar_prefetch=1,
            grid=(count,),
            in_specs=[
                pl.BlockSpec(
                    (PIECE, cols), lambda i, group: (placed_piece(i, group[0], half), 0)
                ),
                pl.BlockSpec(
                    (blocks, PIECE), lambda i, group: (0, placed_piece(i, group[0], half))
                ),
            ],
            out_specs=[span_spec(low, high) for low, high in spans],
        ),
        compiler_params=pltpu.CompilerParams(vmem_limit_bytes=32 * 2**20),
        cost_estimate=pl.CostEstimate(flops=0, transcendentals=0, bytes_accessed=0),
    )(group, codes, scales)


def value_columns(first, count):
    group_cols = (HEADS // KV_HEADS + 1) * HEAD_DIM
    column = first + lax.broadcasted_iota(jnp.int32, (count, 1), 0)
    return lax.rem(column, group_cols) >= HEADS // KV_HEADS * HEAD_DIM


def product_kernel(first, hidden, cotangent, chosen_a, chosen_b, out):
    value = value_columns(first[0], cotangent.shape[1])
    plain = chosen_b[...]
    empty = jnp.zeros_like(plain)
    joined = jnp.concatenate(
        [jnp.where(value, empty, plain), jnp.where(value, plain, empty)], axis=1
    )
    inner = jnp.dot(hidden[:LIVE, :], chosen_a[...], preferred_element_type=jnp.float32)
    outer = jnp.dot(cotangent[:LIVE, :], joined, preferred_element_type=jnp.float32)
    out[...] = jnp.concatenate([inner, outer], axis=1).astype(out.dtype)


def factor_kernel(scalars, hidden, cotangent, parts, down, up, low_grad):
    rank = low_grad.shape[1]
    total = parts[0].astype(jnp.float32)
    for i in range(1, parts.shape[0]):
        total = total + parts[i].astype(jnp.float32)
    keep = lax.broadcasted_iota(jnp.int32, (LIVE, 1), 0) < scalars[1]
    sums = jnp.where(keep, total, 0.0).astype(jnp.bfloat16)
    low, grad = sums[:, :rank], sums[:, rank:]
    low_grad[...] = grad
    contract = (((0,), (0,)), ((), ()))
    down[...] = adapter_scale * lax.dot_general(
        hidden[:LIVE, :], grad, contract, preferred_element_type=jnp.float32
    )
    mixed = lax.dot_general(
        cotangent[:LIVE, :], low, contract, preferred_element_type=jnp.float32
    )
    half = rank // 2
    value = value_columns(scalars[0], cotangent.shape[1])
    up[...] = adapter_scale * jnp.where(value, mixed[:, half:], mixed[:, :half])


def joined_factor_kernel(scalars, hidden, cotangent, *refs):
    parts, outs = refs[:-3], refs[-3:]
    factor_kernel(scalars, hidden, cotangent, Stack(parts), *outs)


class Stack:
    def __init__(self, refs):
        self.refs, self.shape = refs, (len(refs),) + refs[0].shape

    def __getitem__(self, index):
        return self.refs[index][...]


def row_kernel(down, up, task, out):
    down_cols, up_cols = down.shape[1], up.shape[1]
    out[:, :down_cols] = down[...]
    out[:, down_cols : down_cols + up_cols] = up[...]
    out[:, down_cols + up_cols :] = task[...]


def pair_kernel(first, second, out):
    out[0:1, :] = first[...]
    out[1:2, :] = second[...]


def head_kernel(states, *refs):
    head, grad, part = refs[-3:]
    rows = jnp.concatenate([ref[...] for ref in refs[:-3]], axis=0)
    grad[...] = lax.dot_general(
        states[...], rows, (((0,), (0,)), ((), ())), preferred_element_type=jnp.float32
    )

    @pl.when(pl.program_id(0) == 0)
    def _():
        part[...] = jnp.zeros_like(part)

    part[...] += lax.dot_general(
        rows, head[...], (((1,), (1,)), ((), ())), preferred_element_type=jnp.float32
    )


def head_grads(states, rows, head, first, block):
    hidden_units, cols = head.shape
    sequences = sum(row.shape[0] for row in rows)
    return pl.pallas_call(
        head_kernel,
        out_shape=[
            jax.ShapeDtypeStruct((hidden_units, cols), jnp.float32),
            jax.ShapeDtypeStruct((sequences, hidden_units), jnp.float32),
        ],
        grid=(cols // block,),
        in_specs=[
            pl.BlockSpec((sequences, hidden_units), lambda i: (0, 0)),
        ]
        + [pl.BlockSpec((row.shape[0], block), lambda i: (0, first // block + i)) for row in rows]
        + [pl.BlockSpec((hidden_units, block), lambda i: (0, i))],
        out_specs=[
            pl.BlockSpec((hidden_units, block), lambda i: (0, i)),
            pl.BlockSpec((sequences, hidden_units), lambda i: (0, 0)),
        ],
        compiler_params=pltpu.CompilerParams(vmem_limit_bytes=32 * 2**20),
        cost_estimate=pl.CostEstimate(flops=0, transcendentals=0, bytes_accessed=0),
    )(states, *rows, head)


def whole_call(kernel, out_shape, *operands, scalars=()):
    spec = pl.BlockSpec(memory_space=pltpu.VMEM)
    return pl.pallas_call(
        kernel,
        out_shape=out_shape,
        in_specs=[pl.BlockSpec(memory_space=pltpu.SMEM)] * len(scalars) + [spec] * len(operands),
        out_specs=jax.tree.map(lambda _: spec, out_shape),
        compiler_params=pltpu.CompilerParams(vmem_limit_bytes=32 * 2**20),
        cost_estimate=pl.CostEstimate(flops=0, transcendentals=0, bytes_accessed=0),
    )(*scalars, *operands)


def after(value, *done):
    return lax.optimization_barrier((value, done))[0]


def last_slot(z):
    return jnp.where(z == 0, 1, jnp.where(z == 3, 3, 2))


def order_of(slot, last):
    return jnp.where(slot == last, 3, jnp.where(slot < last, slot, slot - 1))


def start_copy(condition, source, target, sem):
    pl.when(condition)(lambda: pltpu.make_async_copy(source, target, sem).start())


def early_kernel(where, half, *refs):
    meta, low, chosen, own, up1, dn1, up2, dn2 = refs[:8]
    arrays, (out, cot, wbuf, csem, wsem) = refs[8:-5], refs[-5:]
    z, p, y, valid = meta[0], meta[1], meta[2], meta[3]
    depth, cols, tiles = wbuf.shape[0], own.shape[1], len(where)
    last = last_slot(z)

    def send(tile, slot):
        for side in range(2):
            for j in range(4):
                index, offset = where[tile][side][1][j]
                back = jnp.bitwise_and(z - jnp.bitwise_xor(p, j), 3)
                place = order_of(back, last)
                at = pl.multiple_of(jnp.minimum(place, 2) * cols, 128)
                start_copy(
                    back != last,
                    arrays[index].at[offset],
                    wbuf.at[slot, pl.ds(side * PIECE, PIECE), pl.ds(at, cols)],
                    wsem.at[slot, side, jnp.minimum(place, 2)],
                )

    for slot in range(min(depth - 1, tiles)):
        send(slot, slot)
    part = lambda place: cot.at[:, pl.ds(place * cols, cols)]
    start_copy(z >= 0, own, part(0), csem.at[0])
    start_copy(z == 0, dn2, part(1), csem.at[1])
    start_copy(z >= 1, up1, part(1), csem.at[1])
    start_copy(z <= 2, dn1, part(2), csem.at[2])
    start_copy(z == 3, up2, part(2), csem.at[2])
    keep = lax.broadcasted_iota(jnp.int32, (LIVE, 1), 0) < valid
    rows = (((1,), (1,)), ((), ()))
    for place in range(3):
        pltpu.make_async_copy(own, part(place), csem.at[place]).wait()
    for tile in range(tiles):
        slot = tile % depth
        if tile + depth - 1 < tiles:
            send(tile + depth - 1, (tile + depth - 1) % depth)
        for side in range(2):
            for place in range(3):
                target = wbuf.at[
                    slot, pl.ds(side * PIECE, PIECE), pl.ds(place * cols, cols)
                ]
                pltpu.make_async_copy(target, target, wsem.at[slot, side, place]).wait()
        total = lax.dot_general(cot[...], wbuf[slot], rows, preferred_element_type=jnp.float32)
        for side in range(2):
            start = pl.multiple_of(placed_piece(where[tile][side][0], y, half) * PIECE, PIECE)
            adapter = adapter_scale * lax.dot_general(
                low[...], chosen[pl.ds(start, PIECE), :], rows, preferred_element_type=jnp.float32
            )
            piece = total[:, side * PIECE : (side + 1) * PIECE]
            at = tile * TILE + side * PIECE
            out[:, at : at + PIECE] = jnp.where(keep, piece, 0.0) + adapter


def late_kernel(where, half, accumulated, *refs):
    meta, dn2, up2, dn3, up3 = refs[:5]
    sums = refs[5 : 5 + accumulated]
    arrays, (out, cot, wbuf, csem, wsem) = refs[5 + accumulated : -5], refs[-5:]
    z, p, y, valid = meta[0], meta[1], meta[2], meta[3]
    depth, tiles = wbuf.shape[0], len(where)
    block = jnp.bitwise_and(z - last_slot(z), 3)
    needed = jnp.bitwise_xor(block, p)

    def send(tile, slot):
        for side in range(2):
            for j in range(4):
                index, offset = where[tile][side][1][j]
                start_copy(
                    needed == j,
                    arrays[index].at[offset],
                    wbuf.at[slot, pl.ds(side * PIECE, PIECE)],
                    wsem.at[slot, side],
                )

    start_copy(z == 0, dn3, cot, csem)
    start_copy(z == 1, dn2, cot, csem)
    start_copy(z == 2, up2, cot, csem)
    start_copy(z == 3, up3, cot, csem)
    for slot in range(depth - 1):
        send(slot, slot)
    keep = lax.broadcasted_iota(jnp.int32, (LIVE, 1), 0) < valid
    out[LIVE:, :] = jnp.zeros((out.shape[0] - LIVE, out.shape[1]), out.dtype)
    pltpu.make_async_copy(cot, cot, csem).wait()
    for tile in range(tiles):
        slot = tile % depth
        if tile + depth - 1 < tiles:
            send(tile + depth - 1, (tile + depth - 1) % depth)
        for side in range(2):
            target = wbuf.at[slot, pl.ds(side * PIECE, PIECE)]
            pltpu.make_async_copy(target, target, wsem.at[slot, side]).wait()
        total = lax.dot_general(
            cot[...], wbuf[slot], (((1,), (1,)), ((), ())), preferred_element_type=jnp.float32
        )
        before = sums[where[tile][2]]
        for side in range(2):
            start = pl.multiple_of(placed_piece(where[tile][side][0], y, half) * PIECE, PIECE)
            piece = total[:, side * PIECE : (side + 1) * PIECE]
            at = where[tile][3] * TILE + side * PIECE
            result = before[:, at : at + PIECE] + jnp.where(keep, piece, 0.0)
            out[:LIVE, pl.ds(start, PIECE)] = result.astype(out.dtype)


def matmul_call(kernel, out_shape, operands, vmem_count, scratch):
    smem = pl.BlockSpec(memory_space=pltpu.SMEM)
    vmem = pl.BlockSpec(memory_space=pltpu.VMEM)
    hbm = pl.BlockSpec(memory_space=pltpu.HBM)
    first, last = vmem_count
    specs = [smem] + [
        vmem if first <= i < last else hbm for i in range(1, len(operands))
    ]
    return pl.pallas_call(
        kernel,
        out_shape=out_shape,
        in_specs=specs,
        out_specs=vmem,
        scratch_shapes=scratch,
        compiler_params=pltpu.CompilerParams(vmem_limit_bytes=44 * 2**20),
        cost_estimate=pl.CostEstimate(flops=0, transcendentals=0, bytes_accessed=0),
    )(*operands)


def early_call(meta, low, chosen, near, arrays, where, half):
    cols, depth = near[0].shape[1], 3
    return matmul_call(
        lambda *refs: early_kernel(where, half, *refs),
        jax.ShapeDtypeStruct((LIVE, len(where) * TILE), jnp.float32),
        (meta, low, chosen, *near, *arrays),
        (1, 3),
        [
            pltpu.VMEM((LIVE, 3 * cols), jnp.bfloat16),
            pltpu.VMEM((depth, TILE, 3 * cols), jnp.bfloat16),
            pltpu.SemaphoreType.DMA((3,)),
            pltpu.SemaphoreType.DMA((depth, 2, 3)),
        ],
    )


def late_call(meta, near, sums, arrays, where, half, seq_len):
    cols, depth = near[0].shape[1], 4
    return matmul_call(
        lambda *refs: late_kernel(where, half, len(sums), *refs),
        jax.ShapeDtypeStruct((seq_len, len(where) * TILE), jnp.bfloat16),
        (meta, *near, *sums, *arrays),
        (5, 5 + len(sums)),
        [
            pltpu.VMEM((LIVE, cols), jnp.bfloat16),
            pltpu.VMEM((depth, TILE, cols), jnp.bfloat16),
            pltpu.SemaphoreType.DMA,
            pltpu.SemaphoreType.DMA((depth, 2)),
        ],
    )


def gather_kernel(*refs):
    out, at = refs[-1], 0
    for ref in refs[:-1]:
        out[at : at + ref.shape[0]] = ref[...]
        at += ref.shape[0]


def gather_pieces(arrays):
    count = sum(array.shape[0] for array in arrays)
    shape = jax.ShapeDtypeStruct((count,) + arrays[0].shape[1:], arrays[0].dtype)
    return whole_call(gather_kernel, shape, *arrays)


def across(value):
    return lax.ppermute(value, "dp", [(i, i ^ 2) for i in range(4)])


def core(value):
    return lax.ppermute(value, "dp", [(i, i ^ 1) for i in range(4)])


def over(value):
    return lax.ppermute(value, "groups", [(0, 1), (1, 0)])


def line(value, step):
    def send(value, sign, far):
        pairs = [(i, i + 1) for i in range(far, 3)]
        return lax.ppermute(value, "fsdp", pairs if sign > 0 else [(3 - a, 3 - b) for a, b in pairs])

    return lambda sign: send(value, sign, step)


def turns(value):
    return [lax.ppermute(value, "fsdp", [(i, (i + k) % 4) for i in range(4)]) for k in (1, 2, 3)]


class Plan:
    def __init__(self, own, codes, scales, y):
        self.own, self.codes, self.scales = own, codes, scales.T
        self.pieces = codes.shape[0] // PIECE
        self.half = sum(SENT)
        self.group = y.astype(jnp.int32).reshape(1)
        self.up1, self.dn1 = line(own, 0)(1), line(own, 0)(-1)
        ranges = [(0, SENT[0]), (SENT[0], self.half), (2 * self.half, self.pieces)]
        self.mine, head, self.first, self.direct = weight_pieces(
            self.group, codes, self.scales, self.pieces, self.half, ranges
        )
        self.x0 = across(head)
        self.sibling = core(self.mine)

    def sum_parts(self, parts):
        self.x1 = across(self.first)
        self.y0 = over(self.x0)
        others = turns(after(parts, self.up1, self.dn1, self.x0, self.sibling))
        self.up2 = line(after(self.up1, *others), 1)(1)
        self.dn2 = line(after(self.dn1, *others), 1)(-1)
        return [parts] + others

    def gather_rows(self, row):
        pair = whole_call(
            pair_kernel, jax.ShapeDtypeStruct((2, row.shape[1]), row.dtype), row, core(row)
        )
        rows = across(pair)
        done = (self.x1, self.y0, self.up2, self.dn2, rows)
        self.y1 = over(after(self.x1, *done))
        self.x2 = across(after(self.direct, *done))
        self.up3 = line(after(self.up2, *done), 2)(1)
        self.dn3 = line(after(self.dn2, *done), 2)(-1)
        self.far1 = gather_pieces(after((self.x0, self.x1, self.y0), *done))
        self.sib_far1 = core(self.far1)
        return after([pair, rows], self.sib_far1)

    def finish(self, done, state_part, meta, low, chosen, seq_len):
        half, far, sib_far = self.half, self.far1, self.sib_far1
        near = [self.own, self.up1, self.dn1, self.up2, self.dn2]
        arrays = [self.mine, self.sibling, far, sib_far]

        early_count = half + SENT[0]
        far_at = {i: (2, i) for i in range(early_count)}
        far_at.update({early_count + i: (4, i) for i in range(2 * half - early_count)})
        far_at.update({2 * half + i: (6, i) for i in range(self.pieces - 2 * half)})

        def entry(i):
            index, offset = far_at[i]
            return (i, ((0, i), (1, i), (index, offset), (index + 1, offset)))

        tiles = [(entry(i), entry(i + 1)) for i in range(0, self.pieces, 2)]
        where1, where2 = tiles[: early_count // 2], tiles[early_count // 2 :]
        sum1 = early_call(after(meta, done), low, chosen, near, arrays, where1, half)
        sib_y1 = core(after(self.y1, sum1))
        sib_x2 = core(after(self.x2, sib_y1, self.up3, self.dn3))
        state_sum = state_part
        for other in turns(after(state_part, self.up3, self.dn3)):
            state_sum = state_sum + other
        arrays2 = arrays + [self.y1, sib_y1, self.x2, sib_x2]
        sum2 = early_call(meta, low, chosen, near, arrays2, where2, half)
        where = [pair + (0, t) for t, pair in enumerate(where1)]
        where += [pair + (1, t) for t, pair in enumerate(where2)]
        last = [self.dn2, self.up2, self.dn3, self.up3]
        result = late_call(meta, last, [sum1, sum2], arrays2, where, half, seq_len)
        return result, state_sum


def shards(
    hidden_in,
    cotangent,
    base_codes,
    base_scales,
    factor_a,
    factor_b,
    task_state,
    head_a,
    head_b,
    task_ids,
    valid_counts,
    owners,
):
    f32, bf16 = jnp.float32, jnp.bfloat16
    n_groups, n_fsdp, n_dp = (lax.axis_size(a) for a in ("groups", "fsdp", "dp"))
    z, p, y = (lax.axis_index(a) for a in ("fsdp", "dp", "groups"))
    seq_len, width_part = hidden_in.shape
    tasks_all, factor_cols = factor_a.shape
    rank_double = factor_cols // width_part
    rank_half = rank_double // 2
    joined_part = cotangent.shape[1]
    own = cotangent[:LIVE]
    lines = (n_groups, n_fsdp, n_dp) == (2, 4, 4) and width_part == 16 * PIECE
    plan = Plan(own, base_codes, base_scales, y) if lines else None

    task_rows = lax.broadcasted_iota(jnp.int32, (tasks_all, tasks_all), 0)
    task_other = lax.broadcasted_iota(jnp.int32, (tasks_all, tasks_all), 1)
    same_owner = owners[:, None] == owners[None, :]
    slot_index = jnp.sum((same_owner & (task_other < task_rows)).astype(jnp.int32), axis=1)
    target = owners * SLOTS + slot_index

    task = task_ids[0]
    chosen_a = lax.dynamic_slice_in_dim(factor_a, task, 1, 0).reshape(width_part, rank_double)
    chosen_b = lax.dynamic_slice_in_dim(factor_b, task, 1, 0).reshape(joined_part, rank_half)
    first_column = (z * joined_part).astype(jnp.int32).reshape(1)
    parts = whole_call(
        product_kernel,
        jax.ShapeDtypeStruct((LIVE, 2 * rank_double), bf16),
        hidden_in,
        cotangent,
        chosen_a,
        chosen_b,
        scalars=(first_column,),
    )
    if lines:
        kernel, parts = joined_factor_kernel, plan.sum_parts(parts)
    else:
        kernel, parts = factor_kernel, [lax.all_gather(parts, "fsdp", axis=0)]
    scalars = jnp.stack([first_column[0], valid_counts[0]])
    down_gradient, up_gradient, low_grad = whole_call(
        kernel,
        [
            jax.ShapeDtypeStruct((width_part, rank_double), f32),
            jax.ShapeDtypeStruct((joined_part, rank_half), f32),
            jax.ShapeDtypeStruct((LIVE, rank_double), bf16),
        ],
        hidden_in,
        cotangent,
        *parts,
        scalars=(scalars,),
    )
    down_cols = width_part * rank_double
    up_cols = joined_part * rank_half
    row = whole_call(
        row_kernel,
        jax.ShapeDtypeStruct((1, down_cols + up_cols + 128), bf16),
        down_gradient.astype(bf16).reshape(1, down_cols),
        up_gradient.astype(bf16).reshape(1, up_cols),
        jnp.full((1, 128), task, f32).astype(bf16),
    )
    rows = plan.gather_rows(row) if lines else [lax.all_gather(row, "dp", axis=0, tiled=True)]
    ids = jnp.concatenate([row[:, down_cols + up_cols] for row in rows]).astype(jnp.int32)
    one_hot = ids[:, None] == lax.broadcasted_iota(jnp.int32, (1, tasks_all), 1)
    states = jnp.dot(one_hot.astype(bf16), task_state, preferred_element_type=f32).astype(bf16)
    block = math.gcd(down_cols, up_cols)
    grad_head_b, part_b = head_grads(states, rows, head_b, down_cols, block)
    if lines:
        rows = after(rows, grad_head_b)
    grad_head_a, part_a = head_grads(states, rows, head_a, 0, block)
    state_part = part_a + part_b
    seq_target = jnp.sum(jnp.where(one_hot, target[None, :], 0), axis=1)
    own_rows = z * SLOTS + lax.broadcasted_iota(jnp.int32, (SLOTS, 1), 0)
    selector = (own_rows == seq_target[None, :]).astype(f32)
    if lines:
        done = (grad_head_a, grad_head_b, selector)
        meta = jnp.stack([z, p, y, valid_counts[0]]).astype(jnp.int32)
        input_gradient, state_sum = plan.finish(
            done, state_part, meta, low_grad, chosen_a, seq_len
        )
    else:
        state_sum = jnp.sum(lax.all_gather(state_part, "fsdp", axis=0), axis=0)
    grad_state = jnp.sum(selector[:, :, None] * state_sum[None, :, :], axis=1)

    if not lines:
        weight = dequantize(
            lax.all_gather(base_codes, "dp", axis=1, tiled=True),
            lax.all_gather(base_scales, "dp", axis=1, tiled=True),
        )
        merged = lax.dot_general(
            lax.all_gather(own, "fsdp", axis=1, tiled=True),
            weight,
            (((1,), (1,)), ((), ())),
            preferred_element_type=f32,
        )
        adapter = lax.dot_general(
            low_grad, chosen_a, (((1,), (1,)), ((), ())), preferred_element_type=f32
        )
        keep = lax.broadcasted_iota(jnp.int32, (LIVE, 1), 0) < valid_counts[0]
        live = (jnp.where(keep, merged, 0.0) + adapter_scale * adapter).astype(bf16)
        input_gradient = jnp.pad(live, ((0, seq_len - LIVE), (0, 0)))
    return (input_gradient, grad_head_a, grad_head_b, grad_state)


def solution(mesh):
    placed = (
        P(("groups", "dp"), "fsdp"),
        P(("groups", "dp"), "fsdp"),
        P("fsdp", "dp"),
        P("fsdp", "dp"),
        P("groups", "fsdp"),
        P("groups", "fsdp"),
        P("groups", "dp"),
        P("dp", "fsdp"),
        P("dp", "fsdp"),
        P(("groups", "dp")),
        P(("groups", "dp")),
        P("groups"),
    )
    return jax.shard_map(
        shards,
        mesh=mesh,
        in_specs=placed,
        out_specs=(
            P(("groups", "dp"), "fsdp"),
            P(("groups", "dp"), "fsdp"),
            P(("groups", "dp"), "fsdp"),
            P(("groups", "fsdp"), "dp"),
        ),
        check_vma=False,
    )
```

time: 235 us -> 225 us (0.957)
  Pallas kernels: 52.3 us -> 90.5 us
  waiting for transfers between devices: 101 us -> 75.5 us
  local copies, waits for them, and re-layouts: 38 us -> 21.2 us
  other arithmetic: 5.97 us -> 1.47 us
    pallas_call x3 -> x4, Pallas kernels: 28.8 us -> 63.4 us  [the longest x3 47.1 us: matmul_call(): pl.pallas_call(kernel, out_shape=out_shape, in_specs=specs, out_specs=vme...]
    ppermute x5 -> x4, waiting for transfers between devices: 51.2 us -> 24 us  [across(): return lax.ppermute(value, 'dp', [(i, i ^ 2) for i in range(4)])]
    ppermute x6, waiting for transfers between devices: 13.3 us -> 38.4 us  [send(): lax.ppermute(value, 'fsdp', pairs if sign > 0 else [(3 - a, 3 - b) for a,...]
    ppermute x3 -> x2, waiting for transfers between devices: 22.5 us -> 0.01 us  [over(): return lax.ppermute(value, 'groups', [(0, 1), (1, 0)])]
    unnamed x70 -> x34, local copies, waits for them, and re-layouts: 31.3 us -> 15.3 us
    ppermute x6 -> x5, waiting for transfers between devices: 10.8 us -> 5.19 us  [core(): return lax.ppermute(value, 'dp', [(i, i ^ 1) for i in range(4)])]
    ppermute x6, waiting for transfers between devices: 3.37 us -> 7.96 us  [turns(): lax.ppermute(value, 'fsdp', [(i, (i + k) % 4) for i in range(4)])]
    pallas_call x3 -> x5, Pallas kernels: 5.48 us -> 9.21 us  [whole_call(): pl.pallas_call(kernel, out_shape=out_shape, in_specs=[pl.BlockSpec(memory...]
  transfers between devices with their start and end apart: 26 -> 23, of which waited for: 8 -> 11; matrix products, arithmetic and copies ran while one was open for 4% -> 3% of each run, Pallas kernels for 11% -> 17%
where the time goes in v4:
time: 225 us; the launch traced here: 224 us
  Pallas kernels  90.5 us (40%)
  waiting for transfers between devices  75.5 us (34%)
  starting transfers between devices  32.6 us (14%)
  local copies, waits for them, and re-layouts  21.2 us (9%)
  between operations  2.4 us (1%)
    pallas_call x3, Pallas kernels, matmul_call(): pl.pallas_call(kernel, out_shape=out_shape, in_specs=specs, out_specs=vme...  47.1 us
    ppermute x6, waiting for transfers between devices, send(): lax.ppermute(value, 'fsdp', pairs if sign > 0 else [(3 - a, 3 - b) for a,...  38.4 us
    ppermute x4, waiting for transfers between devices, across(): return lax.ppermute(value, 'dp', [(i, i ^ 2) for i in range(4)])  24 us
    pallas_call x2, Pallas kernels, head_grads(): pl.pallas_call(head_kernel, out_shape=[jax.ShapeDtypeStruct((hidden_units...  17.9 us
    pallas_call x1, Pallas kernels, weight_pieces(): pl.pallas_call(lambda *refs: weight_kernel(ranges, *refs), out_shape=[jax...  16.3 us
    unnamed x34, local copies, waits for them, and re-layouts  15.3 us
    ppermute x6, starting transfers between devices, send(): lax.ppermute(value, 'fsdp', pairs if sign > 0 else [(3 - a, 3 - b) for a,...  12.4 us
    ppermute x6, starting transfers between devices, turns(): lax.ppermute(value, 'fsdp', [(i, (i + k) % 4) for i in range(4)])  10.4 us
  transfers between devices with their start and end apart: 23, of which 11 were waited for; matrix products, arithmetic and copies ran while one was open for 3% of the time, Pallas kernels for 17%

profile of v4, /device:TPU:0, one launch (start us, length us, event | category | flops | bytes accessed | tf_op | source)
XLA Modules:
  0.0 223.8 jit_solution(14311589604015162628)
XLA Ops:
  1.7 16.3 %shard_map.148 = (bf16[16,128,2304]{2,1,0:T(8,128)(2,1)}, bf16[3,128,2304]{2,1,0:T(8,128)(2,1)}, bf16[3,128,2304]{2,1,0:T(8,128)(2,1)}, bf16[4,128,2304]{2,1,0:T(8,128)(2,1)}) custom-call(s32[1]{0:T(128)} %bitcast.2.refs_0_, bf16[2048,2304]{1,0:T(8,128)(2,1)} %refs_1_.1, bf16[36,2048]{1,0:T(8,128)(2,1)S(1)} %bitcast.11), custom_call_target="tpu_custom_call" | custom-call | tf_op jit(solution)/shard_map/pallas_call | solution.py:69
  19.7 5.7 %collective-permute-start.1 = (bf16[384,2304]{1,0:T(8,128)(2,1)}, bf16[384,2304]{1,0:T(8,128)(2,1)}, u32[]{:S(2)}, u32[]{:S(2)}) collective-permute-start(bf16[384,2304]{1,0:T(8,128)(2,1)} %slice.9.refs_3_), channel_id=1, source_target_pairs={{0,4},{4,8},{8,12},{1,5},{5,9},{9,13},{2,6},{6,10},{10,14},{3,7},{... | collective-permute-start | bytes 5308424 | tf_op jit(solution)/shard_map/ppermute | solution.py:405
  26.8 1.6 collective-permute-start.2
  30.9 1.5 reshape.76.chosen_b
  32.5 1.6 copy-done.3
  36.4 26.7 %collective-permute-done.1.refs_4_ = bf16[384,2304]{1,0:T(8,128)(2,1)} collective-permute-done((bf16[384,2304]{1,0:T(8,128)(2,1)}, bf16[384,2304]{1,0:T(8,128)(2,1)}, u32[]{:S(2)}, u32[]{:S(2)}) %collective-permute-start.1) | collective-permute-done | bytes 1769504 | tf_op jit(solution)/shard_map/ppermute | solution.py:405
  63.0 5.4 %collective-permute-done.refs_5_ = bf16[384,2304]{1,0:T(8,128)(2,1)} collective-permute-done((bf16[384,2304]{1,0:T(8,128)(2,1)}, bf16[384,2304]{1,0:T(8,128)(2,1)}, u32[]{:S(2)}, u32[]{:S(2)}) %collective-permute-start) | collective-permute-done | bytes 1769504 | tf_op jit(solution)/shard_map/ppermute | solution.py:405
  68.4 3.8 %collective-permute-start.6 = (bf16[384,32]{1,0:T(8,128)(2,1)S(1)}, bf16[384,32]{1,0:T(8,128)(2,1)S(1)}, u32[]{:S(2)}, u32[]{:S(2)}) collective-permute-start(bf16[384,32]{1,0:T(8,128)(2,1)S(1)} %shard_map.147.refs_0_), channel_id=1, source_target_pairs={{0,12},{4,0},{8,4},{12,8},{1,13},{5,1},{9,5},{13,9},{2,14},{6,2},{... | collective-permute-start | bytes 73736 | tf_op jit(solution)/shard_map/ppermute | solution.py:411
  72.8 1.5 collective-permute-start.9
  74.3 1.5 collective-permute-start.10
  75.8 4.8 %collective-permute-done.5.refs_2_ = bf16[384,32]{1,0:T(8,128)(2,1)S(1)} collective-permute-done((bf16[384,32]{1,0:T(8,128)(2,1)S(1)}, bf16[384,32]{1,0:T(8,128)(2,1)S(1)}, u32[]{:S(2)}, u32[]{:S(2)}) %collective-permute-start.5) | collective-permute-done | bytes 24608 | tf_op jit(solution)/shard_map/ppermute | solution.py:411
  81.9 1.9 collective-permute-start.8
  84.5 1.6 copy-done.4
  86.1 2.7 %shard_map.149 = (f32[2048,16]{1,0:T(8,128)S(1)}, f32[2304,8]{1,0:T(8,128)S(1)}, bf16[384,16]{1,0:T(8,128)(2,1)S(1)}) custom-call(s32[2]{0:T(128)S(1)} %pad_add_fusion.1.scalars, bf16[512,2048]{1,0:T(8,128)(2,1)S(1)} %copy-done.4, bf16[512,2304]{1,0:T(8,128)(2,1)S(1)} %copy-done.2, bf16[384,32]{1,0:T(8,128)(2,1)S(1)} %shard_map.147.refs_0_, ...), custom_call_target="tpu_custom_call" | custom-call | tf_op jit(solution)/shard_map/pallas_call | solution.py:198
  93.3 1.6 collective-permute-start.12
  94.9 19.5 %collective-permute-done.9.refs_1_ = bf16[3,128,2304]{2,1,0:T(8,128)(2,1)} collective-permute-done((bf16[3,128,2304]{2,1,0:T(8,128)(2,1)}, bf16[3,128,2304]{2,1,0:T(8,128)(2,1)}, u32[]{:S(2)}, u32[]{:S(2)}) %collective-permute-start.9) | collective-permute-done | bytes 1769504 | tf_op jit(solution)/shard_map/ppermute | solution.py:391
  114.3 2.1 collective-permute-done.12.refs_1_
  116.4 6.3 %collective-permute-done.7.refs_7_.refs_1_ = bf16[384,2304]{1,0:T(8,128)(2,1)} collective-permute-done((bf16[384,2304]{1,0:T(8,128)(2,1)}, bf16[384,2304]{1,0:T(8,128)(2,1)}, u32[]{:S(2)}, u32[]{:S(2)}) %collective-permute-start.7) | collective-permute-done | bytes 1769504 | tf_op jit(solution)/shard_map/ppermute | solution.py:405
  122.7 5.2 %shard_map.152.refs_10_.refs_9_ = bf16[9,128,2304]{2,1,0:T(8,128)(2,1)} custom-call(bf16[3,128,2304]{2,1,0:T(8,128)(2,1)} %collective-permute-done.2.refs_0_, bf16[3,128,2304]{2,1,0:T(8,128)(2,1)} %collective-permute-done.9.refs_1_, bf16[3,128,2304]{2,1,0:T(8,128)(2,1)} %collective-permute-done.10.refs_2_), custom_call_target="tpu_custom_call" | custom-call | tf_op jit(solution)/shard_map/pallas_call | solution.py:198
  127.9 1.5 collective-permute-start.16
  133.3 3.7 %collective-permute-done.15.refs_11_.refs_10_ = bf16[9,128,2304]{2,1,0:T(8,128)(2,1)} collective-permute-done((bf16[9,128,2304]{2,1,0:T(8,128)(2,1)}, bf16[9,128,2304]{2,1,0:T(8,128)(2,1)}, u32[]{:S(2)}, u32[]{:S(2)}) %collective-permute-start.15) | collective-permute-done | bytes 5308448 | tf_op jit(solution)/shard_map/ppermute | solution.py:395
  137.4 2.3 %copy-done.6 = bf16[128,18432]{1,0:T(8,128)(2,1)S(1)} copy-done((bf16[128,18432]{1,0:T(8,128)(2,1)S(1)}, bf16[128,18432]{1,0:T(8,128)(2,1)}, u32[]{:S(2)}) %copy-start.6) | copy-done | bytes 4718616
  139.8 6.7 %shard_map.153 = (f32[128,18432]{1,0:T(8,128)}, f32[4,128]{1,0:T(4,128)S(1)}) custom-call(bf16[4,128]{1,0:T(4,128)(2,1)S(1)} %convolution_convert_fusion.states, bf16[2,51328]{1,0:T(2,128)(2,1)S(1)} %shard_map.151.refs_0_, bf16[2,51328]{1,0:T(2,128)(2,1)S(1)} %collective-permute-done.12.refs_1_, bf16[128,18432]{1,0:T(8,128)(2,1)S(1)} %copy-done.6), custom_call_target="tpu_custom_call" | custom-call | tf_op jit(solution)/shard_map/pallas_call | solution.py:175
  146.4 3.4 %copy-done.5 = bf16[128,32768]{1,0:T(8,128)(2,1)S(1)} copy-done((bf16[128,32768]{1,0:T(8,128)(2,1)S(1)}, bf16[128,32768]{1,0:T(8,128)(2,1)}, u32[]{:S(2)}) %copy-start.5) | copy-done | bytes 8388632
  149.8 11.3 %shard_map.154 = (f32[128,32768]{1,0:T(8,128)}, f32[4,128]{1,0:T(4,128)S(1)}) custom-call(bf16[4,128]{1,0:T(4,128)(2,1)S(1)} %convolution_convert_fusion.states, bf16[2,51328]{1,0:T(2,128)(2,1)S(1)} %shard_map.151.refs_0_, bf16[2,51328]{1,0:T(2,128)(2,1)S(1)} %collective-permute-done.12.refs_1_, bf16[128,32768]{1,0:T(8,128)(2,1)S(1)} %copy-done.5), custom_call_target="tpu_custom_call" | custom-call | tf_op jit(solution)/shard_map/pallas_call | solution.py:175
  161.1 17.0 %shard_map.155.refs_5_ = f32[384,1024]{1,0:T(8,128)S(1)} custom-call(s32[4]{0:T(128)S(1)} %pad_add_fusion.refs_0_, bf16[384,16]{1,0:T(8,128)(2,1)S(1)} %get-tuple-element.53.refs_1_, bf16[2048,16]{1,0:T(8,128)(2,1)S(1)} %reshape.75.chosen_a.refs_2_, bf16[384,2304]{1,0:T(8,128)(2,1)} %slice.9.refs_3_, bf16[384,2304]{1,0:T(8,128)(2,1)} %collective-permute-done.1.refs_4_, ...), custom_call_target="tpu_custom_call" | custom-call | tf_op jit(solution)/shard_map/pallas_call | solution.py:334
  180.7 2.4 %collective-permute-done.18.refs_14_.refs_13_ = bf16[4,128,2304]{2,1,0:T(8,128)(2,1)} collective-permute-done((bf16[4,128,2304]{2,1,0:T(8,128)(2,1)}, bf16[4,128,2304]{2,1,0:T(8,128)(2,1)}, u32[]{:S(2)}, u32[]{:S(2)}) %collective-permute-start.18) | collective-permute-done | bytes 2359328 | tf_op jit(solution)/shard_map/ppermute | solution.py:391
  183.4 3.7 %collective-permute-start.22 = (f32[4,128]{1,0:T(4,128)S(1)}, f32[4,128]{1,0:T(4,128)S(1)}, u32[]{:S(2)}, u32[]{:S(2)}) collective-permute-start(f32[4,128]{1,0:T(4,128)S(1)} %add.34), channel_id=1, source_target_pairs={{0,12},{4,0},{8,4},{12,8},{1,13},{5,1},{9,5},{13,9},{2,14},{6,2},{... | collective-permute-start | bytes 6152 | tf_op jit(solution)/shard_map/ppermute | solution.py:411
  187.5 1.9 collective-permute-start.20
  189.7 1.9 collective-permute-done.21
  193.5 17.3 %shard_map.156.refs_6_ = f32[384,1024]{1,0:T(8,128)S(1)} custom-call(s32[4]{0:T(128)S(1)} %pad_add_fusion.refs_0_, bf16[384,16]{1,0:T(8,128)(2,1)S(1)} %get-tuple-element.53.refs_1_, bf16[2048,16]{1,0:T(8,128)(2,1)S(1)} %reshape.75.chosen_a.refs_2_, bf16[384,2304]{1,0:T(8,128)(2,1)} %slice.9.refs_3_, bf16[384,2304]{1,0:T(8,128)(2,1)} %collective-permute-done.1.refs_4_, ...), custom_call_target="tpu_custom_call" | custom-call | tf_op jit(solution)/shard_map/pallas_call | solution.py:334
  210.9 12.7 %shard_map.157 = bf16[512,2048]{1,0:T(8,128)(2,1)} custom-call(s32[4]{0:T(128)S(1)} %pad_add_fusion.refs_0_, bf16[384,2304]{1,0:T(8,128)(2,1)} %collective-permute-done.7.refs_7_.refs_1_, bf16[384,2304]{1,0:T(8,128)(2,1)} %collective-permute-done.8.refs_6_.refs_2_, bf16[384,2304]{1,0:T(8,128)(2,1)S(1)} %copy-done.9, bf16[384,2304]{1,0:T(8,128)(2,1)S(1)} %copy-done.11, ...), custom_call_target="tpu_custom_call" | custom-call | tf_op jit(solution)/shard_map/pallas_call | solution.py:334
  (82 shorter events, 24.3 us)
Async XLA Ops:
  0.6 28.3 %copy-start = (bf16[16,32768]{1,0:T(8,128)(2,1)S(1)}, bf16[16,32768]{1,0:T(8,128)(2,1)}, u32[]{:S(2)}) copy-start(bf16[16,32768]{1,0:T(8,128)(2,1)} %param.16) | copy-start | bytes 3145732
  1.7 16.7 %copy-start.2 = (bf16[512,2304]{1,0:T(8,128)(2,1)S(1)}, bf16[512,2304]{1,0:T(8,128)(2,1)}, u32[]{:S(2)}) copy-start(bf16[512,2304]{1,0:T(8,128)(2,1)} %cotangent.3) | copy-start | bytes 7077892
  17.9 50.5 %collective-permute-start.3 = (bf16[16,128,2304]{2,1,0:T(8,128)(2,1)}, bf16[16,128,2304]{2,1,0:T(8,128)(2,1)}, u32[]{:S(2)}, u32[]{:S(2)}) collective-permute-start(bf16[16,128,2304]{2,1,0:T(8,128)(2,1)} %get-tuple-element.34.refs_8_.refs_7_), channel_id=1, source_target_pairs={{0,1},{1,0},{2,3},{3,2},{4,5},{5,4},{6,7},{7,6},{8,9},{9,8},{10,11... | collective-permute-start | bytes 28311560 | tf_op jit(solution)/shard_map/ppermute | solution.py:395
  19.7 43.3 %collective-permute-start.1 = (bf16[384,2304]{1,0:T(8,128)(2,1)}, bf16[384,2304]{1,0:T(8,128)(2,1)}, u32[]{:S(2)}, u32[]{:S(2)}) collective-permute-start(bf16[384,2304]{1,0:T(8,128)(2,1)} %slice.9.refs_3_), channel_id=1, source_target_pairs={{0,4},{4,8},{8,12},{1,5},{5,9},{9,13},{2,6},{6,10},{10,14},{3,7},{... | collective-permute-start | bytes 5308424 | tf_op jit(solution)/shard_map/ppermute | solution.py:405
  25.5 42.9 %collective-permute-start = (bf16[384,2304]{1,0:T(8,128)(2,1)}, bf16[384,2304]{1,0:T(8,128)(2,1)}, u32[]{:S(2)}, u32[]{:S(2)}) collective-permute-start(bf16[384,2304]{1,0:T(8,128)(2,1)} %slice.9.refs_3_), channel_id=1, source_target_pairs={{12,8},{8,4},{4,0},{13,9},{9,5},{5,1},{14,10},{10,6},{6,2},{15,11}... | collective-permute-start | bytes 5308424 | tf_op jit(solution)/shard_map/ppermute | solution.py:405
  26.8 41.7 %collective-permute-start.2 = (bf16[3,128,2304]{2,1,0:T(8,128)(2,1)}, bf16[3,128,2304]{2,1,0:T(8,128)(2,1)}, u32[]{:S(2)}, u32[]{:S(2)}) collective-permute-start(bf16[3,128,2304]{2,1,0:T(8,128)(2,1)} %get-tuple-element.33), channel_id=1, source_target_pairs={{0,2},{1,3},{2,0},{3,1},{4,6},{5,7},{6,4},{7,5},{8,10},{9,11},{10,... | collective-permute-start | bytes 5308424 | tf_op jit(solution)/shard_map/ppermute | solution.py:391
  68.4 7.4 %collective-permute-start.6 = (bf16[384,32]{1,0:T(8,128)(2,1)S(1)}, bf16[384,32]{1,0:T(8,128)(2,1)S(1)}, u32[]{:S(2)}, u32[]{:S(2)}) collective-permute-start(bf16[384,32]{1,0:T(8,128)(2,1)S(1)} %shard_map.147.refs_0_), channel_id=1, source_target_pairs={{0,12},{4,0},{8,4},{12,8},{1,13},{5,1},{9,5},{13,9},{2,14},{6,2},{... | collective-permute-start | bytes 73736 | tf_op jit(solution)/shard_map/ppermute | solution.py:411
  72.2 8.4 %collective-permute-start.5 = (bf16[384,32]{1,0:T(8,128)(2,1)S(1)}, bf16[384,32]{1,0:T(8,128)(2,1)S(1)}, u32[]{:S(2)}, u32[]{:S(2)}) collective-permute-start(bf16[384,32]{1,0:T(8,128)(2,1)S(1)} %shard_map.147.refs_0_), channel_id=1, source_target_pairs={{0,8},{4,12},{8,0},{12,4},{1,9},{5,13},{9,1},{13,5},{2,10},{6,14},... | collective-permute-start | bytes 73736 | tf_op jit(solution)/shard_map/ppermute | solution.py:411
  72.2 8.4 %collective-permute-start.4 = (bf16[384,32]{1,0:T(8,128)(2,1)S(1)}, bf16[384,32]{1,0:T(8,128)(2,1)S(1)}, u32[]{:S(2)}, u32[]{:S(2)}) collective-permute-start(bf16[384,32]{1,0:T(8,128)(2,1)S(1)} %shard_map.147.refs_0_), channel_id=1, source_target_pairs={{0,4},{4,8},{8,12},{12,0},{1,5},{5,9},{9,13},{13,1},{2,6},{6,10},{... | collective-permute-start | bytes 73736 | tf_op jit(solution)/shard_map/ppermute | solution.py:411
  72.8 41.6 %collective-permute-start.9 = (bf16[3,128,2304]{2,1,0:T(8,128)(2,1)}, bf16[3,128,2304]{2,1,0:T(8,128)(2,1)}, u32[]{:S(2)}, u32[]{:S(2)}) collective-permute-start(bf16[3,128,2304]{2,1,0:T(8,128)(2,1)} %get-tuple-element.38), channel_id=1, source_target_pairs={{0,2},{1,3},{2,0},{3,1},{4,6},{5,7},{6,4},{7,5},{8,10},{9,11},{10,... | collective-permute-start | bytes 5308424 | tf_op jit(solution)/shard_map/ppermute | solution.py:391
  74.3 40.1 %collective-permute-start.10 = (bf16[3,128,2304]{2,1,0:T(8,128)(2,1)}, bf16[3,128,2304]{2,1,0:T(8,128)(2,1)}, u32[]{:S(2)}, u32[]{:S(2)}) collective-permute-start(bf16[3,128,2304]{2,1,0:T(8,128)(2,1)} %collective-permute-done.2.refs_0_), channel_id=1, source_target_pairs={{0,16},{16,0},{1,17},{17,1},{2,18},{18,2},{3,19},{19,3},{4,20},{20... | collective-permute-start | bytes 5308424 | tf_op jit(solution)/shard_map/ppermute | solution.py:399
  80.6 42.2 %collective-permute-start.7 = (bf16[384,2304]{1,0:T(8,128)(2,1)}, bf16[384,2304]{1,0:T(8,128)(2,1)}, u32[]{:S(2)}, u32[]{:S(2)}) collective-permute-start(bf16[384,2304]{1,0:T(8,128)(2,1)} %collective-permute-done.refs_5_), channel_id=1, source_target_pairs={{8,4},{4,0},{9,5},{5,1},{10,6},{6,2},{11,7},{7,3},{24,20},{20,16},... | collective-permute-start | bytes 5308424 | tf_op jit(solution)/shard_map/ppermute | solution.py:405
  81.9 40.9 %collective-permute-start.8 = (bf16[384,2304]{1,0:T(8,128)(2,1)}, bf16[384,2304]{1,0:T(8,128)(2,1)}, u32[]{:S(2)}, u32[]{:S(2)}) collective-permute-start(bf16[384,2304]{1,0:T(8,128)(2,1)} %collective-permute-done.1.refs_4_), channel_id=1, source_target_pairs={{4,8},{8,12},{5,9},{9,13},{6,10},{10,14},{7,11},{11,15},{20,24},{2... | collective-permute-start | bytes 5308424 | tf_op jit(solution)/shard_map/ppermute | solution.py:405
  91.7 1.5 collective-permute-start.11
  93.3 44.0 %copy-start.15 = (bf16[16,128]{1,0:T(8,128)(2,1)S(1)}, bf16[16,128]{1,0:T(8,128)(2,1)}, u32[]{:S(2)}) copy-start(bf16[16,128]{1,0:T(8,128)(2,1)} %param.18) | copy-start | bytes 12292
  93.3 23.1 %collective-permute-start.12 = (bf16[2,51328]{1,0:T(2,128)(2,1)S(1)}, bf16[2,51328]{1,0:T(2,128)(2,1)S(1)}, u32[]{:S(2)}, u32[]{:S(2)}) collective-permute-start(bf16[2,51328]{1,0:T(2,128)(2,1)S(1)} %shard_map.151.refs_0_), channel_id=1, source_target_pairs={{0,2},{1,3},{2,0},{3,1},{4,6},{5,7},{6,4},{7,5},{8,10},{9,11},{10,... | collective-permute-start | bytes 615944 | tf_op jit(solution)/shard_map/ppermute | solution.py:391
  127.9 9.1 %collective-permute-start.15 = (bf16[9,128,2304]{2,1,0:T(8,128)(2,1)}, bf16[9,128,2304]{2,1,0:T(8,128)(2,1)}, u32[]{:S(2)}, u32[]{:S(2)}) collective-permute-start(bf16[9,128,2304]{2,1,0:T(8,128)(2,1)} %shard_map.152.refs_10_.refs_9_), channel_id=1, source_target_pairs={{0,1},{1,0},{2,3},{3,2},{4,5},{5,4},{6,7},{7,6},{8,9},{9,8},{10,11... | collective-permute-start | bytes 15925256 | tf_op jit(solution)/shard_map/ppermute | solution.py:395
  127.9 50.2 %collective-permute-start.16 = (bf16[3,128,2304]{2,1,0:T(8,128)(2,1)}, bf16[3,128,2304]{2,1,0:T(8,128)(2,1)}, u32[]{:S(2)}, u32[]{:S(2)}) collective-permute-start(bf16[3,128,2304]{2,1,0:T(8,128)(2,1)} %collective-permute-done.9.refs_1_), channel_id=1, source_target_pairs={{0,16},{16,0},{1,17},{17,1},{2,18},{18,2},{3,19},{19,3},{4,20},{20... | collective-permute-start | bytes 5308424 | tf_op jit(solution)/shard_map/ppermute | solution.py:399
  129.5 53.7 %collective-permute-start.18 = (bf16[4,128,2304]{2,1,0:T(8,128)(2,1)}, bf16[4,128,2304]{2,1,0:T(8,128)(2,1)}, u32[]{:S(2)}, u32[]{:S(2)}) collective-permute-start(bf16[4,128,2304]{2,1,0:T(8,128)(2,1)} %get-tuple-element.57), channel_id=1, source_target_pairs={{0,2},{1,3},{2,0},{3,1},{4,6},{5,7},{6,4},{7,5},{8,10},{9,11},{10,... | collective-permute-start | bytes 7077896 | tf_op jit(solution)/shard_map/ppermute | solution.py:391
  131.0 47.2 %collective-permute-start.13 = (bf16[384,2304]{1,0:T(8,128)(2,1)}, bf16[384,2304]{1,0:T(8,128)(2,1)S(1)}, u32[]{:S(2)}, u32[]{:S(2)}) collective-permute-start(bf16[384,2304]{1,0:T(8,128)(2,1)} %collective-permute-done.7.refs_7_.refs_1_), channel_id=1, source_target_pairs={{4,0},{5,1},{6,2},{7,3},{20,16},{21,17},{22,18},{23,19}} | collective-permute-start | bytes 5308424 | tf_op jit(solution)/shard_map/ppermute | solution.py:405
  132.3 47.2 %collective-permute-start.14 = (bf16[384,2304]{1,0:T(8,128)(2,1)}, bf16[384,2304]{1,0:T(8,128)(2,1)S(1)}, u32[]{:S(2)}, u32[]{:S(2)}) collective-permute-start(bf16[384,2304]{1,0:T(8,128)(2,1)} %collective-permute-done.8.refs_6_.refs_2_), channel_id=1, source_target_pairs={{8,12},{9,13},{10,14},{11,15},{24,28},{25,29},{26,30},{27,31}} | collective-permute-start | bytes 5308424 | tf_op jit(solution)/shard_map/ppermute | solution.py:405
  137.4 2.3 %copy-start.6 = (bf16[128,18432]{1,0:T(8,128)(2,1)S(1)}, bf16[128,18432]{1,0:T(8,128)(2,1)}, u32[]{:S(2)}) copy-start(bf16[128,18432]{1,0:T(8,128)(2,1)} %refs_2_.2) | copy-start | bytes 14155780
  146.4 3.4 %copy-start.5 = (bf16[128,32768]{1,0:T(8,128)(2,1)S(1)}, bf16[128,32768]{1,0:T(8,128)(2,1)}, u32[]{:S(2)}) copy-start(bf16[128,32768]{1,0:T(8,128)(2,1)} %refs_2_.3) | copy-start | bytes 25165828
  161.1 22.1 %copy-start.16 = (s32[16]{0:T(128)S(1)}, s32[16]{0:T(128)}, u32[]{:S(2)}) copy-start(s32[16]{0:T(128)} %param.23) | copy-start | bytes 196
  178.2 5.0 %collective-permute-start.17 = (bf16[3,128,2304]{2,1,0:T(8,128)(2,1)}, bf16[3,128,2304]{2,1,0:T(8,128)(2,1)}, u32[]{:S(2)}, u32[]{:S(2)}) collective-permute-start(bf16[3,128,2304]{2,1,0:T(8,128)(2,1)} %collective-permute-done.16.refs_12_.refs_11_), channel_id=1, source_target_pairs={{0,1},{1,0},{2,3},{3,2},{4,5},{5,4},{6,7},{7,6},{8,9},{9,8},{10,11... | collective-permute-start | bytes 5308424 | tf_op jit(solution)/shard_map/ppermute | solution.py:395
  183.2 10.4 %collective-permute-start.19 = (bf16[4,128,2304]{2,1,0:T(8,128)(2,1)}, bf16[4,128,2304]{2,1,0:T(8,128)(2,1)}, u32[]{:S(2)}, u32[]{:S(2)}) collective-permute-start(bf16[4,128,2304]{2,1,0:T(8,128)(2,1)} %collective-permute-done.18.refs_14_.refs_13_), channel_id=1, source_target_pairs={{0,1},{1,0},{2,3},{3,2},{4,5},{5,4},{6,7},{7,6},{8,9},{9,8},{10,11... | collective-permute-start | bytes 7077896 | tf_op jit(solution)/shard_map/ppermute | solution.py:395
  183.4 6.3 %collective-permute-start.22 = (f32[4,128]{1,0:T(4,128)S(1)}, f32[4,128]{1,0:T(4,128)S(1)}, u32[]{:S(2)}, u32[]{:S(2)}) collective-permute-start(f32[4,128]{1,0:T(4,128)S(1)} %add.34), channel_id=1, source_target_pairs={{0,12},{4,0},{8,4},{12,8},{1,13},{5,1},{9,5},{13,9},{2,14},{6,2},{... | collective-permute-start | bytes 6152 | tf_op jit(solution)/shard_map/ppermute | solution.py:411
  187.1 4.5 %collective-permute-start.21 = (f32[4,128]{1,0:T(4,128)S(1)}, f32[4,128]{1,0:T(4,128)S(1)}, u32[]{:S(2)}, u32[]{:S(2)}) collective-permute-start(f32[4,128]{1,0:T(4,128)S(1)} %add.34), channel_id=1, source_target_pairs={{0,8},{4,12},{8,0},{12,4},{1,9},{5,13},{9,1},{13,5},{2,10},{6,14},... | collective-permute-start | bytes 6152 | tf_op jit(solution)/shard_map/ppermute | solution.py:411
  187.5 5.4 %collective-permute-start.20 = (f32[4,128]{1,0:T(4,128)S(1)}, f32[4,128]{1,0:T(4,128)S(1)}, u32[]{:S(2)}, u32[]{:S(2)}) collective-permute-start(f32[4,128]{1,0:T(4,128)S(1)} %add.34), channel_id=1, source_target_pairs={{0,4},{4,8},{8,12},{12,0},{1,5},{5,9},{9,13},{13,1},{2,6},{6,10},{... | collective-permute-start | bytes 6152 | tf_op jit(solution)/shard_map/ppermute | solution.py:411
  193.5 17.3 %copy-start.9 = (bf16[384,2304]{1,0:T(8,128)(2,1)S(1)}, bf16[384,2304]{1,0:T(8,128)(2,1)}, u32[]{:S(2)}) copy-start(bf16[384,2304]{1,0:T(8,128)(2,1)} %copy-done.8) | copy-start | bytes 5308420
  193.5 17.3 %copy-start.11 = (bf16[384,2304]{1,0:T(8,128)(2,1)S(1)}, bf16[384,2304]{1,0:T(8,128)(2,1)}, u32[]{:S(2)}) copy-start(bf16[384,2304]{1,0:T(8,128)(2,1)} %copy-done.10) | copy-start | bytes 5308420
  210.9 12.7 %copy-start.1 = (bf16[16,32768]{1,0:T(8,128)(2,1)S(1)}, bf16[16,32768]{1,0:T(8,128)(2,1)}, u32[]{:S(2)}) copy-start(bf16[16,32768]{1,0:T(8,128)(2,1)} %param.16) | copy-start | bytes 3145732
  (8 other events, 10.0 us)

commit v5 on v4

--- a/solution.py
+++ b/solution.py
@@ -33,7 +33,7 @@
     )
 
 
-def weight_kernel(ranges, group, codes, scales, out, *copies):
+def weight_kernel(spans, group, codes, scales, *outs):
     cols, blocks = codes.shape[1], scales.shape[0]
     spread = (
         lax.broadcasted_iota(jnp.int32, (blocks, cols), 1) // QBLOCK
@@ -43,13 +43,12 @@
         scales[...], spread, (((0,), (0,)), ((), ())), preferred_element_type=jnp.float32
     )
     piece = (codes[...].astype(jnp.float32) * wide).astype(jnp.bfloat16)
-    out[0] = piece
     i = pl.program_id(0)
-    for (low, high), copy in zip(ranges, copies):
+    for (low, high), out in zip(spans, outs):
 
         @pl.when((i >= low) & (i < high))
-        def _(copy=copy):
-            copy[0] = piece
+        def _(out=out):
+            out[0] = piece
 
 
 def placed_piece(at, group, half):
@@ -57,9 +56,9 @@
     return jnp.where(at < 2 * half, moved, at)
 
 
-def weight_pieces(group, codes, scales, count, half, ranges):
+def weight_pieces(group, codes, scales, count, half, spans, whole=True):
     cols, blocks = codes.shape[1], scales.shape[0]
-    spans = [(0, count)] + list(ranges)
+    spans = ([(0, count)] if whole else []) + spans
 
     def span_spec(low, high):
         return pl.BlockSpec(
@@ -67,7 +66,7 @@
         )
 
     return pl.pallas_call(
-        lambda *refs: weight_kernel(ranges, *refs),
+        lambda *refs: weight_kernel(spans, *refs),
         out_shape=[
             jax.ShapeDtypeStruct((high - low, PIECE, cols), jnp.bfloat16) for low, high in spans
         ],
@@ -128,29 +127,11 @@
     up[...] = adapter_scale * jnp.where(value, mixed[:, half:], mixed[:, :half])
 
 
-def joined_factor_kernel(scalars, hidden, cotangent, *refs):
-    parts, outs = refs[:-3], refs[-3:]
-    factor_kernel(scalars, hidden, cotangent, Stack(parts), *outs)
-
-
-class Stack:
-    def __init__(self, refs):
-        self.refs, self.shape = refs, (len(refs),) + refs[0].shape
-
-    def __getitem__(self, index):
-        return self.refs[index][...]
-
-
 def row_kernel(down, up, task, out):
     down_cols, up_cols = down.shape[1], up.shape[1]
     out[:, :down_cols] = down[...]
     out[:, down_cols : down_cols + up_cols] = up[...]
     out[:, down_cols + up_cols :] = task[...]
-
-
-def pair_kernel(first, second, out):
-    out[0:1, :] = first[...]
-    out[1:2, :] = second[...]
 
 
 def head_kernel(states, *refs):
@@ -275,51 +256,78 @@
             out[:, at : at + PIECE] = jnp.where(keep, piece, 0.0) + adapter
 
 
-def late_kernel(where, half, accumulated, *refs):
-    meta, dn2, up2, dn3, up3 = refs[:5]
-    sums = refs[5 : 5 + accumulated]
-    arrays, (out, cot, wbuf, csem, wsem) = refs[5 + accumulated : -5], refs[-5:]
+def late_kernel(where, half, early, *refs):
+    meta, own, up1, dn1, up2, dn2, up3, dn3, low, chosen, sums = refs[:11]
+    arrays, (out, cot, wbuf, csem, wsem) = refs[11:-5], refs[-5:]
     z, p, y, valid = meta[0], meta[1], meta[2], meta[3]
-    depth, tiles = wbuf.shape[0], len(where)
-    block = jnp.bitwise_and(z - last_slot(z), 3)
-    needed = jnp.bitwise_xor(block, p)
+    depth, cols, tiles = wbuf.shape[0], own.shape[1], len(where)
+    last = last_slot(z)
 
     def send(tile, slot):
         for side in range(2):
             for j in range(4):
                 index, offset = where[tile][side][1][j]
+                back = jnp.bitwise_and(z - jnp.bitwise_xor(p, j), 3)
+                place = order_of(back, last)
                 start_copy(
-                    needed == j,
+                    (back == last) if tile < early else (back >= 0),
                     arrays[index].at[offset],
-                    wbuf.at[slot, pl.ds(side * PIECE, PIECE)],
-                    wsem.at[slot, side],
+                    wbuf.at[
+                        slot,
+                        pl.ds(side * PIECE, PIECE),
+                        pl.ds(pl.multiple_of(place * cols, 128), cols),
+                    ],
+                    wsem.at[slot, side, place],
                 )
 
-    start_copy(z == 0, dn3, cot, csem)
-    start_copy(z == 1, dn2, cot, csem)
-    start_copy(z == 2, up2, cot, csem)
-    start_copy(z == 3, up3, cot, csem)
+    part = lambda place: cot.at[:, pl.ds(place * cols, cols)]
+    start_copy(z == 0, dn3, part(3), csem.at[3])
+    start_copy(z == 1, dn2, part(3), csem.at[3])
+    start_copy(z == 2, up2, part(3), csem.at[3])
+    start_copy(z == 3, up3, part(3), csem.at[3])
     for slot in range(depth - 1):
         send(slot, slot)
+    start_copy(z >= 0, own, part(0), csem.at[0])
+    start_copy(z == 0, dn2, part(1), csem.at[1])
+    start_copy(z >= 1, up1, part(1), csem.at[1])
+    start_copy(z <= 2, dn1, part(2), csem.at[2])
+    start_copy(z == 3, up2, part(2), csem.at[2])
     keep = lax.broadcasted_iota(jnp.int32, (LIVE, 1), 0) < valid
+    rows = (((1,), (1,)), ((), ()))
     out[LIVE:, :] = jnp.zeros((out.shape[0] - LIVE, out.shape[1]), out.dtype)
-    pltpu.make_async_copy(cot, cot, csem).wait()
+    pltpu.make_async_copy(part(3), part(3), csem.at[3]).wait()
     for tile in range(tiles):
         slot = tile % depth
         if tile + depth - 1 < tiles:
             send(tile + depth - 1, (tile + depth - 1) % depth)
+        if tile == early:
+            for place in range(3):
+                pltpu.make_async_copy(part(place), part(place), csem.at[place]).wait()
+        first = 3 if tile < early else 0
         for side in range(2):
-            target = wbuf.at[slot, pl.ds(side * PIECE, PIECE)]
-            pltpu.make_async_copy(target, target, wsem.at[slot, side]).wait()
+            for place in range(first, 4):
+                target = wbuf.at[slot, pl.ds(side * PIECE, PIECE), pl.ds(place * cols, cols)]
+                pltpu.make_async_copy(target, target, wsem.at[slot, side, place]).wait()
         total = lax.dot_general(
-            cot[...], wbuf[slot], (((1,), (1,)), ((), ())), preferred_element_type=jnp.float32
-        )
-        before = sums[where[tile][2]]
+            cot[:, first * cols :],
+            wbuf[slot, :, first * cols :],
+            rows,
+            preferred_element_type=jnp.float32,
+        )
         for side in range(2):
             start = pl.multiple_of(placed_piece(where[tile][side][0], y, half) * PIECE, PIECE)
+            at = tile * TILE + side * PIECE
+            if tile < early:
+                before = sums[:, at : at + PIECE]
+            else:
+                before = adapter_scale * lax.dot_general(
+                    low[...],
+                    chosen[pl.ds(start, PIECE), :],
+                    rows,
+                    preferred_element_type=jnp.float32,
+                )
             piece = total[:, side * PIECE : (side + 1) * PIECE]
-            at = where[tile][3] * TILE + side * PIECE
-            result = before[:, at : at + PIECE] + jnp.where(keep, piece, 0.0)
+            result = before + jnp.where(keep, piece, 0.0)
             out[:LIVE, pl.ds(start, PIECE)] = result.astype(out.dtype)
 
 
@@ -358,18 +366,18 @@
     )
 
 
-def late_call(meta, near, sums, arrays, where, half, seq_len):
-    cols, depth = near[0].shape[1], 4
+def late_call(meta, near, low, chosen, sums, arrays, where, half, early, seq_len):
+    cols, depth = near[0].shape[1], 3
     return matmul_call(
-        lambda *refs: late_kernel(where, half, len(sums), *refs),
+        lambda *refs: late_kernel(where, half, early, *refs),
         jax.ShapeDtypeStruct((seq_len, len(where) * TILE), jnp.bfloat16),
-        (meta, *near, *sums, *arrays),
-        (5, 5 + len(sums)),
+        (meta, *near, low, chosen, sums, *arrays),
+        (1 + len(near), 4 + len(near)),
         [
-            pltpu.VMEM((LIVE, cols), jnp.bfloat16),
-            pltpu.VMEM((depth, TILE, cols), jnp.bfloat16),
-            pltpu.SemaphoreType.DMA,
-            pltpu.SemaphoreType.DMA((depth, 2)),
+            pltpu.VMEM((LIVE, 4 * cols), jnp.bfloat16),
+            pltpu.VMEM((depth, TILE, 4 * cols), jnp.bfloat16),
+            pltpu.SemaphoreType.DMA((4,)),
+            pltpu.SemaphoreType.DMA((depth, 2, 4)),
         ],
     )
 
@@ -418,34 +426,35 @@
         self.half = sum(SENT)
         self.group = y.astype(jnp.int32).reshape(1)
         self.up1, self.dn1 = line(own, 0)(1), line(own, 0)(-1)
-        ranges = [(0, SENT[0]), (SENT[0], self.half), (2 * self.half, self.pieces)]
-        self.mine, head, self.first, self.direct = weight_pieces(
-            self.group, codes, self.scales, self.pieces, self.half, ranges
+        (head,) = weight_pieces(
+            self.group, codes, self.scales, SENT[0], self.half, [(0, SENT[0])], False
         )
         self.x0 = across(head)
-        self.sibling = core(self.mine)
 
     def sum_parts(self, parts):
-        self.x1 = across(self.first)
-        self.y0 = over(self.x0)
-        others = turns(after(parts, self.up1, self.dn1, self.x0, self.sibling))
-        self.up2 = line(after(self.up1, *others), 1)(1)
-        self.dn2 = line(after(self.dn1, *others), 1)(-1)
-        return [parts] + others
+        ranges = [(SENT[0], self.half), (2 * self.half, self.pieces)]
+        self.mine, first, self.direct = weight_pieces(
+            after(self.group, parts), self.codes, self.scales, self.pieces, self.half, ranges
+        )
+        gathered = lax.all_gather(after(parts, self.mine), "fsdp", axis=0)
+        ready = (gathered, self.x0, self.up1, self.dn1)
+        self.x1 = across(after(first, *ready))
+        self.y0 = over(after(self.x0, *ready))
+        self.up2 = line(after(self.up1, *ready), 1)(1)
+        self.dn2 = line(after(self.dn1, *ready), 1)(-1)
+        self.sibling = core(after(self.mine, *ready))
+        return [gathered]
 
     def gather_rows(self, row):
-        pair = whole_call(
-            pair_kernel, jax.ShapeDtypeStruct((2, row.shape[1]), row.dtype), row, core(row)
-        )
-        rows = across(pair)
-        done = (self.x1, self.y0, self.up2, self.dn2, rows)
+        rows = lax.all_gather(row, "dp", axis=0, tiled=True)
+        done = (self.x1, self.y0, self.up2, self.dn2, rows, self.sibling)
         self.y1 = over(after(self.x1, *done))
         self.x2 = across(after(self.direct, *done))
         self.up3 = line(after(self.up2, *done), 2)(1)
         self.dn3 = line(after(self.dn2, *done), 2)(-1)
         self.far1 = gather_pieces(after((self.x0, self.x1, self.y0), *done))
         self.sib_far1 = core(self.far1)
-        return after([pair, rows], self.sib_far1)
+        return after([rows], self.sib_far1)
 
     def finish(self, done, state_part, meta, low, chosen, seq_len):
         half, far, sib_far = self.half, self.far1, self.sib_far1
@@ -462,19 +471,17 @@
             return (i, ((0, i), (1, i), (index, offset), (index + 1, offset)))
 
         tiles = [(entry(i), entry(i + 1)) for i in range(0, self.pieces, 2)]
-        where1, where2 = tiles[: early_count // 2], tiles[early_count // 2 :]
-        sum1 = early_call(after(meta, done), low, chosen, near, arrays, where1, half)
+        early = early_count // 2
+        sum1 = early_call(after(meta, done), low, chosen, near, arrays, tiles[:early], half)
         sib_y1 = core(after(self.y1, sum1))
         sib_x2 = core(after(self.x2, sib_y1, self.up3, self.dn3))
+        others = turns(after(state_part, self.up3, self.dn3, sib_y1))
+        arrays += [self.y1, sib_y1, self.x2, sib_x2]
+        near += [self.up3, self.dn3]
+        result = late_call(meta, near, low, chosen, sum1, arrays, tiles, half, early, seq_len)
         state_sum = state_part
-        for other in turns(after(state_part, self.up3, self.dn3)):
-            state_sum = state_sum + other
-        arrays2 = arrays + [self.y1, sib_y1, self.x2, sib_x2]
-        sum2 = early_call(meta, low, chosen, near, arrays2, where2, half)
-        where = [pair + (0, t) for t, pair in enumerate(where1)]
-        where += [pair + (1, t) for t, pair in enumerate(where2)]
-        last = [self.dn2, self.up2, self.dn3, self.up3]
-        result = late_call(meta, last, [sum1, sum2], arrays2, where, half, seq_len)
+        for other in others:
+            state_sum = state_sum + after(other, result)
         return result, state_sum
 
 
@@ -524,12 +531,12 @@
         scalars=(first_column,),
     )
     if lines:
-        kernel, parts = joined_factor_kernel, plan.sum_parts(parts)
+        parts = plan.sum_parts(parts)
     else:
-        kernel, parts = factor_kernel, [lax.all_gather(parts, "fsdp", axis=0)]
+        parts = [lax.all_gather(parts, "fsdp", axis=0)]
     scalars = jnp.stack([first_column[0], valid_counts[0]])
     down_gradient, up_gradient, low_grad = whole_call(
-        kernel,
+        factor_kernel,
         [
             jax.ShapeDtypeStruct((width_part, rank_double), f32),
             jax.ShapeDtypeStruct((joined_part, rank_half), f32),

time: 225 us -> 209 us (0.929)
  waiting for transfers between devices: 75.5 us -> 8.8 us
  blocking collectives: 0 us -> 62.6 us
  starting transfers between devices: 32.6 us -> 24 us
  Pallas kernels: 90.5 us -> 87.4 us
    all_gather x0 -> x2, blocking collectives: none -> 62.6 us  [the longest x1 35.2 us: gather_rows(): rows = lax.all_gather(row, 'dp', axis=0, tiled=True)]
    ppermute x6, waiting for transfers between devices: 38.4 us -> 0.02 us  [send(): lax.ppermute(value, 'fsdp', pairs if sign > 0 else [(3 - a, 3 - b) for a,...]
    ppermute x4 -> x3, waiting for transfers between devices: 24 us -> 4.82 us  [across(): return lax.ppermute(value, 'dp', [(i, i ^ 2) for i in range(4)])]
    ppermute x6 -> x3, waiting for transfers between devices: 7.96 us -> 0.01 us  [turns(): lax.ppermute(value, 'fsdp', [(i, (i + k) % 4) for i in range(4)])]
    ppermute x6 -> x3, starting transfers between devices: 10.4 us -> 3.9 us  [turns(): lax.ppermute(value, 'fsdp', [(i, (i + k) % 4) for i in range(4)])]
    pallas_call x3 -> x2, Pallas kernels: 47.1 us -> 41.6 us  [matmul_call(): pl.pallas_call(kernel, out_shape=out_shape, in_specs=specs, out_specs=vme...]
    pallas_call x1 -> x2, Pallas kernels: 16.3 us -> 18.7 us  [weight_pieces(): pl.pallas_call(lambda *refs: weight_kernel(spans, *refs), out_shape=[jax....]
    ppermute x4 -> x3, starting transfers between devices: 6.1 us -> 4.07 us  [across(): return lax.ppermute(value, 'dp', [(i, i ^ 2) for i in range(4)])]
  transfers between devices with their start and end apart: 23 -> 18, of which waited for: 11 -> 3; matrix products, arithmetic and copies ran while one was open for 3% -> 3% of each run, Pallas kernels for 17% -> 38%
where the time goes in v5:
time: 209 us
  Pallas kernels  87.4 us (42%)
  blocking collectives  62.6 us (30%)
  starting transfers between devices  24 us (11%)
  local copies, waits for them, and re-layouts  21.8 us (10%)
  waiting for transfers between devices  8.8 us (4%)
  between operations  2.24 us (1%)
    pallas_call x2, Pallas kernels, matmul_call(): pl.pallas_call(kernel, out_shape=out_shape, in_specs=specs, out_specs=vme...  41.6 us
    all_gather x1, blocking collectives, gather_rows(): rows = lax.all_gather(row, 'dp', axis=0, tiled=True)  35.2 us
    all_gather x1, blocking collectives, sum_parts(): gathered = lax.all_gather(after(parts, self.mine), 'fsdp', axis=0)  27.4 us
    pallas_call x2, Pallas kernels, weight_pieces(): pl.pallas_call(lambda *refs: weight_kernel(spans, *refs), out_shape=[jax....  18.7 us
    pallas_call x2, Pallas kernels, head_grads(): pl.pallas_call(head_kernel, out_shape=[jax.ShapeDtypeStruct((hidden_units...  17.9 us
    unnamed x35, local copies, waits for them, and re-layouts  15.9 us
    ppermute x6, starting transfers between devices, send(): lax.ppermute(value, 'fsdp', pairs if sign > 0 else [(3 - a, 3 - b) for a,...  12.3 us
    pallas_call x4, Pallas kernels, whole_call(): pl.pallas_call(kernel, out_shape=out_shape, in_specs=[pl.BlockSpec(memory...  9.14 us
  transfers between devices with their start and end apart: 18, of which 3 were waited for; matrix products, arithmetic and copies ran while one was open for 3% of the time, Pallas kernels for 38%

profile of v5, /device:TPU:0, one launch (start us, length us, event | category | flops | bytes accessed | tf_op | source)
XLA Modules:
  0.0 208.5 jit_solution(6476513510510248142)
XLA Ops:
  0.7 3.8 %copy-done.2 = bf16[2048,2304]{1,0:T(8,128)(2,1)S(1)} copy-done((bf16[2048,2304]{1,0:T(8,128)(2,1)S(1)}, bf16[2048,2304]{1,0:T(8,128)(2,1)}, u32[]{:S(2)}) %copy-start.2) | copy-done | bytes 9437208
  5.3 2.4 %shard_map.149 = bf16[3,128,2304]{2,1,0:T(8,128)(2,1)} custom-call(s32[1]{0:T(128)} %bitcast.2.refs_0_, bf16[2048,2304]{1,0:T(8,128)(2,1)S(1)} %copy-done.2, bf16[36,2048]{1,0:T(8,128)(2,1)S(1)} %bitcast.21), custom_call_target="tpu_custom_call" | custom-call | tf_op jit(solution)/shard_map/pallas_call | solution.py:68
  7.8 2.9 %collective-permute-start.2 = (bf16[3,128,2304]{2,1,0:T(8,128)(2,1)}, bf16[3,128,2304]{2,1,0:T(8,128)(2,1)}, u32[]{:S(2)}, u32[]{:S(2)}) collective-permute-start(bf16[3,128,2304]{2,1,0:T(8,128)(2,1)} %shard_map.149), channel_id=1, source_target_pairs={{0,2},{1,3},{2,0},{3,1},{4,6},{5,7},{6,4},{7,5},{8,10},{9,11},{10,... | collective-permute-start | bytes 5308424 | tf_op jit(solution)/shard_map/ppermute | solution.py:399
  10.7 1.3 slice.6.refs_3_.refs_1_
  12.0 4.7 %collective-permute-start = (bf16[384,2304]{1,0:T(8,128)(2,1)}, bf16[384,2304]{1,0:T(8,128)(2,1)}, u32[]{:S(2)}, u32[]{:S(2)}) collective-permute-start(bf16[384,2304]{1,0:T(8,128)(2,1)} %slice.6.refs_3_.refs_1_), channel_id=1, source_target_pairs={{0,4},{4,8},{8,12},{1,5},{5,9},{9,13},{2,6},{6,10},{10,14},{3,7},{... | collective-permute-start | bytes 5308424 | tf_op jit(solution)/shard_map/ppermute | solution.py:413
  16.8 1.3 collective-permute-start.1
  19.5 1.4 dynamic-slice_reduce_fusion.1
  20.9 1.5 reshape.61.chosen_b
  22.4 1.6 copy-done.6
  24.0 1.1 copy-done.10
  25.0 1.2 shard_map.147
  26.3 16.3 %shard_map.148 = (bf16[16,128,2304]{2,1,0:T(8,128)(2,1)}, bf16[3,128,2304]{2,1,0:T(8,128)(2,1)}, bf16[4,128,2304]{2,1,0:T(8,128)(2,1)}) custom-call(s32[1]{0:T(128)} %bitcast.2.refs_0_, bf16[2048,2304]{1,0:T(8,128)(2,1)} %refs_1_.5, bf16[36,2048]{1,0:T(8,128)(2,1)S(1)} %bitcast.22), custom_call_target="tpu_custom_call" | custom-call | tf_op jit(solution)/shard_map/pallas_call | solution.py:68
  42.6 27.4 %all-gather = bf16[1536,32]{1,0:T(8,128)(2,1)S(1)} all-gather(bf16[384,32]{1,0:T(8,128)(2,1)S(1)} %shard_map.147), channel_id=2, replica_groups=mesh['groups'=2,'fsdp'=4,'dp'=4] {'fsdp'}, dimensions={0}, use_global_device_ids=true | all-gather | bytes 122880 | tf_op jit(solution)/shard_map/all_gather | solution.py:439
  70.7 1.3 collective-permute-start.4
  71.9 1.9 collective-permute-start.3
  73.8 1.5 collective-permute-start.6
  76.1 2.7 %shard_map.150 = (f32[2048,16]{1,0:T(8,128)S(1)}, f32[2304,8]{1,0:T(8,128)S(1)}, bf16[384,16]{1,0:T(8,128)(2,1)S(1)}) custom-call(s32[2]{0:T(128)S(1)} %pad_add_fusion.1.scalars, bf16[512,2048]{1,0:T(8,128)(2,1)S(1)} %copy-done.7, bf16[512,2304]{1,0:T(8,128)(2,1)S(1)} %copy-done.3, bf16[4,384,32]{2,1,0:T(8,128)(2,1)S(1)} %bitcast.19), custom_call_target="tpu_custom_call" | custom-call | tf_op jit(solution)/shard_map/pallas_call | solution.py:179
  81.4 35.2 %all-gather.1 = bf16[4,1,51328]{2,1,0:T(2,128)(2,1)S(1)} all-gather(bf16[1,1,51328]{2,1,0:T(2,128)(2,1)S(1)} %bitcast.20), channel_id=1, replica_groups=mesh['groups'=2,'fsdp'=4,'dp'=4] {'dp'}, dimensions={0}, use_global_device_ids=true | all-gather | bytes 513280 | tf_op jit(solution)/shard_map/all_gather | solution.py:449
  116.9 5.2 %shard_map.152.refs_10_.refs_13_ = bf16[9,128,2304]{2,1,0:T(8,128)(2,1)} custom-call(bf16[3,128,2304]{2,1,0:T(8,128)(2,1)} %collective-permute-done.2.refs_0_, bf16[3,128,2304]{2,1,0:T(8,128)(2,1)} %collective-permute-done.5.refs_1_, bf16[3,128,2304]{2,1,0:T(8,128)(2,1)} %collective-permute-done.6.refs_2_), custom_call_target="tpu_custom_call" | custom-call | tf_op jit(solution)/shard_map/pallas_call | solution.py:179
  122.4 1.5 collective-permute-start.11
  124.6 1.3 collective-permute-start.9
  125.8 1.9 collective-permute-start.8
  127.7 3.4 %collective-permute-done.10.refs_11_.refs_14_ = bf16[9,128,2304]{2,1,0:T(8,128)(2,1)} collective-permute-done((bf16[9,128,2304]{2,1,0:T(8,128)(2,1)}, bf16[9,128,2304]{2,1,0:T(8,128)(2,1)}, u32[]{:S(2)}, u32[]{:S(2)}) %collective-permute-start.10) | collective-permute-done | bytes 5308448 | tf_op jit(solution)/shard_map/ppermute | solution.py:403
  131.5 2.3 %copy-done.9 = bf16[128,18432]{1,0:T(8,128)(2,1)S(1)} copy-done((bf16[128,18432]{1,0:T(8,128)(2,1)S(1)}, bf16[128,18432]{1,0:T(8,128)(2,1)}, u32[]{:S(2)}) %copy-start.9) | copy-done | bytes 4718616
  133.8 6.7 %shard_map.153 = (f32[128,18432]{1,0:T(8,128)}, f32[4,128]{1,0:T(4,128)S(1)}) custom-call(bf16[4,128]{1,0:T(4,128)(2,1)S(1)} %convolution_convert_fusion.states, bf16[4,51328]{1,0:T(4,128)(2,1)S(1)} %bitcast.17, bf16[128,18432]{1,0:T(8,128)(2,1)S(1)} %copy-done.9), custom_call_target="tpu_custom_call" | custom-call | tf_op jit(solution)/shard_map/pallas_call | solution.py:156
  140.5 3.4 %copy-done.8 = bf16[128,32768]{1,0:T(8,128)(2,1)S(1)} copy-done((bf16[128,32768]{1,0:T(8,128)(2,1)S(1)}, bf16[128,32768]{1,0:T(8,128)(2,1)}, u32[]{:S(2)}) %copy-start.8) | copy-done | bytes 8388632
  143.9 11.3 %shard_map.154 = (f32[128,32768]{1,0:T(8,128)}, f32[4,128]{1,0:T(4,128)S(1)}) custom-call(bf16[4,128]{1,0:T(4,128)(2,1)S(1)} %convolution_convert_fusion.states, bf16[4,51328]{1,0:T(4,128)(2,1)S(1)} %bitcast.18, bf16[128,32768]{1,0:T(8,128)(2,1)S(1)} %copy-done.8), custom_call_target="tpu_custom_call" | custom-call | tf_op jit(solution)/shard_map/pallas_call | solution.py:156
  155.1 17.0 %shard_map.155.refs_10_ = f32[384,1024]{1,0:T(8,128)S(1)} custom-call(s32[4]{0:T(128)S(1)} %pad_add_fusion.refs_0_, bf16[384,16]{1,0:T(8,128)(2,1)S(1)} %get-tuple-element.50.refs_1_.refs_8_, bf16[2048,16]{1,0:T(8,128)(2,1)S(1)} %reshape.60.chosen_a.refs_2_.refs_9_, bf16[384,2304]{1,0:T(8,128)(2,1)} %slice.6.refs_3_.refs_1_, ...), custom_call_target="tpu_custom_call" | custom-call | tf_op jit(solution)/shard_map/pallas_call | solution.py:342
  172.5 4.8 %collective-permute-done.13.refs_17_ = bf16[4,128,2304]{2,1,0:T(8,128)(2,1)} collective-permute-done((bf16[4,128,2304]{2,1,0:T(8,128)(2,1)}, bf16[4,128,2304]{2,1,0:T(8,128)(2,1)}, u32[]{:S(2)}, u32[]{:S(2)}) %collective-permute-start.13) | collective-permute-done | bytes 2359328 | tf_op jit(solution)/shard_map/ppermute | solution.py:399
  177.7 1.5 collective-permute-start.15
  179.2 2.4 %collective-permute-start.17 = (f32[4,128]{1,0:T(4,128)S(1)}, f32[4,128]{1,0:T(4,128)S(1)}, u32[]{:S(2)}, u32[]{:S(2)}) collective-permute-start(f32[4,128]{1,0:T(4,128)S(1)} %add.34), channel_id=1, source_target_pairs={{0,12},{4,0},{8,4},{12,8},{1,13},{5,1},{9,5},{13,9},{2,14},{6,2},{... | collective-permute-start | bytes 6152 | tf_op jit(solution)/shard_map/ppermute | solution.py:419
  183.2 24.6 %shard_map.156 = bf16[512,2048]{1,0:T(8,128)(2,1)} custom-call(s32[4]{0:T(128)S(1)} %pad_add_fusion.refs_0_, bf16[384,2304]{1,0:T(8,128)(2,1)} %slice.6.refs_3_.refs_1_, bf16[384,2304]{1,0:T(8,128)(2,1)} %collective-permute-done.refs_4_.refs_2_, bf16[384,2304]{1,0:T(8,128)(2,1)} %collective-permute-done.1.refs_5_.refs_3_, ...), custom_call_target="tpu_custom_call" | custom-call | tf_op jit(solution)/shard_map/pallas_call | solution.py:342
  (73 shorter events, 9.6 us)
Async XLA Ops:
  0.6 18.1 %copy-start = (bf16[16,32768]{1,0:T(8,128)(2,1)S(1)}, bf16[16,32768]{1,0:T(8,128)(2,1)}, u32[]{:S(2)}) copy-start(bf16[16,32768]{1,0:T(8,128)(2,1)} %param.16) | copy-start | bytes 3145732
  0.7 3.8 %copy-start.2 = (bf16[2048,2304]{1,0:T(8,128)(2,1)S(1)}, bf16[2048,2304]{1,0:T(8,128)(2,1)}, u32[]{:S(2)}) copy-start(bf16[2048,2304]{1,0:T(8,128)(2,1)} %refs_1_.5) | copy-start | bytes 28311556
  5.3 5.4 %copy-start.3 = (bf16[512,2304]{1,0:T(8,128)(2,1)S(1)}, bf16[512,2304]{1,0:T(8,128)(2,1)}, u32[]{:S(2)}) copy-start(bf16[512,2304]{1,0:T(8,128)(2,1)} %cotangent.3) | copy-start | bytes 7077892
  7.8 62.2 %collective-permute-start.2 = (bf16[3,128,2304]{2,1,0:T(8,128)(2,1)}, bf16[3,128,2304]{2,1,0:T(8,128)(2,1)}, u32[]{:S(2)}, u32[]{:S(2)}) collective-permute-start(bf16[3,128,2304]{2,1,0:T(8,128)(2,1)} %shard_map.149), channel_id=1, source_target_pairs={{0,2},{1,3},{2,0},{3,1},{4,6},{5,7},{6,4},{7,5},{8,10},{9,11},{10,... | collective-permute-start | bytes 5308424 | tf_op jit(solution)/shard_map/ppermute | solution.py:399
  12.0 57.9 %collective-permute-start = (bf16[384,2304]{1,0:T(8,128)(2,1)}, bf16[384,2304]{1,0:T(8,128)(2,1)}, u32[]{:S(2)}, u32[]{:S(2)}) collective-permute-start(bf16[384,2304]{1,0:T(8,128)(2,1)} %slice.6.refs_3_.refs_1_), channel_id=1, source_target_pairs={{0,4},{4,8},{8,12},{1,5},{5,9},{9,13},{2,6},{6,10},{10,14},{3,7},{... | collective-permute-start | bytes 5308424 | tf_op jit(solution)/shard_map/ppermute | solution.py:413
  16.8 53.2 %collective-permute-start.1 = (bf16[384,2304]{1,0:T(8,128)(2,1)}, bf16[384,2304]{1,0:T(8,128)(2,1)}, u32[]{:S(2)}, u32[]{:S(2)}) collective-permute-start(bf16[384,2304]{1,0:T(8,128)(2,1)} %slice.6.refs_3_.refs_1_), channel_id=1, source_target_pairs={{12,8},{8,4},{4,0},{13,9},{9,5},{5,1},{14,10},{10,6},{6,2},{15,11}... | collective-permute-start | bytes 5308424 | tf_op jit(solution)/shard_map/ppermute | solution.py:413
  19.5 135.6 %copy-start.4 = (bf16[2048,16]{1,0:T(8,128)(2,1)}, bf16[2048,16]{1,0:T(8,128)(2,1)S(1)}, u32[]{:S(2)}) copy-start(bf16[2048,16]{1,0:T(8,128)(2,1)S(1)} %reshape.60.chosen_a.refs_2_.refs_9_) | copy-start | bytes 196612
  22.4 1.6 copy-start.6
  24.0 1.1 copy-start.10
  25.0 1.3 copy-start.14
  26.3 49.8 %copy-start.7 = (bf16[512,2048]{1,0:T(8,128)(2,1)S(1)}, bf16[512,2048]{1,0:T(8,128)(2,1)}, u32[]{:S(2)}) copy-start(bf16[512,2048]{1,0:T(8,128)(2,1)} %hidden.3) | copy-start | bytes 6291460
  70.0 46.9 %collective-permute-start.7 = (bf16[16,128,2304]{2,1,0:T(8,128)(2,1)}, bf16[16,128,2304]{2,1,0:T(8,128)(2,1)}, u32[]{:S(2)}, u32[]{:S(2)}) collective-permute-start(bf16[16,128,2304]{2,1,0:T(8,128)(2,1)} %get-tuple-element.47.refs_8_.refs_11_), channel_id=1, source_target_pairs={{0,1},{1,0},{2,3},{3,2},{4,5},{5,4},{6,7},{7,6},{8,9},{9,8},{10,11... | collective-permute-start | bytes 28311560 | tf_op jit(solution)/shard_map/ppermute | solution.py:403
  70.1 46.7 %collective-permute-start.5 = (bf16[3,128,2304]{2,1,0:T(8,128)(2,1)}, bf16[3,128,2304]{2,1,0:T(8,128)(2,1)}, u32[]{:S(2)}, u32[]{:S(2)}) collective-permute-start(bf16[3,128,2304]{2,1,0:T(8,128)(2,1)} %get-tuple-element.43), channel_id=1, source_target_pairs={{0,2},{1,3},{2,0},{3,1},{4,6},{5,7},{6,4},{7,5},{8,10},{9,11},{10,... | collective-permute-start | bytes 5308424 | tf_op jit(solution)/shard_map/ppermute | solution.py:399
  70.7 46.1 %collective-permute-start.4 = (bf16[384,2304]{1,0:T(8,128)(2,1)}, bf16[384,2304]{1,0:T(8,128)(2,1)}, u32[]{:S(2)}, u32[]{:S(2)}) collective-permute-start(bf16[384,2304]{1,0:T(8,128)(2,1)} %collective-permute-done.1.refs_5_.refs_3_), channel_id=1, source_target_pairs={{8,4},{4,0},{9,5},{5,1},{10,6},{6,2},{11,7},{7,3},{24,20},{20,16},... | collective-permute-start | bytes 5308424 | tf_op jit(solution)/shard_map/ppermute | solution.py:413
  71.9 44.9 %collective-permute-start.3 = (bf16[384,2304]{1,0:T(8,128)(2,1)}, bf16[384,2304]{1,0:T(8,128)(2,1)}, u32[]{:S(2)}, u32[]{:S(2)}) collective-permute-start(bf16[384,2304]{1,0:T(8,128)(2,1)} %collective-permute-done.refs_4_.refs_2_), channel_id=1, source_target_pairs={{4,8},{8,12},{5,9},{9,13},{6,10},{10,14},{7,11},{11,15},{20,24},{2... | collective-permute-start | bytes 5308424 | tf_op jit(solution)/shard_map/ppermute | solution.py:413
  73.8 43.0 %collective-permute-start.6 = (bf16[3,128,2304]{2,1,0:T(8,128)(2,1)}, bf16[3,128,2304]{2,1,0:T(8,128)(2,1)}, u32[]{:S(2)}, u32[]{:S(2)}) collective-permute-start(bf16[3,128,2304]{2,1,0:T(8,128)(2,1)} %collective-permute-done.2.refs_0_), channel_id=1, source_target_pairs={{0,16},{16,0},{1,17},{17,1},{2,18},{18,2},{3,19},{19,3},{4,20},{20... | collective-permute-start | bytes 5308424 | tf_op jit(solution)/shard_map/ppermute | solution.py:407
  79.7 1.2 copy-start.12
  116.8 14.4 %copy-start.15 = (bf16[16,128]{1,0:T(8,128)(2,1)S(1)}, bf16[16,128]{1,0:T(8,128)(2,1)}, u32[]{:S(2)}) copy-start(bf16[16,128]{1,0:T(8,128)(2,1)} %param.18) | copy-start | bytes 12292
  122.1 9.1 %collective-permute-start.10 = (bf16[9,128,2304]{2,1,0:T(8,128)(2,1)}, bf16[9,128,2304]{2,1,0:T(8,128)(2,1)}, u32[]{:S(2)}, u32[]{:S(2)}) collective-permute-start(bf16[9,128,2304]{2,1,0:T(8,128)(2,1)} %shard_map.152.refs_10_.refs_13_), channel_id=1, source_target_pairs={{0,1},{1,0},{2,3},{3,2},{4,5},{5,4},{6,7},{7,6},{8,9},{9,8},{10,11... | collective-permute-start | bytes 15925256 | tf_op jit(solution)/shard_map/ppermute | solution.py:403
  122.4 49.8 %collective-permute-start.11 = (bf16[3,128,2304]{2,1,0:T(8,128)(2,1)}, bf16[3,128,2304]{2,1,0:T(8,128)(2,1)}, u32[]{:S(2)}, u32[]{:S(2)}) collective-permute-start(bf16[3,128,2304]{2,1,0:T(8,128)(2,1)} %collective-permute-done.5.refs_1_), channel_id=1, source_target_pairs={{0,16},{16,0},{1,17},{17,1},{2,18},{18,2},{3,19},{19,3},{4,20},{20... | collective-permute-start | bytes 5308424 | tf_op jit(solution)/shard_map/ppermute | solution.py:407
  123.9 53.3 %collective-permute-start.13 = (bf16[4,128,2304]{2,1,0:T(8,128)(2,1)}, bf16[4,128,2304]{2,1,0:T(8,128)(2,1)}, u32[]{:S(2)}, u32[]{:S(2)}) collective-permute-start(bf16[4,128,2304]{2,1,0:T(8,128)(2,1)} %get-tuple-element.62), channel_id=1, source_target_pairs={{0,2},{1,3},{2,0},{3,1},{4,6},{5,7},{6,4},{7,5},{8,10},{9,11},{10,... | collective-permute-start | bytes 7077896 | tf_op jit(solution)/shard_map/ppermute | solution.py:399
  124.6 47.9 %collective-permute-start.9 = (bf16[384,2304]{1,0:T(8,128)(2,1)}, bf16[384,2304]{1,0:T(8,128)(2,1)}, u32[]{:S(2)}, u32[]{:S(2)}) collective-permute-start(bf16[384,2304]{1,0:T(8,128)(2,1)} %collective-permute-done.4.refs_7_.refs_5_), channel_id=1, source_target_pairs={{4,0},{5,1},{6,2},{7,3},{20,16},{21,17},{22,18},{23,19}} | collective-permute-start | bytes 5308424 | tf_op jit(solution)/shard_map/ppermute | solution.py:413
  125.8 46.6 %collective-permute-start.8 = (bf16[384,2304]{1,0:T(8,128)(2,1)}, bf16[384,2304]{1,0:T(8,128)(2,1)}, u32[]{:S(2)}, u32[]{:S(2)}) collective-permute-start(bf16[384,2304]{1,0:T(8,128)(2,1)} %collective-permute-done.3.refs_6_.refs_4_), channel_id=1, source_target_pairs={{8,12},{9,13},{10,14},{11,15},{24,28},{25,29},{26,30},{27,31}} | collective-permute-start | bytes 5308424 | tf_op jit(solution)/shard_map/ppermute | solution.py:413
  131.5 2.3 %copy-start.9 = (bf16[128,18432]{1,0:T(8,128)(2,1)S(1)}, bf16[128,18432]{1,0:T(8,128)(2,1)}, u32[]{:S(2)}) copy-start(bf16[128,18432]{1,0:T(8,128)(2,1)} %refs_1_.6) | copy-start | bytes 14155780
  140.5 3.4 %copy-start.8 = (bf16[128,32768]{1,0:T(8,128)(2,1)S(1)}, bf16[128,32768]{1,0:T(8,128)(2,1)}, u32[]{:S(2)}) copy-start(bf16[128,32768]{1,0:T(8,128)(2,1)} %refs_1_.7) | copy-start | bytes 25165828
  155.1 22.2 %copy-start.16 = (s32[16]{0:T(128)S(1)}, s32[16]{0:T(128)}, u32[]{:S(2)}) copy-start(s32[16]{0:T(128)} %param.23) | copy-start | bytes 196
  172.2 5.1 %collective-permute-start.12 = (bf16[3,128,2304]{2,1,0:T(8,128)(2,1)}, bf16[3,128,2304]{2,1,0:T(8,128)(2,1)}, u32[]{:S(2)}, u32[]{:S(2)}) collective-permute-start(bf16[3,128,2304]{2,1,0:T(8,128)(2,1)} %collective-permute-done.11.refs_15_), channel_id=1, source_target_pairs={{0,1},{1,0},{2,3},{3,2},{4,5},{5,4},{6,7},{7,6},{8,9},{9,8},{10,11... | collective-permute-start | bytes 5308424 | tf_op jit(solution)/shard_map/ppermute | solution.py:403
  177.3 4.9 %collective-permute-start.14 = (bf16[4,128,2304]{2,1,0:T(8,128)(2,1)}, bf16[4,128,2304]{2,1,0:T(8,128)(2,1)}, u32[]{:S(2)}, u32[]{:S(2)}) collective-permute-start(bf16[4,128,2304]{2,1,0:T(8,128)(2,1)} %collective-permute-done.13.refs_17_), channel_id=1, source_target_pairs={{0,1},{1,0},{2,3},{3,2},{4,5},{5,4},{6,7},{7,6},{8,9},{9,8},{10,11... | collective-permute-start | bytes 7077896 | tf_op jit(solution)/shard_map/ppermute | solution.py:403
  177.7 30.1 %collective-permute-start.15 = (f32[4,128]{1,0:T(4,128)S(1)}, f32[4,128]{1,0:T(4,128)S(1)}, u32[]{:S(2)}, u32[]{:S(2)}) collective-permute-start(f32[4,128]{1,0:T(4,128)S(1)} %add.34), channel_id=1, source_target_pairs={{0,4},{4,8},{8,12},{12,0},{1,5},{5,9},{9,13},{13,1},{2,6},{6,10},{... | collective-permute-start | bytes 6152 | tf_op jit(solution)/shard_map/ppermute | solution.py:419
  179.1 28.7 %collective-permute-start.16 = (f32[4,128]{1,0:T(4,128)S(1)}, f32[4,128]{1,0:T(4,128)S(1)}, u32[]{:S(2)}, u32[]{:S(2)}) collective-permute-start(f32[4,128]{1,0:T(4,128)S(1)} %add.34), channel_id=1, source_target_pairs={{0,8},{4,12},{8,0},{12,4},{1,9},{5,13},{9,1},{13,5},{2,10},{6,14},... | collective-permute-start | bytes 6152 | tf_op jit(solution)/shard_map/ppermute | solution.py:419
  179.2 28.7 %collective-permute-start.17 = (f32[4,128]{1,0:T(4,128)S(1)}, f32[4,128]{1,0:T(4,128)S(1)}, u32[]{:S(2)}, u32[]{:S(2)}) collective-permute-start(f32[4,128]{1,0:T(4,128)S(1)} %add.34), channel_id=1, source_target_pairs={{0,12},{4,0},{8,4},{12,8},{1,13},{5,1},{9,5},{13,9},{2,14},{6,2},{... | collective-permute-start | bytes 6152 | tf_op jit(solution)/shard_map/ppermute | solution.py:419
  183.2 25.3 %copy-start.1 = (bf16[16,32768]{1,0:T(8,128)(2,1)S(1)}, bf16[16,32768]{1,0:T(8,128)(2,1)}, u32[]{:S(2)}) copy-start(bf16[16,32768]{1,0:T(8,128)(2,1)} %param.16) | copy-start | bytes 3145732
  (3 other events, 2.9 us)

commit v6 on v5

--- a/solution.py
+++ b/solution.py
@@ -56,9 +56,9 @@
     return jnp.where(at < 2 * half, moved, at)
 
 
-def weight_pieces(group, codes, scales, count, half, spans, whole=True):
+def weight_pieces(group, codes, scales, order, half, spans):
     cols, blocks = codes.shape[1], scales.shape[0]
-    spans = ([(0, count)] if whole else []) + spans
+    count = spans[0][1]
 
     def span_spec(low, high):
         return pl.BlockSpec(
@@ -75,10 +75,10 @@
             grid=(count,),
             in_specs=[
                 pl.BlockSpec(
-                    (PIECE, cols), lambda i, group: (placed_piece(i, group[0], half), 0)
+                    (PIECE, cols), lambda i, group: (placed_piece(order(i), group[0], half), 0)
                 ),
                 pl.BlockSpec(
-                    (blocks, PIECE), lambda i, group: (0, placed_piece(i, group[0], half))
+                    (blocks, PIECE), lambda i, group: (0, placed_piece(order(i), group[0], half))
                 ),
             ],
             out_specs=[span_spec(low, high) for low, high in spans],
@@ -235,25 +235,25 @@
     rows = (((1,), (1,)), ((), ()))
     for place in range(3):
         pltpu.make_async_copy(own, part(place), csem.at[place]).wait()
-    for tile in range(tiles):
-        slot = tile % depth
-        if tile + depth - 1 < tiles:
-            send(tile + depth - 1, (tile + depth - 1) % depth)
+
+    @pl.loop(0, tiles)
+    def _(tile):
+        slot = lax.rem(tile, depth)
+        for index in range(depth - 1, tiles):
+            pl.when(tile + depth - 1 == index)(lambda index=index: send(index, index % depth))
         for side in range(2):
             for place in range(3):
-                target = wbuf.at[
-                    slot, pl.ds(side * PIECE, PIECE), pl.ds(place * cols, cols)
-                ]
+                target = wbuf.at[slot, pl.ds(side * PIECE, PIECE), pl.ds(place * cols, cols)]
                 pltpu.make_async_copy(target, target, wsem.at[slot, side, place]).wait()
         total = lax.dot_general(cot[...], wbuf[slot], rows, preferred_element_type=jnp.float32)
         for side in range(2):
-            start = pl.multiple_of(placed_piece(where[tile][side][0], y, half) * PIECE, PIECE)
+            start = pl.multiple_of(placed_piece(2 * tile + side, y, half) * PIECE, PIECE)
             adapter = adapter_scale * lax.dot_general(
                 low[...], chosen[pl.ds(start, PIECE), :], rows, preferred_element_type=jnp.float32
             )
             piece = total[:, side * PIECE : (side + 1) * PIECE]
-            at = tile * TILE + side * PIECE
-            out[:, at : at + PIECE] = jnp.where(keep, piece, 0.0) + adapter
+            at = pl.multiple_of(tile * TILE + side * PIECE, PIECE)
+            out[:, pl.ds(at, PIECE)] = jnp.where(keep, piece, 0.0) + adapter
 
 
 def late_kernel(where, half, early, *refs):
@@ -296,39 +296,47 @@
     rows = (((1,), (1,)), ((), ()))
     out[LIVE:, :] = jnp.zeros((out.shape[0] - LIVE, out.shape[1]), out.dtype)
     pltpu.make_async_copy(part(3), part(3), csem.at[3]).wait()
-    for tile in range(tiles):
-        slot = tile % depth
-        if tile + depth - 1 < tiles:
-            send(tile + depth - 1, (tile + depth - 1) % depth)
-        if tile == early:
-            for place in range(3):
-                pltpu.make_async_copy(part(place), part(place), csem.at[place]).wait()
-        first = 3 if tile < early else 0
+
+    def product(tile, first):
+        slot = lax.rem(tile, depth)
+        for index in range(depth - 1, tiles):
+            pl.when(tile + depth - 1 == index)(lambda index=index: send(index, index % depth))
         for side in range(2):
             for place in range(first, 4):
                 target = wbuf.at[slot, pl.ds(side * PIECE, PIECE), pl.ds(place * cols, cols)]
                 pltpu.make_async_copy(target, target, wsem.at[slot, side, place]).wait()
-        total = lax.dot_general(
+        return lax.dot_general(
             cot[:, first * cols :],
             wbuf[slot, :, first * cols :],
             rows,
             preferred_element_type=jnp.float32,
         )
+
+    def store(tile, side, total, before):
+        start = pl.multiple_of(placed_piece(2 * tile + side, y, half) * PIECE, PIECE)
+        piece = jnp.where(keep, total[:, side * PIECE : (side + 1) * PIECE], 0.0)
+        out[:LIVE, pl.ds(start, PIECE)] = (before(start) + piece).astype(out.dtype)
+
+    @pl.loop(0, early)
+    def _(tile):
+        total = product(tile, 3)
         for side in range(2):
-            start = pl.multiple_of(placed_piece(where[tile][side][0], y, half) * PIECE, PIECE)
-            at = tile * TILE + side * PIECE
-            if tile < early:
-                before = sums[:, at : at + PIECE]
-            else:
-                before = adapter_scale * lax.dot_general(
-                    low[...],
-                    chosen[pl.ds(start, PIECE), :],
-                    rows,
-                    preferred_element_type=jnp.float32,
-                )
-            piece = total[:, side * PIECE : (side + 1) * PIECE]
-            result = before + jnp.where(keep, piece, 0.0)
-            out[:LIVE, pl.ds(start, PIECE)] = result.astype(out.dtype)
+            at = pl.multiple_of(tile * TILE + side * PIECE, PIECE)
+            store(tile, side, total, lambda start: sums[:, pl.ds(at, PIECE)])
+
+    for place in range(3):
+        pltpu.make_async_copy(part(place), part(place), csem.at[place]).wait()
+
+    def adapter(start):
+        return adapter_scale * lax.dot_general(
+            low[...], chosen[pl.ds(start, PIECE), :], rows, preferred_element_type=jnp.float32
+        )
+
+    @pl.loop(early, tiles)
+    def _(tile):
+        total = product(tile, 0)
+        for side in range(2):
+            store(tile, side, total, adapter)
 
 
 def matmul_call(kernel, out_shape, operands, vmem_count, scratch):
@@ -382,17 +390,40 @@
     )
 
 
-def gather_kernel(*refs):
-    out, at = refs[-1], 0
-    for ref in refs[:-1]:
-        out[at : at + ref.shape[0]] = ref[...]
-        at += ref.shape[0]
+def gather_kernel(count, *refs):
+    inputs, (out, buffer, come, go) = refs[:-4], refs[-4:]
+    at, moves = 0, []
+    for i, ref in enumerate(inputs):
+        size = ref.shape[0]
+        part = buffer.at[pl.ds(at, size)]
+        arrive = pltpu.make_async_copy(ref, part, come.at[i])
+        moves.append((arrive, pltpu.make_async_copy(part, out.at[pl.ds(at, size)], go.at[i])))
+        arrive.start()
+        at += size
+    for arrive, leave in moves:
+        arrive.wait()
+        leave.start()
+    for arrive, leave in moves:
+        leave.wait()
 
 
 def gather_pieces(arrays):
+    spec = pl.BlockSpec(memory_space=pltpu.HBM)
     count = sum(array.shape[0] for array in arrays)
-    shape = jax.ShapeDtypeStruct((count,) + arrays[0].shape[1:], arrays[0].dtype)
-    return whole_call(gather_kernel, shape, *arrays)
+    shape = (count,) + arrays[0].shape[1:]
+    return pl.pallas_call(
+        lambda *refs: gather_kernel(count, *refs),
+        out_shape=jax.ShapeDtypeStruct(shape, arrays[0].dtype),
+        in_specs=[spec] * len(arrays),
+        out_specs=spec,
+        scratch_shapes=[
+            pltpu.VMEM(shape, arrays[0].dtype),
+            pltpu.SemaphoreType.DMA((len(arrays),)),
+            pltpu.SemaphoreType.DMA((len(arrays),)),
+        ],
+        compiler_params=pltpu.CompilerParams(vmem_limit_bytes=32 * 2**20),
+        cost_estimate=pl.CostEstimate(flops=0, transcendentals=0, bytes_accessed=0),
+    )(*arrays)
 
 
 def across(value):
@@ -426,20 +457,26 @@
         self.half = sum(SENT)
         self.group = y.astype(jnp.int32).reshape(1)
         self.up1, self.dn1 = line(own, 0)(1), line(own, 0)(-1)
+        sent, direct = SENT[0], 2 * self.half
         (head,) = weight_pieces(
-            self.group, codes, self.scales, SENT[0], self.half, [(0, SENT[0])], False
+            self.group,
+            codes,
+            self.scales,
+            lambda i: jnp.where(i < sent, i, direct),
+            self.half,
+            [(0, sent + 1)],
         )
         self.x0 = across(head)
 
     def sum_parts(self, parts):
-        ranges = [(SENT[0], self.half), (2 * self.half, self.pieces)]
+        spans = [(0, self.pieces), (SENT[0], self.half), (2 * self.half + 1, self.pieces)]
         self.mine, first, self.direct = weight_pieces(
-            after(self.group, parts), self.codes, self.scales, self.pieces, self.half, ranges
+            after(self.group, parts), self.codes, self.scales, lambda i: i, self.half, spans
         )
         gathered = lax.all_gather(after(parts, self.mine), "fsdp", axis=0)
         ready = (gathered, self.x0, self.up1, self.dn1)
         self.x1 = across(after(first, *ready))
-        self.y0 = over(after(self.x0, *ready))
+        self.y0 = over(after(self.x0[: SENT[0]], *ready))
         self.up2 = line(after(self.up1, *ready), 1)(1)
         self.dn2 = line(after(self.dn1, *ready), 1)(-1)
         self.sibling = core(after(self.mine, *ready))
@@ -457,14 +494,16 @@
         return after([rows], self.sib_far1)
 
     def finish(self, done, state_part, meta, low, chosen, seq_len):
-        half, far, sib_far = self.half, self.far1, self.sib_far1
+        half, sent = self.half, SENT[0]
         near = [self.own, self.up1, self.dn1, self.up2, self.dn2]
-        arrays = [self.mine, self.sibling, far, sib_far]
-
-        early_count = half + SENT[0]
-        far_at = {i: (2, i) for i in range(early_count)}
-        far_at.update({early_count + i: (4, i) for i in range(2 * half - early_count)})
-        far_at.update({2 * half + i: (6, i) for i in range(self.pieces - 2 * half)})
+        arrays = [self.mine, self.sibling, self.far1, self.sib_far1]
+
+        far_at = {i: (2, i) for i in range(sent)}
+        far_at[2 * half] = (2, sent)
+        far_at.update({i: (2, 1 + i) for i in range(sent, half + sent)})
+        far_at.update({half + sent + i: (4, i) for i in range(half - sent)})
+        far_at.update({i: (6, i - 2 * half - 1) for i in range(2 * half + 1, self.pieces)})
+        early_count = half + sent
 
         def entry(i):
             index, offset = far_at[i]

time: 209 us -> 204 us (0.976)
  Pallas kernels: 87.4 us -> 69.4 us
  local copies, waits for them, and re-layouts: 21.8 us -> 30.2 us
  starting transfers between devices: 24 us -> 29.7 us
    pallas_call x2, Pallas kernels: 41.6 us -> 29.2 us  [matmul_call(): pl.pallas_call(kernel, out_shape=out_shape, in_specs=specs, out_specs=vme...]
    unnamed x35 -> x37, local copies, waits for them, and re-layouts: 15.9 us -> 21.5 us
    pallas_call x4 -> x3, Pallas kernels: 9.14 us -> 3.93 us  [whole_call(): pl.pallas_call(kernel, out_shape=out_shape, in_specs=[pl.BlockSpec(memory...]
    ppermute x3, waiting for transfers between devices: 4.82 us -> 0.01 us  [across(): return lax.ppermute(value, 'dp', [(i, i ^ 2) for i in range(4)])]
    pallas_call x2, Pallas kernels: 18.7 us -> 14.1 us  [weight_pieces(): pl.pallas_call(lambda *refs: weight_kernel(spans, *refs), out_shape=[jax....]
    pallas_call x0 -> x1, Pallas kernels: none -> 4.21 us  [gather_pieces(): pl.pallas_call(lambda *refs: gather_kernel(count, *refs), out_shape=jax.S...]
    ppermute x3, starting transfers between devices: 3.9 us -> 7.91 us  [turns(): lax.ppermute(value, 'fsdp', [(i, (i + k) % 4) for i in range(4)])]
    ppermute x4, waiting for transfers between devices: 3.95 us -> 6.87 us  [core(): return lax.ppermute(value, 'dp', [(i, i ^ 1) for i in range(4)])]
  transfers between devices with their start and end apart: 18 -> 18, of which waited for: 3 -> 3; matrix products, arithmetic and copies ran while one was open for 3% -> 5% of each run, Pallas kernels for 38% -> 31%
where the time goes in v6:
time: 204 us
  Pallas kernels  69.4 us (34%)
  blocking collectives  62.6 us (31%)
  local copies, waits for them, and re-layouts  30.2 us (15%)
  starting transfers between devices  29.7 us (15%)
  waiting for transfers between devices  7.96 us (4%)
  between operations  2.24 us (1%)
    all_gather x1, blocking collectives, gather_rows(): rows = lax.all_gather(row, 'dp', axis=0, tiled=True)  36.5 us
    pallas_call x2, Pallas kernels, matmul_call(): pl.pallas_call(kernel, out_shape=out_shape, in_specs=specs, out_specs=vme...  29.2 us
    all_gather x1, blocking collectives, sum_parts(): gathered = lax.all_gather(after(parts, self.mine), 'fsdp', axis=0)  26.1 us
    unnamed x37, local copies, waits for them, and re-layouts  21.5 us
    pallas_call x2, Pallas kernels, head_grads(): pl.pallas_call(head_kernel, out_shape=[jax.ShapeDtypeStruct((hidden_units...  17.9 us
    pallas_call x2, Pallas kernels, weight_pieces(): pl.pallas_call(lambda *refs: weight_kernel(spans, *refs), out_shape=[jax....  14.1 us
    ppermute x6, starting transfers between devices, send(): lax.ppermute(value, 'fsdp', pairs if sign > 0 else [(3 - a, 3 - b) for a,...  13.4 us
    ppermute x3, starting transfers between devices, turns(): lax.ppermute(value, 'fsdp', [(i, (i + k) % 4) for i in range(4)])  7.91 us
  transfers between devices with their start and end apart: 18, of which 3 were waited for; matrix products, arithmetic and copies ran while one was open for 5% of the time, Pallas kernels for 31%

profile of v6, /device:TPU:0, one launch (start us, length us, event | category | flops | bytes accessed | tf_op | source)
XLA Modules:
  0.0 203.8 jit_solution(17559776143424374780)
XLA Ops:
  0.7 3.8 %copy-done.2 = bf16[2048,2304]{1,0:T(8,128)(2,1)S(1)} copy-done((bf16[2048,2304]{1,0:T(8,128)(2,1)S(1)}, bf16[2048,2304]{1,0:T(8,128)(2,1)}, u32[]{:S(2)}) %copy-start.2) | copy-done | bytes 9437208
  5.3 2.8 %shard_map.149 = bf16[4,128,2304]{2,1,0:T(8,128)(2,1)} custom-call(s32[1]{0:T(128)} %bitcast.2.refs_0_, bf16[2048,2304]{1,0:T(8,128)(2,1)S(1)} %copy-done.2, bf16[36,2048]{1,0:T(8,128)(2,1)S(1)} %bitcast.21), custom_call_target="tpu_custom_call" | custom-call | tf_op jit(solution)/shard_map/pallas_call | solution.py:68
  8.2 2.9 %collective-permute-start.2 = (bf16[4,128,2304]{2,1,0:T(8,128)(2,1)}, bf16[4,128,2304]{2,1,0:T(8,128)(2,1)}, u32[]{:S(2)}, u32[]{:S(2)}) collective-permute-start(bf16[4,128,2304]{2,1,0:T(8,128)(2,1)} %shard_map.149), channel_id=1, source_target_pairs={{0,2},{1,3},{2,0},{3,1},{4,6},{5,7},{6,4},{7,5},{8,10},{9,11},{10,... | collective-permute-start | bytes 7077896 | tf_op jit(solution)/shard_map/ppermute | solution.py:430
  11.1 1.3 slice.9.refs_3_.refs_1_
  12.5 1.3 collective-permute-start.1
  13.7 5.8 %collective-permute-start = (bf16[384,2304]{1,0:T(8,128)(2,1)}, bf16[384,2304]{1,0:T(8,128)(2,1)}, u32[]{:S(2)}, u32[]{:S(2)}) collective-permute-start(bf16[384,2304]{1,0:T(8,128)(2,1)} %slice.9.refs_3_.refs_1_), channel_id=1, source_target_pairs={{0,4},{4,8},{8,12},{1,5},{5,9},{9,13},{2,6},{6,10},{10,14},{3,7},{... | collective-permute-start | bytes 5308424 | tf_op jit(solution)/shard_map/ppermute | solution.py:444
  21.0 1.4 dynamic-slice_reduce_fusion.1
  22.4 1.5 reshape.61.chosen_b
  23.8 1.6 copy-done.7
  27.8 3.7 %copy-done.3 = bf16[2048,2304]{1,0:T(8,128)(2,1)S(1)} copy-done((bf16[2048,2304]{1,0:T(8,128)(2,1)S(1)}, bf16[2048,2304]{1,0:T(8,128)(2,1)}, u32[]{:S(2)}) %copy-start.3) | copy-done | bytes 9437208
  31.4 11.3 %shard_map.148 = (bf16[16,128,2304]{2,1,0:T(8,128)(2,1)}, bf16[3,128,2304]{2,1,0:T(8,128)(2,1)}, bf16[3,128,2304]{2,1,0:T(8,128)(2,1)}) custom-call(s32[1]{0:T(128)} %bitcast.2.refs_0_, bf16[2048,2304]{1,0:T(8,128)(2,1)S(1)} %copy-done.3, bf16[36,2048]{1,0:T(8,128)(2,1)S(1)} %bitcast.22), custom_call_target="tpu_custom_call" | custom-call | tf_op jit(solution)/shard_map/pallas_call | solution.py:68
  42.7 26.1 %all-gather = bf16[1536,32]{1,0:T(8,128)(2,1)S(1)} all-gather(bf16[384,32]{1,0:T(8,128)(2,1)S(1)} %shard_map.147), channel_id=2, replica_groups=mesh['groups'=2,'fsdp'=4,'dp'=4] {'fsdp'}, dimensions={0}, use_global_device_ids=true | all-gather | bytes 122880 | tf_op jit(solution)/shard_map/all_gather | solution.py:476
  68.9 2.8 %slice.12 = bf16[3,128,2304]{2,1,0:T(8,128)(2,1)} slice(bf16[4,128,2304]{2,1,0:T(8,128)(2,1)} %collective-permute-done.2.refs_0_), slice={[0:3], [0:128], [0:2304]} | slice | bytes 3538944 | tf_op jit(solution)/shard_map/slice | solution.py:479
  71.7 1.9 collective-permute-start.3
  75.5 1.6 collective-permute-start.6
  77.8 1.6 copy-done.8
  79.4 2.7 %shard_map.150 = (f32[2048,16]{1,0:T(8,128)S(1)}, f32[2304,8]{1,0:T(8,128)S(1)}, bf16[384,16]{1,0:T(8,128)(2,1)S(1)}) custom-call(s32[2]{0:T(128)S(1)} %pad_add_fusion.1.scalars, bf16[512,2048]{1,0:T(8,128)(2,1)S(1)} %copy-done.8, bf16[512,2304]{1,0:T(8,128)(2,1)S(1)} %copy-done.4, bf16[4,384,32]{2,1,0:T(8,128)(2,1)S(1)} %bitcast.19), custom_call_target="tpu_custom_call" | custom-call | tf_op jit(solution)/shard_map/pallas_call | solution.py:179
  85.0 36.5 %all-gather.1 = bf16[4,1,51328]{2,1,0:T(2,128)(2,1)S(1)} all-gather(bf16[1,1,51328]{2,1,0:T(2,128)(2,1)S(1)} %bitcast.20), channel_id=1, replica_groups=mesh['groups'=2,'fsdp'=4,'dp'=4] {'dp'}, dimensions={0}, use_global_device_ids=true | all-gather | bytes 513280 | tf_op jit(solution)/shard_map/all_gather | solution.py:486
  121.8 4.2 %shard_map.152.refs_10_.refs_13_ = bf16[10,128,2304]{2,1,0:T(8,128)(2,1)} custom-call(bf16[4,128,2304]{2,1,0:T(8,128)(2,1)} %collective-permute-done.2.refs_0_, bf16[3,128,2304]{2,1,0:T(8,128)(2,1)} %collective-permute-done.5.refs_1_, bf16[3,128,2304]{2,1,0:T(8,128)(2,1)} %collective-permute-done.6.refs_2_), custom_call_target="tpu_custom_call" | custom-call | tf_op jit(solution)/shard_map/pallas_call | solution.py:414
  126.4 1.5 collective-permute-start.11
  128.0 1.9 collective-permute-start.8
  131.8 4.2 %collective-permute-done.10.refs_11_.refs_14_ = bf16[10,128,2304]{2,1,0:T(8,128)(2,1)} collective-permute-done((bf16[10,128,2304]{2,1,0:T(8,128)(2,1)}, bf16[10,128,2304]{2,1,0:T(8,128)(2,1)}, u32[]{:S(2)}, u32[]{:S(2)}) %collective-permute-start.10) | collective-permute-done | bytes 5898272 | tf_op jit(solution)/shard_map/ppermute | solution.py:434
  136.3 2.3 %copy-done.10 = bf16[128,18432]{1,0:T(8,128)(2,1)S(1)} copy-done((bf16[128,18432]{1,0:T(8,128)(2,1)S(1)}, bf16[128,18432]{1,0:T(8,128)(2,1)}, u32[]{:S(2)}) %copy-start.10) | copy-done | bytes 4718616
  138.7 6.7 %shard_map.153 = (f32[128,18432]{1,0:T(8,128)}, f32[4,128]{1,0:T(4,128)S(1)}) custom-call(bf16[4,128]{1,0:T(4,128)(2,1)S(1)} %convolution_convert_fusion.states, bf16[4,51328]{1,0:T(4,128)(2,1)S(1)} %bitcast.17, bf16[128,18432]{1,0:T(8,128)(2,1)S(1)} %copy-done.10), custom_call_target="tpu_custom_call" | custom-call | tf_op jit(solution)/shard_map/pallas_call | solution.py:156
  145.3 3.4 %copy-done.9 = bf16[128,32768]{1,0:T(8,128)(2,1)S(1)} copy-done((bf16[128,32768]{1,0:T(8,128)(2,1)S(1)}, bf16[128,32768]{1,0:T(8,128)(2,1)}, u32[]{:S(2)}) %copy-start.9) | copy-done | bytes 8388632
  148.7 11.3 %shard_map.154 = (f32[128,32768]{1,0:T(8,128)}, f32[4,128]{1,0:T(4,128)S(1)}) custom-call(bf16[4,128]{1,0:T(4,128)(2,1)S(1)} %convolution_convert_fusion.states, bf16[4,51328]{1,0:T(4,128)(2,1)S(1)} %bitcast.18, bf16[128,32768]{1,0:T(8,128)(2,1)S(1)} %copy-done.9), custom_call_target="tpu_custom_call" | custom-call | tf_op jit(solution)/shard_map/pallas_call | solution.py:156
  160.0 12.0 %shard_map.155.refs_10_ = f32[384,1024]{1,0:T(8,128)S(1)} custom-call(s32[4]{0:T(128)S(1)} %pad_add_fusion.refs_0_, bf16[384,16]{1,0:T(8,128)(2,1)S(1)} %get-tuple-element.50.refs_1_.refs_8_, bf16[2048,16]{1,0:T(8,128)(2,1)S(1)} %reshape.60.chosen_a.refs_2_.refs_9_, bf16[384,2304]{1,0:T(8,128)(2,1)} %slice.9.refs_3_.refs_1_, ...), custom_call_target="tpu_custom_call" | custom-call | tf_op jit(solution)/shard_map/pallas_call | solution.py:350
  173.5 2.6 %collective-permute-done.12.refs_16_ = bf16[3,128,2304]{2,1,0:T(8,128)(2,1)} collective-permute-done((bf16[3,128,2304]{2,1,0:T(8,128)(2,1)}, bf16[3,128,2304]{2,1,0:T(8,128)(2,1)}, u32[]{:S(2)}, u32[]{:S(2)}) %collective-permute-start.12) | collective-permute-done | bytes 1769504 | tf_op jit(solution)/shard_map/ppermute | solution.py:434
  176.9 4.2 %collective-permute-start.17 = (f32[4,128]{1,0:T(4,128)S(1)}, f32[4,128]{1,0:T(4,128)S(1)}, u32[]{:S(2)}, u32[]{:S(2)}) collective-permute-start(f32[4,128]{1,0:T(4,128)S(1)} %add.34), channel_id=1, source_target_pairs={{0,12},{4,0},{8,4},{12,8},{1,13},{5,1},{9,5},{13,9},{2,14},{6,2},{... | collective-permute-start | bytes 6152 | tf_op jit(solution)/shard_map/ppermute | solution.py:450
  181.1 1.8 collective-permute-start.16
  182.8 1.9 collective-permute-start.15
  185.9 17.2 %shard_map.156 = bf16[512,2048]{1,0:T(8,128)(2,1)} custom-call(s32[4]{0:T(128)S(1)} %pad_add_fusion.refs_0_, bf16[384,2304]{1,0:T(8,128)(2,1)} %slice.9.refs_3_.refs_1_, bf16[384,2304]{1,0:T(8,128)(2,1)} %collective-permute-done.refs_4_.refs_2_, bf16[384,2304]{1,0:T(8,128)(2,1)} %collective-permute-done.1.refs_5_.refs_3_, ...), custom_call_target="tpu_custom_call" | custom-call | tf_op jit(solution)/shard_map/pallas_call | solution.py:350
  (76 shorter events, 15.9 us)
Async XLA Ops:
  0.6 19.5 %copy-start = (bf16[16,32768]{1,0:T(8,128)(2,1)S(1)}, bf16[16,32768]{1,0:T(8,128)(2,1)}, u32[]{:S(2)}) copy-start(bf16[16,32768]{1,0:T(8,128)(2,1)} %param.16) | copy-start | bytes 3145732
  0.7 3.8 %copy-start.2 = (bf16[2048,2304]{1,0:T(8,128)(2,1)S(1)}, bf16[2048,2304]{1,0:T(8,128)(2,1)}, u32[]{:S(2)}) copy-start(bf16[2048,2304]{1,0:T(8,128)(2,1)} %refs_1_.5) | copy-start | bytes 28311556
  5.3 5.8 %copy-start.4 = (bf16[512,2304]{1,0:T(8,128)(2,1)S(1)}, bf16[512,2304]{1,0:T(8,128)(2,1)}, u32[]{:S(2)}) copy-start(bf16[512,2304]{1,0:T(8,128)(2,1)} %cotangent.3) | copy-start | bytes 7077892
  8.2 60.7 %collective-permute-start.2 = (bf16[4,128,2304]{2,1,0:T(8,128)(2,1)}, bf16[4,128,2304]{2,1,0:T(8,128)(2,1)}, u32[]{:S(2)}, u32[]{:S(2)}) collective-permute-start(bf16[4,128,2304]{2,1,0:T(8,128)(2,1)} %shard_map.149), channel_id=1, source_target_pairs={{0,2},{1,3},{2,0},{3,1},{4,6},{5,7},{6,4},{7,5},{8,10},{9,11},{10,... | collective-permute-start | bytes 7077896 | tf_op jit(solution)/shard_map/ppermute | solution.py:430
  12.5 56.4 %collective-permute-start.1 = (bf16[384,2304]{1,0:T(8,128)(2,1)}, bf16[384,2304]{1,0:T(8,128)(2,1)}, u32[]{:S(2)}, u32[]{:S(2)}) collective-permute-start(bf16[384,2304]{1,0:T(8,128)(2,1)} %slice.9.refs_3_.refs_1_), channel_id=1, source_target_pairs={{12,8},{8,4},{4,0},{13,9},{9,5},{5,1},{14,10},{10,6},{6,2},{15,11}... | collective-permute-start | bytes 5308424 | tf_op jit(solution)/shard_map/ppermute | solution.py:444
  13.7 55.1 %collective-permute-start = (bf16[384,2304]{1,0:T(8,128)(2,1)}, bf16[384,2304]{1,0:T(8,128)(2,1)}, u32[]{:S(2)}, u32[]{:S(2)}) collective-permute-start(bf16[384,2304]{1,0:T(8,128)(2,1)} %slice.9.refs_3_.refs_1_), channel_id=1, source_target_pairs={{0,4},{4,8},{8,12},{1,5},{5,9},{9,13},{2,6},{6,10},{10,14},{3,7},{... | collective-permute-start | bytes 5308424 | tf_op jit(solution)/shard_map/ppermute | solution.py:444
  21.0 139.0 %copy-start.5 = (bf16[2048,16]{1,0:T(8,128)(2,1)}, bf16[2048,16]{1,0:T(8,128)(2,1)S(1)}, u32[]{:S(2)}) copy-start(bf16[2048,16]{1,0:T(8,128)(2,1)S(1)} %reshape.60.chosen_a.refs_2_.refs_9_) | copy-start | bytes 196612
  23.8 1.6 copy-start.7
  26.5 1.3 copy-start.15
  27.8 3.7 %copy-start.3 = (bf16[2048,2304]{1,0:T(8,128)(2,1)S(1)}, bf16[2048,2304]{1,0:T(8,128)(2,1)}, u32[]{:S(2)}) copy-start(bf16[2048,2304]{1,0:T(8,128)(2,1)} %refs_1_.5) | copy-start | bytes 28311556
  68.9 52.9 %collective-permute-start.7 = (bf16[16,128,2304]{2,1,0:T(8,128)(2,1)}, bf16[16,128,2304]{2,1,0:T(8,128)(2,1)}, u32[]{:S(2)}, u32[]{:S(2)}) collective-permute-start(bf16[16,128,2304]{2,1,0:T(8,128)(2,1)} %get-tuple-element.47.refs_8_.refs_11_), channel_id=1, source_target_pairs={{0,1},{1,0},{2,3},{3,2},{4,5},{5,4},{6,7},{7,6},{8,9},{9,8},{10,11... | collective-permute-start | bytes 28311560 | tf_op jit(solution)/shard_map/ppermute | solution.py:434
  71.7 50.0 %collective-permute-start.3 = (bf16[384,2304]{1,0:T(8,128)(2,1)}, bf16[384,2304]{1,0:T(8,128)(2,1)}, u32[]{:S(2)}, u32[]{:S(2)}) collective-permute-start(bf16[384,2304]{1,0:T(8,128)(2,1)} %collective-permute-done.refs_4_.refs_2_), channel_id=1, source_target_pairs={{4,8},{8,12},{5,9},{9,13},{6,10},{10,14},{7,11},{11,15},{20,24},{2... | collective-permute-start | bytes 5308424 | tf_op jit(solution)/shard_map/ppermute | solution.py:444
  73.7 48.1 %collective-permute-start.4 = (bf16[384,2304]{1,0:T(8,128)(2,1)}, bf16[384,2304]{1,0:T(8,128)(2,1)}, u32[]{:S(2)}, u32[]{:S(2)}) collective-permute-start(bf16[384,2304]{1,0:T(8,128)(2,1)} %collective-permute-done.1.refs_5_.refs_3_), channel_id=1, source_target_pairs={{8,4},{4,0},{9,5},{5,1},{10,6},{6,2},{11,7},{7,3},{24,20},{20,16},... | collective-permute-start | bytes 5308424 | tf_op jit(solution)/shard_map/ppermute | solution.py:444
  74.9 46.8 %collective-permute-start.5 = (bf16[3,128,2304]{2,1,0:T(8,128)(2,1)}, bf16[3,128,2304]{2,1,0:T(8,128)(2,1)}, u32[]{:S(2)}, u32[]{:S(2)}) collective-permute-start(bf16[3,128,2304]{2,1,0:T(8,128)(2,1)} %get-tuple-element.43), channel_id=1, source_target_pairs={{0,2},{1,3},{2,0},{3,1},{4,6},{5,7},{6,4},{7,5},{8,10},{9,11},{10,... | collective-permute-start | bytes 5308424 | tf_op jit(solution)/shard_map/ppermute | solution.py:430
  75.5 46.3 %collective-permute-start.6 = (bf16[3,128,2304]{2,1,0:T(8,128)(2,1)}, bf16[3,128,2304]{2,1,0:T(8,128)(2,1)}, u32[]{:S(2)}, u32[]{:S(2)}) collective-permute-start(bf16[3,128,2304]{2,1,0:T(8,128)(2,1)} %slice.12), channel_id=1, source_target_pairs={{0,16},{16,0},{1,17},{17,1},{2,18},{18,2},{3,19},{19,3},{4,20},{20... | collective-permute-start | bytes 5308424 | tf_op jit(solution)/shard_map/ppermute | solution.py:438
  77.8 1.6 copy-start.8
  83.1 1.3 copy-start.13
  121.8 14.4 %copy-start.16 = (bf16[16,128]{1,0:T(8,128)(2,1)S(1)}, bf16[16,128]{1,0:T(8,128)(2,1)}, u32[]{:S(2)}) copy-start(bf16[16,128]{1,0:T(8,128)(2,1)} %param.18) | copy-start | bytes 12292
  126.0 10.0 %collective-permute-start.10 = (bf16[10,128,2304]{2,1,0:T(8,128)(2,1)}, bf16[10,128,2304]{2,1,0:T(8,128)(2,1)}, u32[]{:S(2)}, u32[]{:S(2)}) collective-permute-start(bf16[10,128,2304]{2,1,0:T(8,128)(2,1)} %shard_map.152.refs_10_.refs_13_), channel_id=1, source_target_pairs={{0,1},{1,0},{2,3},{3,2},{4,5},{5,4},{6,7},{7,6},{8,9},{9,8},{10,11... | collective-permute-start | bytes 17694728 | tf_op jit(solution)/shard_map/ppermute | solution.py:434
  126.4 45.6 %collective-permute-start.11 = (bf16[3,128,2304]{2,1,0:T(8,128)(2,1)}, bf16[3,128,2304]{2,1,0:T(8,128)(2,1)}, u32[]{:S(2)}, u32[]{:S(2)}) collective-permute-start(bf16[3,128,2304]{2,1,0:T(8,128)(2,1)} %collective-permute-done.5.refs_1_), channel_id=1, source_target_pairs={{0,16},{16,0},{1,17},{17,1},{2,18},{18,2},{3,19},{19,3},{4,20},{20... | collective-permute-start | bytes 5308424 | tf_op jit(solution)/shard_map/ppermute | solution.py:438
  128.0 44.5 %collective-permute-start.8 = (bf16[384,2304]{1,0:T(8,128)(2,1)}, bf16[384,2304]{1,0:T(8,128)(2,1)}, u32[]{:S(2)}, u32[]{:S(2)}) collective-permute-start(bf16[384,2304]{1,0:T(8,128)(2,1)} %collective-permute-done.3.refs_6_.refs_4_), channel_id=1, source_target_pairs={{8,12},{9,13},{10,14},{11,15},{24,28},{25,29},{26,30},{27,31}} | collective-permute-start | bytes 5308424 | tf_op jit(solution)/shard_map/ppermute | solution.py:444
  129.8 43.7 %collective-permute-start.9 = (bf16[384,2304]{1,0:T(8,128)(2,1)}, bf16[384,2304]{1,0:T(8,128)(2,1)}, u32[]{:S(2)}, u32[]{:S(2)}) collective-permute-start(bf16[384,2304]{1,0:T(8,128)(2,1)} %collective-permute-done.4.refs_7_.refs_5_), channel_id=1, source_target_pairs={{4,0},{5,1},{6,2},{7,3},{20,16},{21,17},{22,18},{23,19}} | collective-permute-start | bytes 5308424 | tf_op jit(solution)/shard_map/ppermute | solution.py:444
  131.1 42.4 %collective-permute-start.13 = (bf16[3,128,2304]{2,1,0:T(8,128)(2,1)}, bf16[3,128,2304]{2,1,0:T(8,128)(2,1)}, u32[]{:S(2)}, u32[]{:S(2)}) collective-permute-start(bf16[3,128,2304]{2,1,0:T(8,128)(2,1)} %get-tuple-element.62), channel_id=1, source_target_pairs={{0,2},{1,3},{2,0},{3,1},{4,6},{5,7},{6,4},{7,5},{8,10},{9,11},{10,... | collective-permute-start | bytes 5308424 | tf_op jit(solution)/shard_map/ppermute | solution.py:430
  136.3 2.3 %copy-start.10 = (bf16[128,18432]{1,0:T(8,128)(2,1)S(1)}, bf16[128,18432]{1,0:T(8,128)(2,1)}, u32[]{:S(2)}) copy-start(bf16[128,18432]{1,0:T(8,128)(2,1)} %refs_1_.6) | copy-start | bytes 14155780
  145.3 3.4 %copy-start.9 = (bf16[128,32768]{1,0:T(8,128)(2,1)S(1)}, bf16[128,32768]{1,0:T(8,128)(2,1)}, u32[]{:S(2)}) copy-start(bf16[128,32768]{1,0:T(8,128)(2,1)} %refs_1_.7) | copy-start | bytes 25165828
  160.0 16.5 %copy-start.17 = (s32[16]{0:T(128)S(1)}, s32[16]{0:T(128)}, u32[]{:S(2)}) copy-start(s32[16]{0:T(128)} %param.23) | copy-start | bytes 196
  172.0 4.1 %collective-permute-start.12 = (bf16[3,128,2304]{2,1,0:T(8,128)(2,1)}, bf16[3,128,2304]{2,1,0:T(8,128)(2,1)}, u32[]{:S(2)}, u32[]{:S(2)}) collective-permute-start(bf16[3,128,2304]{2,1,0:T(8,128)(2,1)} %collective-permute-done.11.refs_15_), channel_id=1, source_target_pairs={{0,1},{1,0},{2,3},{3,2},{4,5},{5,4},{6,7},{7,6},{8,9},{9,8},{10,11... | collective-permute-start | bytes 5308424 | tf_op jit(solution)/shard_map/ppermute | solution.py:434
  176.1 8.7 %collective-permute-start.14 = (bf16[3,128,2304]{2,1,0:T(8,128)(2,1)}, bf16[3,128,2304]{2,1,0:T(8,128)(2,1)}, u32[]{:S(2)}, u32[]{:S(2)}) collective-permute-start(bf16[3,128,2304]{2,1,0:T(8,128)(2,1)} %collective-permute-done.13.refs_17_), channel_id=1, source_target_pairs={{0,1},{1,0},{2,3},{3,2},{4,5},{5,4},{6,7},{7,6},{8,9},{9,8},{10,11... | collective-permute-start | bytes 5308424 | tf_op jit(solution)/shard_map/ppermute | solution.py:434
  176.9 26.2 %collective-permute-start.17 = (f32[4,128]{1,0:T(4,128)S(1)}, f32[4,128]{1,0:T(4,128)S(1)}, u32[]{:S(2)}, u32[]{:S(2)}) collective-permute-start(f32[4,128]{1,0:T(4,128)S(1)} %add.34), channel_id=1, source_target_pairs={{0,12},{4,0},{8,4},{12,8},{1,13},{5,1},{9,5},{13,9},{2,14},{6,2},{... | collective-permute-start | bytes 6152 | tf_op jit(solution)/shard_map/ppermute | solution.py:450
  181.1 22.1 %collective-permute-start.16 = (f32[4,128]{1,0:T(4,128)S(1)}, f32[4,128]{1,0:T(4,128)S(1)}, u32[]{:S(2)}, u32[]{:S(2)}) collective-permute-start(f32[4,128]{1,0:T(4,128)S(1)} %add.34), channel_id=1, source_target_pairs={{0,8},{4,12},{8,0},{12,4},{1,9},{5,13},{9,1},{13,5},{2,10},{6,14},... | collective-permute-start | bytes 6152 | tf_op jit(solution)/shard_map/ppermute | solution.py:450
  182.8 20.3 %collective-permute-start.15 = (f32[4,128]{1,0:T(4,128)S(1)}, f32[4,128]{1,0:T(4,128)S(1)}, u32[]{:S(2)}, u32[]{:S(2)}) collective-permute-start(f32[4,128]{1,0:T(4,128)S(1)} %add.34), channel_id=1, source_target_pairs={{0,4},{4,8},{8,12},{12,0},{1,5},{5,9},{9,13},{13,1},{2,6},{6,10},{... | collective-permute-start | bytes 6152 | tf_op jit(solution)/shard_map/ppermute | solution.py:450
  185.9 17.9 %copy-start.1 = (bf16[16,32768]{1,0:T(8,128)(2,1)S(1)}, bf16[16,32768]{1,0:T(8,128)(2,1)}, u32[]{:S(2)}) copy-start(bf16[16,32768]{1,0:T(8,128)(2,1)} %param.16) | copy-start | bytes 3145732
  (4 other events, 4.0 us)

commit v7 on v6

--- a/solution.py
+++ b/solution.py
@@ -56,7 +56,7 @@
     return jnp.where(at < 2 * half, moved, at)
 
 
-def weight_pieces(group, codes, scales, order, half, spans):
+def weight_pieces(group, codes, scales, half, spans):
     cols, blocks = codes.shape[1], scales.shape[0]
     count = spans[0][1]
 
@@ -75,10 +75,10 @@
             grid=(count,),
             in_specs=[
                 pl.BlockSpec(
-                    (PIECE, cols), lambda i, group: (placed_piece(order(i), group[0], half), 0)
+                    (PIECE, cols), lambda i, group: (placed_piece(i, group[0], half), 0)
                 ),
                 pl.BlockSpec(
-                    (blocks, PIECE), lambda i, group: (0, placed_piece(order(i), group[0], half))
+                    (blocks, PIECE), lambda i, group: (0, placed_piece(i, group[0], half))
                 ),
             ],
             out_specs=[span_spec(low, high) for low, high in spans],
@@ -457,29 +457,21 @@
         self.half = sum(SENT)
         self.group = y.astype(jnp.int32).reshape(1)
         self.up1, self.dn1 = line(own, 0)(1), line(own, 0)(-1)
-        sent, direct = SENT[0], 2 * self.half
-        (head,) = weight_pieces(
-            self.group,
-            codes,
-            self.scales,
-            lambda i: jnp.where(i < sent, i, direct),
-            self.half,
-            [(0, sent + 1)],
-        )
+        (head,) = weight_pieces(self.group, codes, self.scales, self.half, [(0, SENT[0])])
         self.x0 = across(head)
 
     def sum_parts(self, parts):
-        spans = [(0, self.pieces), (SENT[0], self.half), (2 * self.half + 1, self.pieces)]
+        spans = [(0, self.pieces), (SENT[0], self.half), (2 * self.half, self.pieces)]
         self.mine, first, self.direct = weight_pieces(
-            after(self.group, parts), self.codes, self.scales, lambda i: i, self.half, spans
+            after(self.group, parts), self.codes, self.scales, self.half, spans
         )
         gathered = lax.all_gather(after(parts, self.mine), "fsdp", axis=0)
-        ready = (gathered, self.x0, self.up1, self.dn1)
+        ready = (gathered, self.up1, self.dn1)
         self.x1 = across(after(first, *ready))
-        self.y0 = over(after(self.x0[: SENT[0]], *ready))
+        self.y0 = over(after(self.x0, *ready))
         self.up2 = line(after(self.up1, *ready), 1)(1)
         self.dn2 = line(after(self.dn1, *ready), 1)(-1)
-        self.sibling = core(after(self.mine, *ready))
+        self.sibling = core(after(self.mine, *ready, self.x0))
         return [gathered]
 
     def gather_rows(self, row):
@@ -498,11 +490,9 @@
         near = [self.own, self.up1, self.dn1, self.up2, self.dn2]
         arrays = [self.mine, self.sibling, self.far1, self.sib_far1]
 
-        far_at = {i: (2, i) for i in range(sent)}
-        far_at[2 * half] = (2, sent)
-        far_at.update({i: (2, 1 + i) for i in range(sent, half + sent)})
+        far_at = {i: (2, i) for i in range(half + sent)}
         far_at.update({half + sent + i: (4, i) for i in range(half - sent)})
-        far_at.update({i: (6, i - 2 * half - 1) for i in range(2 * half + 1, self.pieces)})
+        far_at.update({i: (6, i - 2 * half) for i in range(2 * half, self.pieces)})
         early_count = half + sent
 
         def entry(i):

time: 204 us -> 194 us (0.951)
  blocking collectives: 62.6 us -> 53 us
  local copies, waits for them, and re-layouts: 30.2 us -> 23.3 us
  Pallas kernels: 69.4 us -> 73.8 us
  waiting for transfers between devices: 7.96 us -> 12.3 us
  starting transfers between devices: 29.7 us -> 26.7 us
    ppermute x3, waiting for transfers between devices: 0.01 us -> 9.33 us  [across(): return lax.ppermute(value, 'dp', [(i, i ^ 2) for i in range(4)])]
    all_gather x1, blocking collectives: 26.1 us -> 18.9 us  [sum_parts(): gathered = lax.all_gather(after(parts, self.mine), 'fsdp', axis=0)]
    unnamed x37 -> x35, local copies, waits for them, and re-layouts: 21.5 us -> 15.8 us
    pallas_call x2, Pallas kernels: 14.1 us -> 18.7 us  [weight_pieces(): pl.pallas_call(lambda *refs: weight_kernel(spans, *refs), out_shape=[jax....]
    ppermute x4, waiting for transfers between devices: 6.87 us -> 2.55 us  [core(): return lax.ppermute(value, 'dp', [(i, i ^ 1) for i in range(4)])]
    ppermute x3, starting transfers between devices: 7.91 us -> 4.2 us  [turns(): lax.ppermute(value, 'fsdp', [(i, (i + k) % 4) for i in range(4)])]
    slice x1 -> x0, local copies, waits for them, and re-layouts: 2.8 us -> none  [sum_parts(): self.y0 = over(after(self.x0[:SENT[0]], *ready))]
    all_gather x1, blocking collectives: 36.5 us -> 34.1 us  [gather_rows(): rows = lax.all_gather(row, 'dp', axis=0, tiled=True)]
  transfers between devices with their start and end apart: 18 -> 18, of which waited for: 3 -> 4; matrix products, arithmetic and copies ran while one was open for 5% -> 3% of each run, Pallas kernels for 31% -> 36%
where the time goes in v7:
time: 194 us; the launch traced here: 193 us
  Pallas kernels  73.8 us (38%)
  blocking collectives  53 us (27%)
  starting transfers between devices  26.7 us (14%)
  local copies, waits for them, and re-layouts  23.3 us (12%)
  waiting for transfers between devices  12.3 us (6%)
  between operations  2.26 us (1%)
    all_gather x1, blocking collectives, gather_rows(): rows = lax.all_gather(row, 'dp', axis=0, tiled=True)  34.1 us
    pallas_call x2, Pallas kernels, matmul_call(): pl.pallas_call(kernel, out_shape=out_shape, in_specs=specs, out_specs=vme...  29.2 us
    all_gather x1, blocking collectives, sum_parts(): gathered = lax.all_gather(after(parts, self.mine), 'fsdp', axis=0)  18.9 us
    pallas_call x2, Pallas kernels, weight_pieces(): pl.pallas_call(lambda *refs: weight_kernel(spans, *refs), out_shape=[jax....  18.7 us
    pallas_call x2, Pallas kernels, head_grads(): pl.pallas_call(head_kernel, out_shape=[jax.ShapeDtypeStruct((hidden_units...  17.9 us
    unnamed x35, local copies, waits for them, and re-layouts  15.8 us
    ppermute x6, starting transfers between devices, send(): lax.ppermute(value, 'fsdp', pairs if sign > 0 else [(3 - a, 3 - b) for a,...  13.8 us
    ppermute x3, waiting for transfers between devices, across(): return lax.ppermute(value, 'dp', [(i, i ^ 2) for i in range(4)])  9.33 us
  transfers between devices with their start and end apart: 18, of which 4 were waited for; matrix products, arithmetic and copies ran while one was open for 3% of the time, Pallas kernels for 36%

profile of v7, /device:TPU:0, one launch (start us, length us, event | category | flops | bytes accessed | tf_op | source)
XLA Modules:
  0.0 193.0 jit_solution(14807622734073104043)
XLA Ops:
  0.6 2.9 %slice.6.refs_3_.refs_1_ = bf16[384,2304]{1,0:T(8,128)(2,1)} slice(bf16[512,2304]{1,0:T(8,128)(2,1)} %cotangent.3), slice={[0:384], [0:2304]} | slice | bytes 3538944 | tf_op jit(solution)/shard_map/slice | solution.py:539
  3.6 6.2 %collective-permute-start = (bf16[384,2304]{1,0:T(8,128)(2,1)}, bf16[384,2304]{1,0:T(8,128)(2,1)}, u32[]{:S(2)}, u32[]{:S(2)}) collective-permute-start(bf16[384,2304]{1,0:T(8,128)(2,1)} %slice.6.refs_3_.refs_1_), channel_id=1, source_target_pairs={{0,4},{4,8},{8,12},{1,5},{5,9},{9,13},{2,6},{6,10},{10,14},{3,7},{... | collective-permute-start | bytes 5308424 | tf_op jit(solution)/shard_map/ppermute | solution.py:444
  9.7 1.3 collective-permute-start.1
  11.0 3.7 %copy-done.2 = bf16[2048,2304]{1,0:T(8,128)(2,1)S(1)} copy-done((bf16[2048,2304]{1,0:T(8,128)(2,1)S(1)}, bf16[2048,2304]{1,0:T(8,128)(2,1)}, u32[]{:S(2)}) %copy-start.2) | copy-done | bytes 9437208
  15.6 2.4 %shard_map.149 = bf16[3,128,2304]{2,1,0:T(8,128)(2,1)} custom-call(s32[1]{0:T(128)} %bitcast.2.refs_0_, bf16[2048,2304]{1,0:T(8,128)(2,1)S(1)} %copy-done.2, bf16[36,2048]{1,0:T(8,128)(2,1)S(1)} %bitcast.21), custom_call_target="tpu_custom_call" | custom-call | tf_op jit(solution)/shard_map/pallas_call | solution.py:68
  18.1 1.5 collective-permute-start.5
  21.0 1.4 dynamic-slice_reduce_fusion.1
  22.4 1.5 reshape.61.chosen_b
  23.9 1.6 copy-done.6
  27.8 16.3 %shard_map.148 = (bf16[16,128,2304]{2,1,0:T(8,128)(2,1)}, bf16[3,128,2304]{2,1,0:T(8,128)(2,1)}, bf16[4,128,2304]{2,1,0:T(8,128)(2,1)}) custom-call(s32[1]{0:T(128)} %bitcast.2.refs_0_, bf16[2048,2304]{1,0:T(8,128)(2,1)} %refs_1_.5, bf16[36,2048]{1,0:T(8,128)(2,1)S(1)} %bitcast.22), custom_call_target="tpu_custom_call" | custom-call | tf_op jit(solution)/shard_map/pallas_call | solution.py:68
  44.0 18.9 %all-gather = bf16[1536,32]{1,0:T(8,128)(2,1)S(1)} all-gather(bf16[384,32]{1,0:T(8,128)(2,1)S(1)} %shard_map.147), channel_id=2, replica_groups=mesh['groups'=2,'fsdp'=4,'dp'=4] {'fsdp'}, dimensions={0}, use_global_device_ids=true | all-gather | bytes 122880 | tf_op jit(solution)/shard_map/all_gather | solution.py:468
  63.0 1.7 collective-permute-start.4
  64.7 1.5 collective-permute-start.6
  66.2 1.3 collective-permute-start.3
  67.5 1.9 collective-permute-start.2
  70.1 2.7 %shard_map.150 = (f32[2048,16]{1,0:T(8,128)S(1)}, f32[2304,8]{1,0:T(8,128)S(1)}, bf16[384,16]{1,0:T(8,128)(2,1)S(1)}) custom-call(s32[2]{0:T(128)S(1)} %pad_add_fusion.1.scalars, bf16[512,2048]{1,0:T(8,128)(2,1)S(1)} %copy-done.7, bf16[512,2304]{1,0:T(8,128)(2,1)S(1)} %copy-done.3, bf16[4,384,32]{2,1,0:T(8,128)(2,1)S(1)} %bitcast.19), custom_call_target="tpu_custom_call" | custom-call | tf_op jit(solution)/shard_map/pallas_call | solution.py:179
  75.4 34.1 %all-gather.1 = bf16[4,1,51328]{2,1,0:T(2,128)(2,1)S(1)} all-gather(bf16[1,1,51328]{2,1,0:T(2,128)(2,1)S(1)} %bitcast.20), channel_id=1, replica_groups=mesh['groups'=2,'fsdp'=4,'dp'=4] {'dp'}, dimensions={0}, use_global_device_ids=true | all-gather | bytes 513280 | tf_op jit(solution)/shard_map/all_gather | solution.py:478
  109.8 4.1 %shard_map.152.refs_10_.refs_13_ = bf16[9,128,2304]{2,1,0:T(8,128)(2,1)} custom-call(bf16[3,128,2304]{2,1,0:T(8,128)(2,1)} %collective-permute-done.5.refs_0_, bf16[3,128,2304]{2,1,0:T(8,128)(2,1)} %collective-permute-done.4.refs_1_, bf16[3,128,2304]{2,1,0:T(8,128)(2,1)} %collective-permute-done.6.refs_2_), custom_call_target="tpu_custom_call" | custom-call | tf_op jit(solution)/shard_map/pallas_call | solution.py:414
  114.3 1.5 collective-permute-start.11
  115.8 1.6 collective-permute-start.13
  117.5 1.3 collective-permute-start.9
  118.8 1.9 collective-permute-start.8
  120.7 2.4 %collective-permute-done.10.refs_11_.refs_14_ = bf16[9,128,2304]{2,1,0:T(8,128)(2,1)} collective-permute-done((bf16[9,128,2304]{2,1,0:T(8,128)(2,1)}, bf16[9,128,2304]{2,1,0:T(8,128)(2,1)}, u32[]{:S(2)}, u32[]{:S(2)}) %collective-permute-start.10) | collective-permute-done | bytes 5308448 | tf_op jit(solution)/shard_map/ppermute | solution.py:434
  123.4 2.3 %copy-done.9 = bf16[128,18432]{1,0:T(8,128)(2,1)S(1)} copy-done((bf16[128,18432]{1,0:T(8,128)(2,1)S(1)}, bf16[128,18432]{1,0:T(8,128)(2,1)}, u32[]{:S(2)}) %copy-start.9) | copy-done | bytes 4718616
  125.7 6.7 %shard_map.153 = (f32[128,18432]{1,0:T(8,128)}, f32[4,128]{1,0:T(4,128)S(1)}) custom-call(bf16[4,128]{1,0:T(4,128)(2,1)S(1)} %convolution_convert_fusion.states, bf16[4,51328]{1,0:T(4,128)(2,1)S(1)} %bitcast.17, bf16[128,18432]{1,0:T(8,128)(2,1)S(1)} %copy-done.9), custom_call_target="tpu_custom_call" | custom-call | tf_op jit(solution)/shard_map/pallas_call | solution.py:156
  132.4 3.4 %copy-done.8 = bf16[128,32768]{1,0:T(8,128)(2,1)S(1)} copy-done((bf16[128,32768]{1,0:T(8,128)(2,1)S(1)}, bf16[128,32768]{1,0:T(8,128)(2,1)}, u32[]{:S(2)}) %copy-start.8) | copy-done | bytes 8388632
  135.8 11.3 %shard_map.154 = (f32[128,32768]{1,0:T(8,128)}, f32[4,128]{1,0:T(4,128)S(1)}) custom-call(bf16[4,128]{1,0:T(4,128)(2,1)S(1)} %convolution_convert_fusion.states, bf16[4,51328]{1,0:T(4,128)(2,1)S(1)} %bitcast.18, bf16[128,32768]{1,0:T(8,128)(2,1)S(1)} %copy-done.8), custom_call_target="tpu_custom_call" | custom-call | tf_op jit(solution)/shard_map/pallas_call | solution.py:156
  147.0 12.0 %shard_map.155.refs_10_ = f32[384,1024]{1,0:T(8,128)S(1)} custom-call(s32[4]{0:T(128)S(1)} %pad_add_fusion.refs_0_, bf16[384,16]{1,0:T(8,128)(2,1)S(1)} %get-tuple-element.50.refs_1_.refs_8_, bf16[2048,16]{1,0:T(8,128)(2,1)S(1)} %reshape.60.chosen_a.refs_2_.refs_9_, bf16[384,2304]{1,0:T(8,128)(2,1)} %slice.6.refs_3_.refs_1_, ...), custom_call_target="tpu_custom_call" | custom-call | tf_op jit(solution)/shard_map/pallas_call | solution.py:350
  159.8 9.3 %collective-permute-done.13.refs_17_ = bf16[4,128,2304]{2,1,0:T(8,128)(2,1)} collective-permute-done((bf16[4,128,2304]{2,1,0:T(8,128)(2,1)}, bf16[4,128,2304]{2,1,0:T(8,128)(2,1)}, u32[]{:S(2)}, u32[]{:S(2)}) %collective-permute-start.13) | collective-permute-done | bytes 2359328 | tf_op jit(solution)/shard_map/ppermute | solution.py:430
  169.6 1.5 collective-permute-start.16
  171.1 2.6 %collective-permute-start.17 = (f32[4,128]{1,0:T(4,128)S(1)}, f32[4,128]{1,0:T(4,128)S(1)}, u32[]{:S(2)}, u32[]{:S(2)}) collective-permute-start(f32[4,128]{1,0:T(4,128)S(1)} %add.34), channel_id=1, source_target_pairs={{0,12},{4,0},{8,4},{12,8},{1,13},{5,1},{9,5},{13,9},{2,14},{6,2},{... | collective-permute-start | bytes 6152 | tf_op jit(solution)/shard_map/ppermute | solution.py:450
  175.1 17.2 %shard_map.156 = bf16[512,2048]{1,0:T(8,128)(2,1)} custom-call(s32[4]{0:T(128)S(1)} %pad_add_fusion.refs_0_, bf16[384,2304]{1,0:T(8,128)(2,1)} %slice.6.refs_3_.refs_1_, bf16[384,2304]{1,0:T(8,128)(2,1)} %collective-permute-done.refs_4_.refs_2_, bf16[384,2304]{1,0:T(8,128)(2,1)} %collective-permute-done.1.refs_5_.refs_3_, ...), custom_call_target="tpu_custom_call" | custom-call | tf_op jit(solution)/shard_map/pallas_call | solution.py:350
  (73 shorter events, 11.0 us)
Async XLA Ops:
  0.6 19.6 %copy-start = (bf16[16,32768]{1,0:T(8,128)(2,1)S(1)}, bf16[16,32768]{1,0:T(8,128)(2,1)}, u32[]{:S(2)}) copy-start(bf16[16,32768]{1,0:T(8,128)(2,1)} %param.16) | copy-start | bytes 3145732
  3.6 59.4 %collective-permute-start = (bf16[384,2304]{1,0:T(8,128)(2,1)}, bf16[384,2304]{1,0:T(8,128)(2,1)}, u32[]{:S(2)}, u32[]{:S(2)}) collective-permute-start(bf16[384,2304]{1,0:T(8,128)(2,1)} %slice.6.refs_3_.refs_1_), channel_id=1, source_target_pairs={{0,4},{4,8},{8,12},{1,5},{5,9},{9,13},{2,6},{6,10},{10,14},{3,7},{... | collective-permute-start | bytes 5308424 | tf_op jit(solution)/shard_map/ppermute | solution.py:444
  9.7 53.2 %collective-permute-start.1 = (bf16[384,2304]{1,0:T(8,128)(2,1)}, bf16[384,2304]{1,0:T(8,128)(2,1)}, u32[]{:S(2)}, u32[]{:S(2)}) collective-permute-start(bf16[384,2304]{1,0:T(8,128)(2,1)} %slice.6.refs_3_.refs_1_), channel_id=1, source_target_pairs={{12,8},{8,4},{4,0},{13,9},{9,5},{5,1},{14,10},{10,6},{6,2},{15,11}... | collective-permute-start | bytes 5308424 | tf_op jit(solution)/shard_map/ppermute | solution.py:444
  11.0 3.7 %copy-start.2 = (bf16[2048,2304]{1,0:T(8,128)(2,1)S(1)}, bf16[2048,2304]{1,0:T(8,128)(2,1)}, u32[]{:S(2)}) copy-start(bf16[2048,2304]{1,0:T(8,128)(2,1)} %refs_1_.5) | copy-start | bytes 28311556
  15.6 8.2 %copy-start.3 = (bf16[512,2304]{1,0:T(8,128)(2,1)S(1)}, bf16[512,2304]{1,0:T(8,128)(2,1)}, u32[]{:S(2)}) copy-start(bf16[512,2304]{1,0:T(8,128)(2,1)} %cotangent.3) | copy-start | bytes 7077892
  18.1 44.9 %collective-permute-start.5 = (bf16[3,128,2304]{2,1,0:T(8,128)(2,1)}, bf16[3,128,2304]{2,1,0:T(8,128)(2,1)}, u32[]{:S(2)}, u32[]{:S(2)}) collective-permute-start(bf16[3,128,2304]{2,1,0:T(8,128)(2,1)} %shard_map.149), channel_id=1, source_target_pairs={{0,2},{1,3},{2,0},{3,1},{4,6},{5,7},{6,4},{7,5},{8,10},{9,11},{10,... | collective-permute-start | bytes 5308424 | tf_op jit(solution)/shard_map/ppermute | solution.py:430
  21.0 126.0 %copy-start.4 = (bf16[2048,16]{1,0:T(8,128)(2,1)}, bf16[2048,16]{1,0:T(8,128)(2,1)S(1)}, u32[]{:S(2)}) copy-start(bf16[2048,16]{1,0:T(8,128)(2,1)S(1)} %reshape.60.chosen_a.refs_2_.refs_9_) | copy-start | bytes 196612
  23.9 1.6 copy-start.6
  25.5 1.1 copy-start.10
  26.5 1.3 copy-start.14
  27.8 42.3 %copy-start.7 = (bf16[512,2048]{1,0:T(8,128)(2,1)S(1)}, bf16[512,2048]{1,0:T(8,128)(2,1)}, u32[]{:S(2)}) copy-start(bf16[512,2048]{1,0:T(8,128)(2,1)} %hidden.3) | copy-start | bytes 6291460
  62.9 46.9 %collective-permute-start.7 = (bf16[16,128,2304]{2,1,0:T(8,128)(2,1)}, bf16[16,128,2304]{2,1,0:T(8,128)(2,1)}, u32[]{:S(2)}, u32[]{:S(2)}) collective-permute-start(bf16[16,128,2304]{2,1,0:T(8,128)(2,1)} %get-tuple-element.47.refs_8_.refs_11_), channel_id=1, source_target_pairs={{0,1},{1,0},{2,3},{3,2},{4,5},{5,4},{6,7},{7,6},{8,9},{9,8},{10,11... | collective-permute-start | bytes 28311560 | tf_op jit(solution)/shard_map/ppermute | solution.py:434
  63.0 46.7 %collective-permute-start.4 = (bf16[3,128,2304]{2,1,0:T(8,128)(2,1)}, bf16[3,128,2304]{2,1,0:T(8,128)(2,1)}, u32[]{:S(2)}, u32[]{:S(2)}) collective-permute-start(bf16[3,128,2304]{2,1,0:T(8,128)(2,1)} %get-tuple-element.43), channel_id=1, source_target_pairs={{0,2},{1,3},{2,0},{3,1},{4,6},{5,7},{6,4},{7,5},{8,10},{9,11},{10,... | collective-permute-start | bytes 5308424 | tf_op jit(solution)/shard_map/ppermute | solution.py:430
  64.7 45.1 %collective-permute-start.6 = (bf16[3,128,2304]{2,1,0:T(8,128)(2,1)}, bf16[3,128,2304]{2,1,0:T(8,128)(2,1)}, u32[]{:S(2)}, u32[]{:S(2)}) collective-permute-start(bf16[3,128,2304]{2,1,0:T(8,128)(2,1)} %collective-permute-done.5.refs_0_), channel_id=1, source_target_pairs={{0,16},{16,0},{1,17},{17,1},{2,18},{18,2},{3,19},{19,3},{4,20},{20... | collective-permute-start | bytes 5308424 | tf_op jit(solution)/shard_map/ppermute | solution.py:438
  66.2 43.5 %collective-permute-start.3 = (bf16[384,2304]{1,0:T(8,128)(2,1)}, bf16[384,2304]{1,0:T(8,128)(2,1)}, u32[]{:S(2)}, u32[]{:S(2)}) collective-permute-start(bf16[384,2304]{1,0:T(8,128)(2,1)} %collective-permute-done.1.refs_5_.refs_3_), channel_id=1, source_target_pairs={{8,4},{4,0},{9,5},{5,1},{10,6},{6,2},{11,7},{7,3},{24,20},{20,16},... | collective-permute-start | bytes 5308424 | tf_op jit(solution)/shard_map/ppermute | solution.py:444
  67.5 42.3 %collective-permute-start.2 = (bf16[384,2304]{1,0:T(8,128)(2,1)}, bf16[384,2304]{1,0:T(8,128)(2,1)}, u32[]{:S(2)}, u32[]{:S(2)}) collective-permute-start(bf16[384,2304]{1,0:T(8,128)(2,1)} %collective-permute-done.refs_4_.refs_2_), channel_id=1, source_target_pairs={{4,8},{8,12},{5,9},{9,13},{6,10},{10,14},{7,11},{11,15},{20,24},{2... | collective-permute-start | bytes 5308424 | tf_op jit(solution)/shard_map/ppermute | solution.py:444
  73.7 1.2 copy-start.12
  109.8 13.4 %copy-start.15 = (bf16[16,128]{1,0:T(8,128)(2,1)S(1)}, bf16[16,128]{1,0:T(8,128)(2,1)}, u32[]{:S(2)}) copy-start(bf16[16,128]{1,0:T(8,128)(2,1)} %param.18) | copy-start | bytes 12292
  113.9 9.2 %collective-permute-start.10 = (bf16[9,128,2304]{2,1,0:T(8,128)(2,1)}, bf16[9,128,2304]{2,1,0:T(8,128)(2,1)}, u32[]{:S(2)}, u32[]{:S(2)}) collective-permute-start(bf16[9,128,2304]{2,1,0:T(8,128)(2,1)} %shard_map.152.refs_10_.refs_13_), channel_id=1, source_target_pairs={{0,1},{1,0},{2,3},{3,2},{4,5},{5,4},{6,7},{7,6},{8,9},{9,8},{10,11... | collective-permute-start | bytes 15925256 | tf_op jit(solution)/shard_map/ppermute | solution.py:434
  114.3 44.8 %collective-permute-start.11 = (bf16[3,128,2304]{2,1,0:T(8,128)(2,1)}, bf16[3,128,2304]{2,1,0:T(8,128)(2,1)}, u32[]{:S(2)}, u32[]{:S(2)}) collective-permute-start(bf16[3,128,2304]{2,1,0:T(8,128)(2,1)} %collective-permute-done.4.refs_1_), channel_id=1, source_target_pairs={{0,16},{16,0},{1,17},{17,1},{2,18},{18,2},{3,19},{19,3},{4,20},{20... | collective-permute-start | bytes 5308424 | tf_op jit(solution)/shard_map/ppermute | solution.py:438
  115.8 53.3 %collective-permute-start.13 = (bf16[4,128,2304]{2,1,0:T(8,128)(2,1)}, bf16[4,128,2304]{2,1,0:T(8,128)(2,1)}, u32[]{:S(2)}, u32[]{:S(2)}) collective-permute-start(bf16[4,128,2304]{2,1,0:T(8,128)(2,1)} %get-tuple-element.62), channel_id=1, source_target_pairs={{0,2},{1,3},{2,0},{3,1},{4,6},{5,7},{6,4},{7,5},{8,10},{9,11},{10,... | collective-permute-start | bytes 7077896 | tf_op jit(solution)/shard_map/ppermute | solution.py:430
  117.5 42.3 %collective-permute-start.9 = (bf16[384,2304]{1,0:T(8,128)(2,1)}, bf16[384,2304]{1,0:T(8,128)(2,1)}, u32[]{:S(2)}, u32[]{:S(2)}) collective-permute-start(bf16[384,2304]{1,0:T(8,128)(2,1)} %collective-permute-done.3.refs_7_.refs_5_), channel_id=1, source_target_pairs={{4,0},{5,1},{6,2},{7,3},{20,16},{21,17},{22,18},{23,19}} | collective-permute-start | bytes 5308424 | tf_op jit(solution)/shard_map/ppermute | solution.py:444
  118.8 41.0 %collective-permute-start.8 = (bf16[384,2304]{1,0:T(8,128)(2,1)}, bf16[384,2304]{1,0:T(8,128)(2,1)}, u32[]{:S(2)}, u32[]{:S(2)}) collective-permute-start(bf16[384,2304]{1,0:T(8,128)(2,1)} %collective-permute-done.2.refs_6_.refs_4_), channel_id=1, source_target_pairs={{8,12},{9,13},{10,14},{11,15},{24,28},{25,29},{26,30},{27,31}} | collective-permute-start | bytes 5308424 | tf_op jit(solution)/shard_map/ppermute | solution.py:444
  123.4 2.3 %copy-start.9 = (bf16[128,18432]{1,0:T(8,128)(2,1)S(1)}, bf16[128,18432]{1,0:T(8,128)(2,1)}, u32[]{:S(2)}) copy-start(bf16[128,18432]{1,0:T(8,128)(2,1)} %refs_1_.6) | copy-start | bytes 14155780
  132.4 3.4 %copy-start.8 = (bf16[128,32768]{1,0:T(8,128)(2,1)S(1)}, bf16[128,32768]{1,0:T(8,128)(2,1)}, u32[]{:S(2)}) copy-start(bf16[128,32768]{1,0:T(8,128)(2,1)} %refs_1_.7) | copy-start | bytes 25165828
  147.0 22.2 %copy-start.16 = (s32[16]{0:T(128)S(1)}, s32[16]{0:T(128)}, u32[]{:S(2)}) copy-start(s32[16]{0:T(128)} %param.23) | copy-start | bytes 196
  159.1 10.1 %collective-permute-start.12 = (bf16[3,128,2304]{2,1,0:T(8,128)(2,1)}, bf16[3,128,2304]{2,1,0:T(8,128)(2,1)}, u32[]{:S(2)}, u32[]{:S(2)}) collective-permute-start(bf16[3,128,2304]{2,1,0:T(8,128)(2,1)} %collective-permute-done.11.refs_15_), channel_id=1, source_target_pairs={{0,1},{1,0},{2,3},{3,2},{4,5},{5,4},{6,7},{7,6},{8,9},{9,8},{10,11... | collective-permute-start | bytes 5308424 | tf_op jit(solution)/shard_map/ppermute | solution.py:434
  169.2 4.9 %collective-permute-start.14 = (bf16[4,128,2304]{2,1,0:T(8,128)(2,1)}, bf16[4,128,2304]{2,1,0:T(8,128)(2,1)}, u32[]{:S(2)}, u32[]{:S(2)}) collective-permute-start(bf16[4,128,2304]{2,1,0:T(8,128)(2,1)} %collective-permute-done.13.refs_17_), channel_id=1, source_target_pairs={{0,1},{1,0},{2,3},{3,2},{4,5},{5,4},{6,7},{7,6},{8,9},{9,8},{10,11... | collective-permute-start | bytes 7077896 | tf_op jit(solution)/shard_map/ppermute | solution.py:434
  169.6 22.7 %collective-permute-start.15 = (f32[4,128]{1,0:T(4,128)S(1)}, f32[4,128]{1,0:T(4,128)S(1)}, u32[]{:S(2)}, u32[]{:S(2)}) collective-permute-start(f32[4,128]{1,0:T(4,128)S(1)} %add.34), channel_id=1, source_target_pairs={{0,4},{4,8},{8,12},{12,0},{1,5},{5,9},{9,13},{13,1},{2,6},{6,10},{... | collective-permute-start | bytes 6152 | tf_op jit(solution)/shard_map/ppermute | solution.py:450
  169.6 22.7 %collective-permute-start.16 = (f32[4,128]{1,0:T(4,128)S(1)}, f32[4,128]{1,0:T(4,128)S(1)}, u32[]{:S(2)}, u32[]{:S(2)}) collective-permute-start(f32[4,128]{1,0:T(4,128)S(1)} %add.34), channel_id=1, source_target_pairs={{0,8},{4,12},{8,0},{12,4},{1,9},{5,13},{9,1},{13,5},{2,10},{6,14},... | collective-permute-start | bytes 6152 | tf_op jit(solution)/shard_map/ppermute | solution.py:450
  171.1 21.2 %collective-permute-start.17 = (f32[4,128]{1,0:T(4,128)S(1)}, f32[4,128]{1,0:T(4,128)S(1)}, u32[]{:S(2)}, u32[]{:S(2)}) collective-permute-start(f32[4,128]{1,0:T(4,128)S(1)} %add.34), channel_id=1, source_target_pairs={{0,12},{4,0},{8,4},{12,8},{1,13},{5,1},{9,5},{13,9},{2,14},{6,2},{... | collective-permute-start | bytes 6152 | tf_op jit(solution)/shard_map/ppermute | solution.py:450
  175.1 17.9 %copy-start.1 = (bf16[16,32768]{1,0:T(8,128)(2,1)S(1)}, bf16[16,32768]{1,0:T(8,128)(2,1)}, u32[]{:S(2)}) copy-start(bf16[16,32768]{1,0:T(8,128)(2,1)} %param.16) | copy-start | bytes 3145732
  (3 other events, 2.9 us)

commit v8 on v7

--- a/solution.py
+++ b/solution.py
@@ -390,16 +390,15 @@
     )
 
 
-def gather_kernel(count, *refs):
+def gather_kernel(parts, *refs):
     inputs, (out, buffer, come, go) = refs[:-4], refs[-4:]
-    at, moves = 0, []
-    for i, ref in enumerate(inputs):
-        size = ref.shape[0]
-        part = buffer.at[pl.ds(at, size)]
-        arrive = pltpu.make_async_copy(ref, part, come.at[i])
-        moves.append((arrive, pltpu.make_async_copy(part, out.at[pl.ds(at, size)], go.at[i])))
+    moves = []
+    for i, (index, source, target, size) in enumerate(parts):
+        held = buffer.at[pl.ds(target, size)]
+        arrive = pltpu.make_async_copy(inputs[index].at[pl.ds(source, size)], held, come.at[i])
+        leave = pltpu.make_async_copy(held, out.at[pl.ds(target, size)], go.at[i])
+        moves.append((arrive, leave))
         arrive.start()
-        at += size
     for arrive, leave in moves:
         arrive.wait()
         leave.start()
@@ -407,23 +406,33 @@
         leave.wait()
 
 
-def gather_pieces(arrays):
+def gather_call(arrays, parts, shape):
     spec = pl.BlockSpec(memory_space=pltpu.HBM)
-    count = sum(array.shape[0] for array in arrays)
-    shape = (count,) + arrays[0].shape[1:]
     return pl.pallas_call(
-        lambda *refs: gather_kernel(count, *refs),
+        lambda *refs: gather_kernel(parts, *refs),
         out_shape=jax.ShapeDtypeStruct(shape, arrays[0].dtype),
         in_specs=[spec] * len(arrays),
         out_specs=spec,
         scratch_shapes=[
             pltpu.VMEM(shape, arrays[0].dtype),
-            pltpu.SemaphoreType.DMA((len(arrays),)),
-            pltpu.SemaphoreType.DMA((len(arrays),)),
+            pltpu.SemaphoreType.DMA((len(parts),)),
+            pltpu.SemaphoreType.DMA((len(parts),)),
         ],
         compiler_params=pltpu.CompilerParams(vmem_limit_bytes=32 * 2**20),
         cost_estimate=pl.CostEstimate(flops=0, transcendentals=0, bytes_accessed=0),
     )(*arrays)
+
+
+def gather_pieces(arrays):
+    parts = [(index, i) for index, array in enumerate(arrays) for i in range(array.shape[0])]
+    moves = [(index, i, at, 1) for at, (index, i) in enumerate(parts)]
+    return gather_call(arrays, moves, (len(moves),) + arrays[0].shape[1:])
+
+
+def live_rows(array):
+    size = LIVE // 8
+    moves = [(0, i * size, i * size, size) for i in range(8)]
+    return gather_call([array], moves, (LIVE, array.shape[1]))
 
 
 def across(value):
@@ -538,6 +547,7 @@
     joined_part = cotangent.shape[1]
     own = cotangent[:LIVE]
     lines = (n_groups, n_fsdp, n_dp) == (2, 4, 4) and width_part == 16 * PIECE
+    own = live_rows(cotangent) if lines else own
     plan = Plan(own, base_codes, base_scales, y) if lines else None
 
     task_rows = lax.broadcasted_iota(jnp.int32, (tasks_all, tasks_all), 0)

time: 194 us -> 197 us (1.015)
  Pallas kernels: 73.8 us -> 78.1 us
    pallas_call x1 -> x2, Pallas kernels: 4.07 us -> 8.36 us  [gather_call(): pl.pallas_call(lambda *refs: gather_kernel(parts, *refs), out_shape=jax.S...]
    slice x1 -> x0, local copies, waits for them, and re-layouts: 2.91 us -> none  [shards(): own = cotangent[:LIVE]]
    unnamed x35 -> x37, local copies, waits for them, and re-layouts: 15.8 us -> 17.6 us
where the time goes in v8:
time: 197 us; the launch traced here: 196 us
  Pallas kernels  78.1 us (40%)
  blocking collectives  52.9 us (27%)
  starting transfers between devices  26.8 us (14%)
  local copies, waits for them, and re-layouts  22.1 us (11%)
  waiting for transfers between devices  12.2 us (6%)
  between operations  2.28 us (1%)
    all_gather x1, blocking collectives, gather_rows(): rows = lax.all_gather(row, 'dp', axis=0, tiled=True)  34.1 us
    pallas_call x2, Pallas kernels, matmul_call(): pl.pallas_call(kernel, out_shape=out_shape, in_specs=specs, out_specs=vme...  29.2 us
    all_gather x1, blocking collectives, sum_parts(): gathered = lax.all_gather(after(parts, self.mine), 'fsdp', axis=0)  18.8 us
    pallas_call x2, Pallas kernels, weight_pieces(): pl.pallas_call(lambda *refs: weight_kernel(spans, *refs), out_shape=[jax....  18.7 us
    pallas_call x2, Pallas kernels, head_grads(): pl.pallas_call(head_kernel, out_shape=[jax.ShapeDtypeStruct((hidden_units...  17.9 us
    unnamed x37, local copies, waits for them, and re-layouts  17.6 us
    ppermute x6, starting transfers between devices, send(): lax.ppermute(value, 'fsdp', pairs if sign > 0 else [(3 - a, 3 - b) for a,...  13.8 us
    ppermute x3, waiting for transfers between devices, across(): return lax.ppermute(value, 'dp', [(i, i ^ 2) for i in range(4)])  9.32 us
  transfers between devices with their start and end apart: 18, of which 4 were waited for; matrix products, arithmetic and copies ran while one was open for 3% of the time, Pallas kernels for 36%

profile of v8, /device:TPU:0, one launch (start us, length us, event | category | flops | bytes accessed | tf_op | source)
XLA Modules:
  0.0 196.1 jit_solution(16393879013602480993)
XLA Ops:
  0.7 1.7 copy-done.3
  2.4 3.6 %shard_map.147.refs_3_.refs_1_ = bf16[384,2304]{1,0:T(8,128)(2,1)} custom-call(bf16[512,2304]{1,0:T(8,128)(2,1)S(1)} %copy-done.3), custom_call_target="tpu_custom_call" | custom-call | tf_op jit(solution)/shard_map/pallas_call | solution.py:411
  6.0 6.2 %collective-permute-start = (bf16[384,2304]{1,0:T(8,128)(2,1)}, bf16[384,2304]{1,0:T(8,128)(2,1)}, u32[]{:S(2)}, u32[]{:S(2)}) collective-permute-start(bf16[384,2304]{1,0:T(8,128)(2,1)} %shard_map.147.refs_3_.refs_1_), channel_id=1, source_target_pairs={{0,4},{4,8},{8,12},{1,5},{5,9},{9,13},{2,6},{6,10},{10,14},{3,7},{... | collective-permute-start | bytes 5308424 | tf_op jit(solution)/shard_map/ppermute | solution.py:453
  12.2 1.3 collective-permute-start.1
  13.5 3.7 %copy-done.2 = bf16[2048,2304]{1,0:T(8,128)(2,1)S(1)} copy-done((bf16[2048,2304]{1,0:T(8,128)(2,1)S(1)}, bf16[2048,2304]{1,0:T(8,128)(2,1)}, u32[]{:S(2)}) %copy-start.2) | copy-done | bytes 9437208
  18.1 2.4 %shard_map.150 = bf16[3,128,2304]{2,1,0:T(8,128)(2,1)} custom-call(s32[1]{0:T(128)} %bitcast.2.refs_0_, bf16[2048,2304]{1,0:T(8,128)(2,1)S(1)} %copy-done.2, bf16[36,2048]{1,0:T(8,128)(2,1)S(1)} %bitcast.21), custom_call_target="tpu_custom_call" | custom-call | tf_op jit(solution)/shard_map/pallas_call | solution.py:68
  20.5 1.5 collective-permute-start.5
  23.5 1.4 dynamic-slice_reduce_fusion.1
  24.9 1.5 reshape.61.chosen_b
  26.4 1.6 copy-done.7
  30.3 16.2 %shard_map.149 = (bf16[16,128,2304]{2,1,0:T(8,128)(2,1)}, bf16[3,128,2304]{2,1,0:T(8,128)(2,1)}, bf16[4,128,2304]{2,1,0:T(8,128)(2,1)}) custom-call(s32[1]{0:T(128)} %bitcast.2.refs_0_, bf16[2048,2304]{1,0:T(8,128)(2,1)} %refs_1_.5, bf16[36,2048]{1,0:T(8,128)(2,1)S(1)} %bitcast.22), custom_call_target="tpu_custom_call" | custom-call | tf_op jit(solution)/shard_map/pallas_call | solution.py:68
  46.5 18.8 %all-gather = bf16[1536,32]{1,0:T(8,128)(2,1)S(1)} all-gather(bf16[384,32]{1,0:T(8,128)(2,1)S(1)} %shard_map.148), channel_id=2, replica_groups=mesh['groups'=2,'fsdp'=4,'dp'=4] {'fsdp'}, dimensions={0}, use_global_device_ids=true | all-gather | bytes 122880 | tf_op jit(solution)/shard_map/all_gather | solution.py:477
  65.5 1.7 collective-permute-start.4
  67.2 1.5 collective-permute-start.6
  70.0 1.9 collective-permute-start.2
  72.6 2.7 %shard_map.151 = (f32[2048,16]{1,0:T(8,128)S(1)}, f32[2304,8]{1,0:T(8,128)S(1)}, bf16[384,16]{1,0:T(8,128)(2,1)S(1)}) custom-call(s32[2]{0:T(128)S(1)} %pad_add_fusion.1.scalars, bf16[512,2048]{1,0:T(8,128)(2,1)S(1)} %copy-done.8, bf16[512,2304]{1,0:T(8,128)(2,1)S(1)} %copy-done.4, bf16[4,384,32]{2,1,0:T(8,128)(2,1)S(1)} %bitcast.19), custom_call_target="tpu_custom_call" | custom-call | tf_op jit(solution)/shard_map/pallas_call | solution.py:179
  77.9 34.1 %all-gather.1 = bf16[4,1,51328]{2,1,0:T(2,128)(2,1)S(1)} all-gather(bf16[1,1,51328]{2,1,0:T(2,128)(2,1)S(1)} %bitcast.20), channel_id=1, replica_groups=mesh['groups'=2,'fsdp'=4,'dp'=4] {'dp'}, dimensions={0}, use_global_device_ids=true | all-gather | bytes 513280 | tf_op jit(solution)/shard_map/all_gather | solution.py:487
  112.3 4.7 %shard_map.153.refs_10_.refs_13_ = bf16[9,128,2304]{2,1,0:T(8,128)(2,1)} custom-call(bf16[3,128,2304]{2,1,0:T(8,128)(2,1)} %collective-permute-done.5.refs_0_, bf16[3,128,2304]{2,1,0:T(8,128)(2,1)} %collective-permute-done.4.refs_1_, bf16[3,128,2304]{2,1,0:T(8,128)(2,1)} %collective-permute-done.6.refs_2_), custom_call_target="tpu_custom_call" | custom-call | tf_op jit(solution)/shard_map/pallas_call | solution.py:411
  117.4 1.5 collective-permute-start.11
  119.0 1.6 collective-permute-start.13
  120.7 1.3 collective-permute-start.9
  122.0 1.9 collective-permute-start.8
  123.8 2.3 %collective-permute-done.10.refs_11_.refs_14_ = bf16[9,128,2304]{2,1,0:T(8,128)(2,1)} collective-permute-done((bf16[9,128,2304]{2,1,0:T(8,128)(2,1)}, bf16[9,128,2304]{2,1,0:T(8,128)(2,1)}, u32[]{:S(2)}, u32[]{:S(2)}) %collective-permute-start.10) | collective-permute-done | bytes 5308448 | tf_op jit(solution)/shard_map/ppermute | solution.py:443
  126.5 2.3 %copy-done.10 = bf16[128,18432]{1,0:T(8,128)(2,1)S(1)} copy-done((bf16[128,18432]{1,0:T(8,128)(2,1)S(1)}, bf16[128,18432]{1,0:T(8,128)(2,1)}, u32[]{:S(2)}) %copy-start.10) | copy-done | bytes 4718616
  128.8 6.7 %shard_map.154 = (f32[128,18432]{1,0:T(8,128)}, f32[4,128]{1,0:T(4,128)S(1)}) custom-call(bf16[4,128]{1,0:T(4,128)(2,1)S(1)} %convolution_convert_fusion.states, bf16[4,51328]{1,0:T(4,128)(2,1)S(1)} %bitcast.17, bf16[128,18432]{1,0:T(8,128)(2,1)S(1)} %copy-done.10), custom_call_target="tpu_custom_call" | custom-call | tf_op jit(solution)/shard_map/pallas_call | solution.py:156
  135.5 3.4 %copy-done.9 = bf16[128,32768]{1,0:T(8,128)(2,1)S(1)} copy-done((bf16[128,32768]{1,0:T(8,128)(2,1)S(1)}, bf16[128,32768]{1,0:T(8,128)(2,1)}, u32[]{:S(2)}) %copy-start.9) | copy-done | bytes 8388632
  138.9 11.3 %shard_map.155 = (f32[128,32768]{1,0:T(8,128)}, f32[4,128]{1,0:T(4,128)S(1)}) custom-call(bf16[4,128]{1,0:T(4,128)(2,1)S(1)} %convolution_convert_fusion.states, bf16[4,51328]{1,0:T(4,128)(2,1)S(1)} %bitcast.18, bf16[128,32768]{1,0:T(8,128)(2,1)S(1)} %copy-done.9), custom_call_target="tpu_custom_call" | custom-call | tf_op jit(solution)/shard_map/pallas_call | solution.py:156
  150.2 12.0 %shard_map.156.refs_10_ = f32[384,1024]{1,0:T(8,128)S(1)} custom-call(s32[4]{0:T(128)S(1)} %pad_add_fusion.refs_0_, bf16[384,16]{1,0:T(8,128)(2,1)S(1)} %get-tuple-element.50.refs_1_.refs_8_, bf16[2048,16]{1,0:T(8,128)(2,1)S(1)} %reshape.60.chosen_a.refs_2_.refs_9_, bf16[384,2304]{1,0:T(8,128)(2,1)} %shard_map.147.refs_3_.refs_1_, ...), custom_call_target="tpu_custom_call" | custom-call | tf_op jit(solution)/shard_map/pallas_call | solution.py:350
  163.0 9.3 %collective-permute-done.13.refs_17_ = bf16[4,128,2304]{2,1,0:T(8,128)(2,1)} collective-permute-done((bf16[4,128,2304]{2,1,0:T(8,128)(2,1)}, bf16[4,128,2304]{2,1,0:T(8,128)(2,1)}, u32[]{:S(2)}, u32[]{:S(2)}) %collective-permute-start.13) | collective-permute-done | bytes 2359328 | tf_op jit(solution)/shard_map/ppermute | solution.py:439
  172.8 1.5 collective-permute-start.16
  174.3 2.6 %collective-permute-start.17 = (f32[4,128]{1,0:T(4,128)S(1)}, f32[4,128]{1,0:T(4,128)S(1)}, u32[]{:S(2)}, u32[]{:S(2)}) collective-permute-start(f32[4,128]{1,0:T(4,128)S(1)} %add.34), channel_id=1, source_target_pairs={{0,12},{4,0},{8,4},{12,8},{1,13},{5,1},{9,5},{13,9},{2,14},{6,2},{... | collective-permute-start | bytes 6152 | tf_op jit(solution)/shard_map/ppermute | solution.py:459
  178.2 17.2 %shard_map.157 = bf16[512,2048]{1,0:T(8,128)(2,1)} custom-call(s32[4]{0:T(128)S(1)} %pad_add_fusion.refs_0_, bf16[384,2304]{1,0:T(8,128)(2,1)} %shard_map.147.refs_3_.refs_1_, bf16[384,2304]{1,0:T(8,128)(2,1)} %collective-permute-done.refs_4_.refs_2_, bf16[384,2304]{1,0:T(8,128)(2,1)} %collective-permute-done.1.refs_5_.refs_3_, ...), custom_call_target="tpu_custom_call" | custom-call | tf_op jit(solution)/shard_map/pallas_call | solution.py:350
  (75 shorter events, 12.3 us)
Async XLA Ops:
  0.6 22.1 %copy-start = (bf16[16,32768]{1,0:T(8,128)(2,1)S(1)}, bf16[16,32768]{1,0:T(8,128)(2,1)}, u32[]{:S(2)}) copy-start(bf16[16,32768]{1,0:T(8,128)(2,1)} %param.16) | copy-start | bytes 3145732
  0.6 1.8 copy-start.3
  6.0 59.4 %collective-permute-start = (bf16[384,2304]{1,0:T(8,128)(2,1)}, bf16[384,2304]{1,0:T(8,128)(2,1)}, u32[]{:S(2)}, u32[]{:S(2)}) collective-permute-start(bf16[384,2304]{1,0:T(8,128)(2,1)} %shard_map.147.refs_3_.refs_1_), channel_id=1, source_target_pairs={{0,4},{4,8},{8,12},{1,5},{5,9},{9,13},{2,6},{6,10},{10,14},{3,7},{... | collective-permute-start | bytes 5308424 | tf_op jit(solution)/shard_map/ppermute | solution.py:453
  12.2 53.2 %collective-permute-start.1 = (bf16[384,2304]{1,0:T(8,128)(2,1)}, bf16[384,2304]{1,0:T(8,128)(2,1)}, u32[]{:S(2)}, u32[]{:S(2)}) collective-permute-start(bf16[384,2304]{1,0:T(8,128)(2,1)} %shard_map.147.refs_3_.refs_1_), channel_id=1, source_target_pairs={{12,8},{8,4},{4,0},{13,9},{9,5},{5,1},{14,10},{10,6},{6,2},{15,11}... | collective-permute-start | bytes 5308424 | tf_op jit(solution)/shard_map/ppermute | solution.py:453
  13.5 3.7 %copy-start.2 = (bf16[2048,2304]{1,0:T(8,128)(2,1)S(1)}, bf16[2048,2304]{1,0:T(8,128)(2,1)}, u32[]{:S(2)}) copy-start(bf16[2048,2304]{1,0:T(8,128)(2,1)} %refs_1_.5) | copy-start | bytes 28311556
  18.1 8.2 %copy-start.4 = (bf16[512,2304]{1,0:T(8,128)(2,1)S(1)}, bf16[512,2304]{1,0:T(8,128)(2,1)}, u32[]{:S(2)}) copy-start(bf16[512,2304]{1,0:T(8,128)(2,1)} %cotangent.3) | copy-start | bytes 7077892
  20.5 44.8 %collective-permute-start.5 = (bf16[3,128,2304]{2,1,0:T(8,128)(2,1)}, bf16[3,128,2304]{2,1,0:T(8,128)(2,1)}, u32[]{:S(2)}, u32[]{:S(2)}) collective-permute-start(bf16[3,128,2304]{2,1,0:T(8,128)(2,1)} %shard_map.150), channel_id=1, source_target_pairs={{0,2},{1,3},{2,0},{3,1},{4,6},{5,7},{6,4},{7,5},{8,10},{9,11},{10,... | collective-permute-start | bytes 5308424 | tf_op jit(solution)/shard_map/ppermute | solution.py:439
  23.5 126.7 %copy-start.5 = (bf16[2048,16]{1,0:T(8,128)(2,1)}, bf16[2048,16]{1,0:T(8,128)(2,1)S(1)}, u32[]{:S(2)}) copy-start(bf16[2048,16]{1,0:T(8,128)(2,1)S(1)} %reshape.60.chosen_a.refs_2_.refs_9_) | copy-start | bytes 196612
  26.4 1.6 copy-start.7
  29.0 1.3 copy-start.15
  30.3 42.3 %copy-start.8 = (bf16[512,2048]{1,0:T(8,128)(2,1)S(1)}, bf16[512,2048]{1,0:T(8,128)(2,1)}, u32[]{:S(2)}) copy-start(bf16[512,2048]{1,0:T(8,128)(2,1)} %hidden.3) | copy-start | bytes 6291460
  65.4 46.9 %collective-permute-start.7 = (bf16[16,128,2304]{2,1,0:T(8,128)(2,1)}, bf16[16,128,2304]{2,1,0:T(8,128)(2,1)}, u32[]{:S(2)}, u32[]{:S(2)}) collective-permute-start(bf16[16,128,2304]{2,1,0:T(8,128)(2,1)} %get-tuple-element.47.refs_8_.refs_11_), channel_id=1, source_target_pairs={{0,1},{1,0},{2,3},{3,2},{4,5},{5,4},{6,7},{7,6},{8,9},{9,8},{10,11... | collective-permute-start | bytes 28311560 | tf_op jit(solution)/shard_map/ppermute | solution.py:443
  65.5 46.7 %collective-permute-start.4 = (bf16[3,128,2304]{2,1,0:T(8,128)(2,1)}, bf16[3,128,2304]{2,1,0:T(8,128)(2,1)}, u32[]{:S(2)}, u32[]{:S(2)}) collective-permute-start(bf16[3,128,2304]{2,1,0:T(8,128)(2,1)} %get-tuple-element.43), channel_id=1, source_target_pairs={{0,2},{1,3},{2,0},{3,1},{4,6},{5,7},{6,4},{7,5},{8,10},{9,11},{10,... | collective-permute-start | bytes 5308424 | tf_op jit(solution)/shard_map/ppermute | solution.py:439
  67.2 45.0 %collective-permute-start.6 = (bf16[3,128,2304]{2,1,0:T(8,128)(2,1)}, bf16[3,128,2304]{2,1,0:T(8,128)(2,1)}, u32[]{:S(2)}, u32[]{:S(2)}) collective-permute-start(bf16[3,128,2304]{2,1,0:T(8,128)(2,1)} %collective-permute-done.5.refs_0_), channel_id=1, source_target_pairs={{0,16},{16,0},{1,17},{17,1},{2,18},{18,2},{3,19},{19,3},{4,20},{20... | collective-permute-start | bytes 5308424 | tf_op jit(solution)/shard_map/ppermute | solution.py:447
  68.7 43.5 %collective-permute-start.3 = (bf16[384,2304]{1,0:T(8,128)(2,1)}, bf16[384,2304]{1,0:T(8,128)(2,1)}, u32[]{:S(2)}, u32[]{:S(2)}) collective-permute-start(bf16[384,2304]{1,0:T(8,128)(2,1)} %collective-permute-done.1.refs_5_.refs_3_), channel_id=1, source_target_pairs={{8,4},{4,0},{9,5},{5,1},{10,6},{6,2},{11,7},{7,3},{24,20},{20,16},... | collective-permute-start | bytes 5308424 | tf_op jit(solution)/shard_map/ppermute | solution.py:453
  70.0 42.3 %collective-permute-start.2 = (bf16[384,2304]{1,0:T(8,128)(2,1)}, bf16[384,2304]{1,0:T(8,128)(2,1)}, u32[]{:S(2)}, u32[]{:S(2)}) collective-permute-start(bf16[384,2304]{1,0:T(8,128)(2,1)} %collective-permute-done.refs_4_.refs_2_), channel_id=1, source_target_pairs={{4,8},{8,12},{5,9},{9,13},{6,10},{10,14},{7,11},{11,15},{20,24},{2... | collective-permute-start | bytes 5308424 | tf_op jit(solution)/shard_map/ppermute | solution.py:453
  76.2 1.2 copy-start.13
  112.3 14.0 %copy-start.16 = (bf16[16,128]{1,0:T(8,128)(2,1)S(1)}, bf16[16,128]{1,0:T(8,128)(2,1)}, u32[]{:S(2)}) copy-start(bf16[16,128]{1,0:T(8,128)(2,1)} %param.18) | copy-start | bytes 12292
  117.0 9.2 %collective-permute-start.10 = (bf16[9,128,2304]{2,1,0:T(8,128)(2,1)}, bf16[9,128,2304]{2,1,0:T(8,128)(2,1)}, u32[]{:S(2)}, u32[]{:S(2)}) collective-permute-start(bf16[9,128,2304]{2,1,0:T(8,128)(2,1)} %shard_map.153.refs_10_.refs_13_), channel_id=1, source_target_pairs={{0,1},{1,0},{2,3},{3,2},{4,5},{5,4},{6,7},{7,6},{8,9},{9,8},{10,11... | collective-permute-start | bytes 15925256 | tf_op jit(solution)/shard_map/ppermute | solution.py:443
  117.4 44.8 %collective-permute-start.11 = (bf16[3,128,2304]{2,1,0:T(8,128)(2,1)}, bf16[3,128,2304]{2,1,0:T(8,128)(2,1)}, u32[]{:S(2)}, u32[]{:S(2)}) collective-permute-start(bf16[3,128,2304]{2,1,0:T(8,128)(2,1)} %collective-permute-done.4.refs_1_), channel_id=1, source_target_pairs={{0,16},{16,0},{1,17},{17,1},{2,18},{18,2},{3,19},{19,3},{4,20},{20... | collective-permute-start | bytes 5308424 | tf_op jit(solution)/shard_map/ppermute | solution.py:447
  119.0 53.3 %collective-permute-start.13 = (bf16[4,128,2304]{2,1,0:T(8,128)(2,1)}, bf16[4,128,2304]{2,1,0:T(8,128)(2,1)}, u32[]{:S(2)}, u32[]{:S(2)}) collective-permute-start(bf16[4,128,2304]{2,1,0:T(8,128)(2,1)} %get-tuple-element.62), channel_id=1, source_target_pairs={{0,2},{1,3},{2,0},{3,1},{4,6},{5,7},{6,4},{7,5},{8,10},{9,11},{10,... | collective-permute-start | bytes 7077896 | tf_op jit(solution)/shard_map/ppermute | solution.py:439
  120.7 42.3 %collective-permute-start.9 = (bf16[384,2304]{1,0:T(8,128)(2,1)}, bf16[384,2304]{1,0:T(8,128)(2,1)}, u32[]{:S(2)}, u32[]{:S(2)}) collective-permute-start(bf16[384,2304]{1,0:T(8,128)(2,1)} %collective-permute-done.3.refs_7_.refs_5_), channel_id=1, source_target_pairs={{4,0},{5,1},{6,2},{7,3},{20,16},{21,17},{22,18},{23,19}} | collective-permute-start | bytes 5308424 | tf_op jit(solution)/shard_map/ppermute | solution.py:453
  122.0 41.0 %collective-permute-start.8 = (bf16[384,2304]{1,0:T(8,128)(2,1)}, bf16[384,2304]{1,0:T(8,128)(2,1)}, u32[]{:S(2)}, u32[]{:S(2)}) collective-permute-start(bf16[384,2304]{1,0:T(8,128)(2,1)} %collective-permute-done.2.refs_6_.refs_4_), channel_id=1, source_target_pairs={{8,12},{9,13},{10,14},{11,15},{24,28},{25,29},{26,30},{27,31}} | collective-permute-start | bytes 5308424 | tf_op jit(solution)/shard_map/ppermute | solution.py:453
  126.5 2.3 %copy-start.10 = (bf16[128,18432]{1,0:T(8,128)(2,1)S(1)}, bf16[128,18432]{1,0:T(8,128)(2,1)}, u32[]{:S(2)}) copy-start(bf16[128,18432]{1,0:T(8,128)(2,1)} %refs_1_.6) | copy-start | bytes 14155780
  135.5 3.4 %copy-start.9 = (bf16[128,32768]{1,0:T(8,128)(2,1)S(1)}, bf16[128,32768]{1,0:T(8,128)(2,1)}, u32[]{:S(2)}) copy-start(bf16[128,32768]{1,0:T(8,128)(2,1)} %refs_1_.7) | copy-start | bytes 25165828
  150.2 22.2 %copy-start.17 = (s32[16]{0:T(128)S(1)}, s32[16]{0:T(128)}, u32[]{:S(2)}) copy-start(s32[16]{0:T(128)} %param.23) | copy-start | bytes 196
  162.2 10.1 %collective-permute-start.12 = (bf16[3,128,2304]{2,1,0:T(8,128)(2,1)}, bf16[3,128,2304]{2,1,0:T(8,128)(2,1)}, u32[]{:S(2)}, u32[]{:S(2)}) collective-permute-start(bf16[3,128,2304]{2,1,0:T(8,128)(2,1)} %collective-permute-done.11.refs_15_), channel_id=1, source_target_pairs={{0,1},{1,0},{2,3},{3,2},{4,5},{5,4},{6,7},{7,6},{8,9},{9,8},{10,11... | collective-permute-start | bytes 5308424 | tf_op jit(solution)/shard_map/ppermute | solution.py:443
  172.3 4.9 %collective-permute-start.14 = (bf16[4,128,2304]{2,1,0:T(8,128)(2,1)}, bf16[4,128,2304]{2,1,0:T(8,128)(2,1)}, u32[]{:S(2)}, u32[]{:S(2)}) collective-permute-start(bf16[4,128,2304]{2,1,0:T(8,128)(2,1)} %collective-permute-done.13.refs_17_), channel_id=1, source_target_pairs={{0,1},{1,0},{2,3},{3,2},{4,5},{5,4},{6,7},{7,6},{8,9},{9,8},{10,11... | collective-permute-start | bytes 7077896 | tf_op jit(solution)/shard_map/ppermute | solution.py:443
  172.7 22.7 %collective-permute-start.15 = (f32[4,128]{1,0:T(4,128)S(1)}, f32[4,128]{1,0:T(4,128)S(1)}, u32[]{:S(2)}, u32[]{:S(2)}) collective-permute-start(f32[4,128]{1,0:T(4,128)S(1)} %add.34), channel_id=1, source_target_pairs={{0,4},{4,8},{8,12},{12,0},{1,5},{5,9},{9,13},{13,1},{2,6},{6,10},{... | collective-permute-start | bytes 6152 | tf_op jit(solution)/shard_map/ppermute | solution.py:459
  172.8 22.7 %collective-permute-start.16 = (f32[4,128]{1,0:T(4,128)S(1)}, f32[4,128]{1,0:T(4,128)S(1)}, u32[]{:S(2)}, u32[]{:S(2)}) collective-permute-start(f32[4,128]{1,0:T(4,128)S(1)} %add.34), channel_id=1, source_target_pairs={{0,8},{4,12},{8,0},{12,4},{1,9},{5,13},{9,1},{13,5},{2,10},{6,14},... | collective-permute-start | bytes 6152 | tf_op jit(solution)/shard_map/ppermute | solution.py:459
  174.3 21.2 %collective-permute-start.17 = (f32[4,128]{1,0:T(4,128)S(1)}, f32[4,128]{1,0:T(4,128)S(1)}, u32[]{:S(2)}, u32[]{:S(2)}) collective-permute-start(f32[4,128]{1,0:T(4,128)S(1)} %add.34), channel_id=1, source_target_pairs={{0,12},{4,0},{8,4},{12,8},{1,13},{5,1},{9,5},{13,9},{2,14},{6,2},{... | collective-permute-start | bytes 6152 | tf_op jit(solution)/shard_map/ppermute | solution.py:459
  178.2 17.9 %copy-start.1 = (bf16[16,32768]{1,0:T(8,128)(2,1)S(1)}, bf16[16,32768]{1,0:T(8,128)(2,1)}, u32[]{:S(2)}) copy-start(bf16[16,32768]{1,0:T(8,128)(2,1)} %param.16) | copy-start | bytes 3145732
  (4 other events, 4.0 us)
